TPU v7x, 32 devices: a whole 2x2x4 slice. The times are simulated.
32 devices in a mesh: dev: 16 (over z, y, core), rhs: 2 (over x).
Axes of the slice: x: 2, y: 2, z: 4, core: 2. Of those that a mesh axis runs over, the one named last changes fastest.
Arguments:
- top_adj: float32 [16, 32, 16, 256], P('rhs', 'dev'), may hold values from -6 to 6
- level1_adj: float32 [16, 16, 64, 128], P('rhs', 'dev'), may hold values from -6 to 6
- image_offsets: int32 [64, 2], P('rhs'), may hold values from -6 to 6
- image_weights: float32 [64], P('rhs'), may hold values from 0.2 to 1
- incidence: float32 [16, 2], replicated, may hold values from -0.6 to 0.6
- child_list: int32 [16, 4], replicated, may hold values from 0 to 63, as said below
- theta_index_top: int32 [128, 3], replicated, may hold values from 0 to 63
- theta_weight_top: float32 [128, 3], replicated, may hold values from -2.7 to 2.7
- phi_weight_top: float32 [32, 3], replicated, may hold values from -2.7 to 2.7
- theta_index_mid: int32 [64, 3], replicated, may hold values from 0 to 31
- theta_weight_mid: float32 [64, 3], replicated, may hold values from -2.7 to 2.7
- phi_weight_mid: float32 [16, 3], replicated, may hold values from -2.7 to 2.7
Outputs:
- level0_adj: float32 [16, 256, 512], P('rhs', 'dev')
Inputs may be any that keep to these rules, and one draw needn't show every extreme that they name: `child_list`: row b holds the middle-level boxes 4 b to 4 b + 3, each once.
All inputs are finite; a program needn't handle non-finite values.
Results may differ from a plain program's by a relative error of at most 0.0003.
Values sent between devices are 32-bit elements; how exact they have to be, the bound alone decides.
No kernel may reach another device: no remote copies, remote signals or barrier semaphores. Data moves between devices by JAX's collectives and lax.ppermute only.
A program may use at most 128 MiB of HBM per device.

v0:
```python
import math

import jax
import jax.numpy as jnp
from jax import lax
from jax.sharding import PartitionSpec as P

PHASE_TOP = 18.85
PHASE_MID = 9.42
LATTICE = 12.57


def padded_2(cells, sides, width):
    for axis, dim in sides:
        count = lax.axis_size(axis)
        head = lax.slice_in_dim(cells, 0, width, axis=dim)
        tail = lax.slice_in_dim(cells, cells.shape[dim] - width, cells.shape[dim], axis=dim)
        cells = jnp.concatenate(
            [
                lax.ppermute(tail, axis, [(i, (i + 1) % count) for i in range(count)]),
                cells,
                lax.ppermute(head, axis, [((i + 1) % count, i) for i in range(count)]),
            ],
            axis=dim,
        )
    return cells


def directions(theta_count, phi_ids, phi_count):
    theta = math.pi / theta_count * (jnp.arange(theta_count, dtype=jnp.float32) + 0.5)
    azimuth = 2.0 * math.pi / phi_count * phi_ids.astype(jnp.float32)
    sin_theta = jnp.sin(theta)
    along_x = jnp.cos(azimuth)[:, None] * sin_theta[None, :]
    along_y = jnp.sin(azimuth)[:, None] * sin_theta[None, :]
    along_z = jnp.cos(theta)
    return (along_x, along_y, along_z)


def theta_matrix(index, weight, columns):
    hits = (index[:, :, None] == jnp.arange(columns, dtype=jnp.int32)[None, None, :]).astype(
        jnp.float32
    )
    return jnp.sum(weight[:, :, None] * hits, axis=1)


def phi_matrix(weight, row_ids, coarse_count, column_ids):
    target = (row_ids[:, None] // 2 + jnp.arange(3, dtype=jnp.int32)[None, :] - 1) % coarse_count
    hits = (target[:, :, None] == column_ids[None, None, :]).astype(jnp.float32)
    return jnp.sum(weight[:, :, None] * hits, axis=1)


def octant_phase(factor, octant, along_x, along_y, along_z):
    sign_x = 2.0 * (octant % 2) - 1.0
    sign_y = 2.0 * (octant // 2) - 1.0
    angle = factor * (sign_x * along_x + sign_y * along_y - along_z[None, :])
    return (jnp.cos(angle), jnp.sin(angle))


def lattice_sum(offsets, weighted, incident, along_x, along_y):
    phase_arg = LATTICE * (
        offsets[:, 0, None, None, None] * (along_x[None, None] - incident[None, :, 0, None, None])
        + offsets[:, 1, None, None, None] * (along_y[None, None] - incident[None, :, 1, None, None])
    )
    sum_real = jnp.sum(weighted[:, None, None, None] * jnp.cos(phase_arg), axis=0)
    sum_imag = jnp.sum(weighted[:, None, None, None] * jnp.sin(phase_arg), axis=0)
    return (sum_real, sum_imag)


def upper_level(
    top_real, top_imag, along_x, along_y, along_z, theta_map, phi_map, children, top_ids
):
    summed = None
    for octant in range(4):
        cosine, sine = octant_phase(PHASE_TOP, octant, along_x, along_y, along_z)
        cosine = cosine[:, None, :]
        sine = sine[:, None, :]
        stacked = jnp.stack(
            [top_real * cosine - top_imag * sine, top_real * sine + top_imag * cosine]
        )
        theta_done = jnp.einsum(
            "...pbt,tu->...pbu", stacked, theta_map, precision=lax.Precision.HIGHEST
        )
        phi_done = jnp.einsum(
            "...pbu,pq->...qbu", theta_done, phi_map, precision=lax.Precision.HIGHEST
        )
        select_map = (
            children[:, octant][:, None] - 4 * top_ids[:, None]
            == jnp.arange(4, dtype=jnp.int32)[None, :]
        ).astype(jnp.float32)
        placed = phi_done[..., None, :] * select_map[:, :, None]
        summed = placed if summed is None else summed + placed
    merged = summed.reshape(summed.shape[:-3] + (summed.shape[-3] * 4, summed.shape[-1]))
    return jnp.concatenate([merged[0], merged[1]], axis=-1)


def lower_level(middle, along_x, along_y, along_z, theta_map, phi_map):
    half_width = middle.shape[-1] // 2
    mid_real = middle[..., :half_width]
    mid_imag = middle[..., half_width:]
    real_parts = []
    imag_parts = []
    for octant in range(4):
        cosine, sine = octant_phase(PHASE_MID, octant, along_x, along_y, along_z)
        cosine = cosine[:, None, :]
        sine = sine[:, None, :]
        real_parts.append(mid_real * cosine - mid_imag * sine)
        imag_parts.append(mid_real * sine + mid_imag * cosine)
    stacked = jnp.stack([jnp.stack(real_parts, axis=-2), jnp.stack(imag_parts, axis=-2)])
    theta_done = jnp.einsum(
        "...pijt,tu->...piju", stacked, theta_map, precision=lax.Precision.HIGHEST
    )
    phi_done = jnp.einsum(
        "c...piju,pq->...ijqcu", theta_done, phi_map, precision=lax.Precision.HIGHEST
    )
    result_shape = phi_done.shape
    return phi_done.reshape(
        result_shape[:-5]
        + (result_shape[-5] * 4, result_shape[-3] * result_shape[-2] * result_shape[-1])
    )


def local(
    top_adj,
    level1_adj,
    image_offsets,
    image_weights,
    incidence,
    child_list,
    theta_index_top,
    theta_weight_top,
    phi_weight_top,
    theta_index_mid,
    theta_weight_mid,
    phi_weight_mid,
):
    dev_count = lax.axis_size("dev")
    dev_index = lax.axis_index("dev")
    rhs_count = lax.axis_size("rhs")
    exc_local, phi_local, top_boxes, top_width = top_adj.shape
    theta_top_count = top_width // 2
    theta_mid_count = theta_top_count // 2
    theta_low_count = theta_top_count // 4
    phi_top_count = phi_local * dev_count
    phi_mid_count = phi_top_count // 2
    phi_low_count = phi_top_count // 4
    image_total = image_offsets.shape[0] * rhs_count
    own_phi = dev_index * phi_local + jnp.arange(phi_local, dtype=jnp.int32)
    own_x, own_y, top_z = directions(theta_top_count, own_phi, phi_top_count)
    scaled = image_weights * float(image_total) ** (-0.5)
    part_real, part_imag = lattice_sum(
        image_offsets.astype(jnp.float32), scaled, incidence, own_x, own_y
    )
    sum_real, sum_imag = (
        lax.psum_scatter(part_real, "rhs", scatter_dimension=0, tiled=True),
        lax.psum_scatter(part_imag, "rhs", scatter_dimension=0, tiled=True),
    )
    sum_real = sum_real[:, :, None, :]
    sum_imag = sum_imag[:, :, None, :]
    top_real = top_adj[..., :theta_top_count]
    top_imag = top_adj[..., theta_top_count:]
    shifted = jnp.concatenate(
        [sum_real * top_real + sum_imag * top_imag, sum_real * top_imag - sum_imag * top_real],
        axis=-1,
    )
    theta_top = theta_matrix(theta_index_top, theta_weight_top, theta_mid_count)
    mid_all = jnp.arange(phi_mid_count, dtype=jnp.int32)
    mid_x, mid_y, mid_z = directions(theta_mid_count, mid_all, phi_mid_count)
    theta_mid = theta_matrix(theta_index_mid, theta_weight_mid, theta_low_count)
    phi_mid = phi_matrix(
        phi_weight_mid, mid_all, phi_low_count, jnp.arange(phi_low_count, dtype=jnp.int32)
    )
    padded = padded_2(shifted, (("dev", 1),), 2)
    padded_phi = (
        dev_index * phi_local - 2 + jnp.arange(phi_local + 4, dtype=jnp.int32)
    ) % phi_top_count
    pad_dirs = directions(theta_top_count, padded_phi, phi_top_count)
    picker = (padded_phi[:, None] == jnp.arange(phi_top_count, dtype=jnp.int32)[None, :]).astype(
        jnp.float32
    )
    pad_weight = jnp.dot(
        picker, phi_weight_top, precision=lax.Precision.HIGHEST, preferred_element_type=jnp.float32
    )
    own_mid = dev_index * (phi_local // 2) + jnp.arange(phi_local // 2, dtype=jnp.int32)
    phi_top = phi_matrix(pad_weight, padded_phi, phi_mid_count, own_mid)
    above = upper_level(
        padded[..., :theta_top_count],
        padded[..., theta_top_count:],
        pad_dirs[0],
        pad_dirs[1],
        top_z,
        theta_top,
        phi_top,
        child_list,
        jnp.arange(top_boxes, dtype=jnp.int32),
    )
    total = level1_adj + above
    return lower_level(
        lax.all_to_all(total, "dev", split_axis=2, concat_axis=1, tiled=True),
        mid_x,
        mid_y,
        mid_z,
        theta_mid,
        phi_mid,
    )


def solution(mesh):
    placed = (
        P("rhs", "dev", None, None),
        P("rhs", "dev", None, None),
        P("rhs", None),
        P("rhs"),
        P(),
        P(),
        P(),
        P(),
        P(),
        P(),
        P(),
        P(),
    )
    return jax.shard_map(
        local, mesh=mesh, in_specs=placed, out_specs=P("rhs", "dev", None), check_vma=False
    )
```

profile of v0, /device:TPU:0, one launch (start us, length us, event | category | flops | bytes accessed | tf_op | source)
XLA Modules:
  0.0 58.5 jit_solution(9289653000353431672)
XLA Ops:
  0.2 0.8 %slice_bitcast_fusion.2 = (f32[16]{0:T(128)S(1)}, f32[16]{0:T(128)S(1)}) fusion(f32[16,2]{0,1:T(2,128)} %param.16), kind=kLoop, calls=%fused_computation.166 | loop fusion | bytes 256 | tf_op jit(solution)/shard_map/sub | solution.py:61
  2.4 2.3 %multiply_reduce_fusion.1 = (f32[16,2,128]{2,0,1:T(8,128)S(1)}, f32[16,2,128]{2,0,1:T(8,128)S(1)}) fusion(f32[16,2,128]{2,0,1:T(8,128)S(1)} %get-tuple-element.71, f32[32]{0:T(128)S(1)} %get-tuple-element.62, f32[16,2,128]{2,0,1:T(8,128)S(1)} %get-tuple-element.72, f32[32]{0:T(128)S(1)} %get-tuple-element.61, f32[32]{0:T(128)S(1)} %broadcast_multiply_fusion.2), kind=kLoop, calls=%fused_computation.36 | loop fusion | flops 1040384 | bytes 65920 | tf_op jit(solution)/shard_map/reduce_sum | solution.py:64
  4.8 9.9 %all-reduce.2 = (f32[16,2,128]{2,1,0:T(2,128)S(1)}, f32[16,2,128]{2,1,0:T(2,128)S(1)}) all-reduce(f32[16,2,128]{2,1,0:T(2,128)S(1)} %copy.63, f32[16,2,128]{2,1,0:T(2,128)S(1)} %copy.62), channel_id=3, replica_groups=mesh['dev'=16,'rhs'=2] {'rhs'}, use_global_device_ids=true, to_apply=%region_5.0.clone | all-reduce | flops 8192 | bytes 65536
  14.8 1.2 %dynamic-slice = u32[1]{0:T(128)} dynamic-slice(u32[32]{0:T(128)} %constant.115, u32[]{:T(128)S(6)} %add.397), dynamic_slice_sizes={1} | dynamic-slice | bytes 12
  16.7 1.0 %multiply_add_fusion.1 = (f32[8,2,16,128]{3,2,1,0:T(8,128)S(1)}, f32[8,2,16,128]{3,2,1,0:T(8,128)S(1)}) fusion(f32[8,2,16,256]{3,2,1,0:T(8,128)} %param.12, f32[8,2,128]{2,1,0:T(2,128)S(1)} %constant_dynamic-slice_fusion, f32[8,2,128]{2,1,0:T(2,128)S(1)} %constant_dynamic-slice_fusion.1), kind=kLoop, calls=%fused_computation.58 | loop fusion | flops 196608 | bytes 540672 | tf_op jit(solution)/shard_map/add | solution.py:162
  17.8 4.4 %collective-permute-start.1 = (f32[8,2,16,256]{3,2,1,0:T(8,128)S(1)}, f32[8,2,16,256]{3,2,1,0:T(8,128)S(1)}, u32[]{:S(2)}, u32[]{:S(2)}) collective-permute-start(f32[8,2,16,256]{3,2,1,0:T(8,128)S(1)} %pad_maximum_fusion.1), channel_id=1, source_target_pairs={{2,0},{4,2},{6,4},{8,6},{10,8},{12,10},{14,12},{16,14},{18,16},{20... | collective-permute-start | bytes 786440 | tf_op jit(solution)/shard_map/ppermute | solution.py:22
  22.3 0.8 %subtract_bitcast_fusion.11 = (s32[16]{0:T(128)S(1)}, s32[16]{0:T(128)S(1)}, s32[16]{0:T(128)S(1)}, s32[16]{0:T(128)S(1)}) fusion(s32[16,4]{0,1:T(4,128)} %param.17), kind=kLoop, calls=%fused_computation.161 | loop fusion | flops 80 | bytes 512 | tf_op jit(solution)/shard_map/eq | solution.py:87
  23.2 0.7 %select_reduce_fusion = f32[128,64]{0,1:T(8,128)S(1)} fusion(f32[128,3]{0,1:T(4,128)} %param.19, s32[128,3]{0,1:T(4,128)} %param.18), kind=kLoop, calls=%fused_computation.59 | loop fusion | flops 65536 | bytes 35840 | tf_op jit(solution)/shard_map/reduce_sum | solution.py:43
  24.5 1.9 %collective-permute-done = f32[8,2,16,256]{3,2,1,0:T(8,128)S(1)} collective-permute-done((f32[8,2,16,256]{3,2,1,0:T(8,128)S(1)}, f32[8,2,16,256]{3,2,1,0:T(8,128)S(1)}, u32[]{:S(2)}, u32[]{:S(2)}) %collective-permute-start) | collective-permute-done | bytes 262176 | tf_op jit(solution)/shard_map/ppermute | solution.py:20
  26.8 0.8 %fusion.13 = f32[2,8,6,16,64]{4,3,2,1,0:T(8,128)S(1)} fusion(f32[1,8,6,16,128]{4,3,2,1,0:T(8,128)S(1)} %get-tuple-element.10, f32[1,8,6,16,128]{4,3,2,1,0:T(8,128)S(1)} %get-tuple-element.9, f32[128,64]{0,1:T(8,128)S(1)} %select_reduce_fusion), kind=kOutput, calls=%fused_computation.18 | convolution fusion | flops 151191552 | bytes 1212416 | tf_op jit(solution)/shard_map/...pbt,tu->...pbu/dot_general | solution.py:80
  27.6 1.1 %fusion.11 = f32[1,2,8,16,64]{4,0,3,2,1:T(1,128)S(1)} fusion(f32[2,8,6,16,64]{4,3,2,1,0:T(8,128)S(1)} %fusion.13, f32[6]{0:T(128)S(1)} %fusion.4), kind=kOutput, calls=%fused_computation.15 | convolution fusion | flops 1179648 | bytes 458776 | tf_op jit(solution)/shard_map/...pbu,pq->...qbu/dot_general | solution.py:83
  28.7 0.8 %fusion.17 = f32[2,8,6,16,64]{4,3,2,1,0:T(8,128)S(1)} fusion(f32[1,8,6,16,128]{4,3,2,1,0:T(8,128)S(1)} %get-tuple-element.17, f32[1,8,6,16,128]{4,3,2,1,0:T(8,128)S(1)} %get-tuple-element.18, f32[128,64]{0,1:T(8,128)S(1)} %select_reduce_fusion), kind=kOutput, calls=%fused_computation.22 | convolution fusion | flops 151191552 | bytes 1212416 | tf_op jit(solution)/shard_map/...pbt,tu->...pbu/dot_general | solution.py:80
  29.5 1.1 %fusion.9 = f32[1,2,8,16,64]{4,0,3,2,1:T(1,128)S(1)} fusion(f32[2,8,6,16,64]{4,3,2,1,0:T(8,128)S(1)} %fusion.17, f32[6]{0:T(128)S(1)} %fusion.4), kind=kOutput, calls=%fused_computation.13 | convolution fusion | flops 1179648 | bytes 458776 | tf_op jit(solution)/shard_map/...pbu,pq->...qbu/dot_general | solution.py:83
  30.6 0.8 %fusion.21 = f32[2,8,6,16,64]{4,3,2,1,0:T(8,128)S(1)} fusion(f32[1,8,6,16,128]{4,3,2,1,0:T(8,128)S(1)} %get-tuple-element.19, f32[1,8,6,16,128]{4,3,2,1,0:T(8,128)S(1)} %get-tuple-element.20, f32[128,64]{0,1:T(8,128)S(1)} %select_reduce_fusion), kind=kOutput, calls=%fused_computation.26 | convolution fusion | flops 151191552 | bytes 1212416 | tf_op jit(solution)/shard_map/...pbt,tu->...pbu/dot_general | solution.py:80
  31.4 1.1 %fusion.7 = f32[1,2,8,16,64]{4,0,3,2,1:T(1,128)S(1)} fusion(f32[2,8,6,16,64]{4,3,2,1,0:T(8,128)S(1)} %fusion.21, f32[6]{0:T(128)S(1)} %fusion.4), kind=kOutput, calls=%fused_computation.11 | convolution fusion | flops 1179648 | bytes 458776 | tf_op jit(solution)/shard_map/...pbu,pq->...qbu/dot_general | solution.py:83
  32.7 0.8 %fusion.25 = f32[2,8,6,16,64]{4,3,2,1,0:T(8,128)S(1)} fusion(f32[1,8,6,16,128]{4,3,2,1,0:T(8,128)S(1)} %get-tuple-element.16, f32[1,8,6,16,128]{4,3,2,1,0:T(8,128)S(1)} %get-tuple-element.15, f32[128,64]{0,1:T(8,128)S(1)} %select_reduce_fusion), kind=kOutput, calls=%fused_computation.30 | convolution fusion | flops 151191552 | bytes 1212416 | tf_op jit(solution)/shard_map/...pbt,tu->...pbu/dot_general | solution.py:80
  33.5 1.1 %fusion.5 = f32[1,2,8,16,64]{4,0,3,2,1:T(1,128)S(1)} fusion(f32[2,8,6,16,64]{4,3,2,1,0:T(8,128)S(1)} %fusion.25, f32[6]{0:T(128)S(1)} %fusion.4), kind=kOutput, calls=%fused_computation.9 | convolution fusion | flops 1179648 | bytes 458776 | tf_op jit(solution)/shard_map/...pbu,pq->...qbu/dot_general | solution.py:83
  35.3 1.0 %copy_add_fusion = f32[8,1,64,128]{3,0,1,2:T(8,128)} fusion(f32[8,1,64,128]{3,2,1,0:T(8,128)S(1)} %pad_maximum_fusion.2, f32[8,1,64,128]{3,2,1,0:T(8,128)S(1)} %copy-done.1), kind=kLoop, calls=%fused_computation.48 | loop fusion | flops 65536 | bytes 786432 | tf_op jit(solution)/shard_map/add | solution.py:196
  36.2 5.7 %all-to-all-start = ((f32[8,1,64,128]{3,0,1,2:T(8,128)}), f32[8,1,64,128]{3,0,1,2:T(8,128)S(1)}, u32[]{:S(2)}, u32[]{:S(2)}) async-start(f32[8,1,64,128]{3,0,1,2:T(8,128)} %copy_add_fusion), calls=%async_computation | async-start | bytes 524288 | tf_op jit(solution)/shard_map/all_to_all | solution.py:198
  42.3 9.7 %all-to-all-done = f32[8,1,64,128]{3,0,1,2:T(8,128)S(1)} async-done(((f32[8,1,64,128]{3,0,1,2:T(8,128)}), f32[8,1,64,128]{3,0,1,2:T(8,128)S(1)}, u32[]{:S(2)}, u32[]{:S(2)}) %all-to-all-start) | async-done | bytes 262176 | tf_op jit(solution)/shard_map/all_to_all | solution.py:198
  52.7 1.8 %fusion = f32[2,8,16,4,4,32]{5,2,4,3,1,0:T(8,128)S(1)} fusion(f32[1,8,16,4,4,64]{5,2,4,3,1,0:T(8,128)S(1)} %maximum_bitcast_fusion.1, f32[64,32]{0,1:T(8,128)S(1)} %select_reduce_fusion.1, f32[8,16,4,1,64]{4,1,2,0,3:T(8,128)S(1)} %get-tuple-element.34, f32[8,16,4,1,64]{4,1,2,0,3:T(8,128)S(1)} %get-tuple-element.32, ...), kind=kOutput, calls=%fused_computation | convolution fusion | flops 101318656 | bytes 1581056 | tf_op jit(solution)/shard_map/...pijt,tu->...piju/dot_general | solution.py:109
  54.4 1.1 %convolution_bitcast_fusion = f32[8,4,4,8,2,32]{5,3,2,1,0,4:T(8,128)S(1)} fusion(f32[2,8,16,4,4,32]{5,2,4,3,1,0:T(8,128)S(1)} %fusion, f32[16,8]{0,1:T(8,128)S(1)} %select_reduce_fusion.2), kind=kOutput, calls=%fused_computation.4 | convolution fusion | flops 12582912 | bytes 786944 | tf_op jit(solution)/shard_map/c...piju,pq->...ijqcu/dot_general | solution.py:112
  55.6 0.8 %copy.72 = f32[8,4,4,8,2,32]{5,4,3,2,1,0:T(2,128)S(1)} copy(f32[8,4,4,8,2,32]{5,3,2,1,0,4:T(8,128)S(1)} %convolution_bitcast_fusion) | data formatting | bytes 524288 | tf_op jit(solution)/shard_map/c...piju,pq->...ijqcu/transpose | solution.py:112
  56.4 2.1 %reshape.1499 = f32[8,16,512]{2,1,0:T(8,128)} reshape(f32[8,4,4,8,2,32]{5,4,3,2,1,0:T(2,128)S(1)} %copy.72) | data formatting | bytes 524288 | tf_op jit(solution)/shard_map/reshape | solution.py:116
  (48 shorter events, 4.4 us)
Async XLA Ops:
  0.0 24.1 %copy-start = (f32[32,3]{0,1:T(4,128)S(1)}, f32[32,3]{0,1:T(4,128)}, u32[]{:S(2)}) copy-start(f32[32,3]{0,1:T(4,128)} %param.20) | copy-start | bytes 1156
  17.7 8.6 %collective-permute-start = (f32[8,2,16,256]{3,2,1,0:T(8,128)S(1)}, f32[8,2,16,256]{3,2,1,0:T(8,128)S(1)}, u32[]{:S(2)}, u32[]{:S(2)}) collective-permute-start(f32[8,2,16,256]{3,2,1,0:T(8,128)S(1)} %pad_maximum_fusion.1), channel_id=1, source_target_pairs={{0,2},{2,4},{4,6},{6,8},{8,10},{10,12},{12,14},{14,16},{16,18},{18... | collective-permute-start | bytes 786440 | tf_op jit(solution)/shard_map/ppermute | solution.py:20
  17.8 8.6 %collective-permute-start.1 = (f32[8,2,16,256]{3,2,1,0:T(8,128)S(1)}, f32[8,2,16,256]{3,2,1,0:T(8,128)S(1)}, u32[]{:S(2)}, u32[]{:S(2)}) collective-permute-start(f32[8,2,16,256]{3,2,1,0:T(8,128)S(1)} %pad_maximum_fusion.1), channel_id=1, source_target_pairs={{2,0},{4,2},{6,4},{8,6},{10,8},{12,10},{14,12},{16,14},{18,16},{20... | collective-permute-start | bytes 786440 | tf_op jit(solution)/shard_map/ppermute | solution.py:22
  33.4 1.8 %copy-start.1 = (f32[8,1,64,128]{3,2,1,0:T(8,128)S(1)}, f32[8,1,64,128]{3,2,1,0:T(8,128)}, u32[]{:S(2)}) copy-start(f32[8,1,64,128]{3,2,1,0:T(8,128)} %param.13) | copy-start | bytes 786436
  34.6 7.4 %copy-start.4 = (f32[16,3]{0,1:T(4,128)S(1)}, f32[16,3]{0,1:T(4,128)}, u32[]{:S(2)}) copy-start(f32[16,3]{0,1:T(4,128)} %param.23) | copy-start | bytes 580
  34.6 7.4 %copy-start.2 = (f32[64,3]{0,1:T(4,128)S(1)}, f32[64,3]{0,1:T(4,128)}, u32[]{:S(2)}) copy-start(f32[64,3]{0,1:T(4,128)} %param.22) | copy-start | bytes 2308
  34.6 7.4 %copy-start.3 = (s32[64,3]{0,1:T(4,128)S(1)}, s32[64,3]{0,1:T(4,128)}, u32[]{:S(2)}) copy-start(s32[64,3]{0,1:T(4,128)} %param.21) | copy-start | bytes 2308
  36.2 15.7 %all-to-all-start = ((f32[8,1,64,128]{3,0,1,2:T(8,128)}), f32[8,1,64,128]{3,0,1,2:T(8,128)S(1)}, u32[]{:S(2)}, u32[]{:S(2)}) async-start(f32[8,1,64,128]{3,0,1,2:T(8,128)} %copy_add_fusion), calls=%async_computation | async-start | bytes 524288 | tf_op jit(solution)/shard_map/all_to_all | solution.py:198
where the time goes:
time: 58.9 us; the launch traced here: 58.5 us
  waiting for transfers between devices  11.6 us (20%)
  matrix products  10.7 us (18%)
  starting transfers between devices  10.2 us (17%)
  blocking collectives  9.94 us (17%)
  other arithmetic  9.84 us (17%)
  local copies, waits for them, and re-layouts  5.15 us (9%)
  between operations  1.03 us (2%)
    unnamed x1, blocking collectives  9.94 us
    all_to_all x1, waiting for transfers between devices, local(): lax.all_to_all(total, 'dev', split_axis=2, concat_axis=1, tiled=True)  9.69 us
    all_to_all x1, starting transfers between devices, local(): lax.all_to_all(total, 'dev', split_axis=2, concat_axis=1, tiled=True)  5.73 us
    dot_general x4, matrix products, upper_level(): jnp.einsum('...pbu,pq->...qbu', theta_done, phi_map, precision=lax.Precis...  4.54 us
    ppermute x1, starting transfers between devices, padded_2(): lax.ppermute(head, axis, [((i + 1) % count, i) for i in range(count)])  4.43 us
    dot_general x4, matrix products, upper_level(): jnp.einsum('...pbt,tu->...pbu', stacked, theta_map, precision=lax.Precisi...  3.09 us
    reduce_sum x1, other arithmetic, lattice_sum(): jnp.sum(weighted[:, None, None, None] * jnp.cos(phase_arg), axis=0)  2.35 us
    reshape x1, local copies, waits for them, and re-layouts, lower_level(): phi_done.reshape(result_shape[:-5] + (result_shape[-5] * 4, result_shape[...  2.08 us
  transfers between devices with their start and end apart: 3, of which 2 were waited for; matrix products, arithmetic and copies ran while one was open for 4% of the time, Pallas kernels for 0%

commit v1 on v0

v1 whole, which is shorter than its diff:
```python
import math

import jax
import jax.numpy as jnp
from jax import lax
from jax.experimental import pallas as pl
from jax.experimental.pallas import tpu as pltpu
from jax.sharding import PartitionSpec as P

PHASE_TOP = 18.85
PHASE_MID = 9.42
LATTICE = 12.57
LANES = 128
HIGHEST = lax.Precision.HIGHEST
VMEM = pl.BlockSpec(memory_space=pltpu.VMEM)
SMEM = pl.BlockSpec(memory_space=pltpu.SMEM)


def sincos(x):
    n = jnp.floor(x * (2.0 / math.pi) + 0.5)
    r = x - n * 1.5703125
    r = r - n * 4.837512969970703125e-4
    r = r - n * 7.54978995489188216e-8
    z = r * r
    s = r + r * z * (-1.6666654611e-1 + z * (8.3321608736e-3 - z * 1.9515295891e-4))
    c = (1.0 - 0.5 * z) + z * z * (
        4.166664568298827e-2 + z * (-1.388731625493765e-3 + z * 2.443315711809948e-5)
    )
    quadrant = n.astype(jnp.int32)
    swap = (quadrant & 1) == 1
    sine = jnp.where(swap, c, s)
    cosine = jnp.where(swap, s, c)
    sine = jnp.where((quadrant & 2) == 2, -sine, sine)
    cosine = jnp.where(((quadrant + 1) & 2) == 2, -cosine, cosine)
    return sine, cosine


def directions(shape, theta_count, phi_count, row0=0):
    rows = lax.broadcasted_iota(jnp.int32, shape, 0).astype(jnp.float32) + row0
    cols = lax.broadcasted_iota(jnp.int32, shape, 1)
    theta = math.pi / theta_count * ((cols % theta_count).astype(jnp.float32) + 0.5)
    sin_theta, cos_theta = sincos(theta)
    sin_phi, cos_phi = sincos(2.0 * math.pi / phi_count * rows)
    return cos_phi * sin_theta, sin_phi * sin_theta, cos_theta


def cmul(ar, ai, br, bi):
    return ar * br - ai * bi, ar * bi + ai * br


def loop(count, body):
    if count <= 16:
        for step in range(count):
            body(step)
    else:
        lax.fori_loop(0, count, lambda step, carry: (body(step), carry)[1], 0)


def pack_kernel(dests, per_dest, re_ref, im_ref, l_ref, o_ref):
    exc, phi_local, boxes, _ = re_ref.shape
    mids = l_ref.shape[2]
    mid_phi = l_ref.shape[1]
    a_rows = [ref.reshape(exc * phi_local * boxes, LANES) for ref in (re_ref, im_ref)]
    l_rows = l_ref.reshape(exc * mid_phi * mids, LANES)
    for dest in range(dests):
        tile = 0
        for phi in range(phi_local):
            for box in range(per_dest):
                row = phi * boxes + dest * per_dest + box
                for part in range(2):
                    o_ref[dest, tile] = a_rows[part][pl.ds(row, exc, stride=phi_local * boxes), :]
                    tile += 1
        for phi in range(mid_phi):
            for mid in range(4 * per_dest):
                row = phi * mids + dest * 4 * per_dest + mid
                o_ref[dest, tile] = l_rows[pl.ds(row, exc, stride=mid_phi * mids), :]
                tile += 1


def pack(top_adj, level1_adj, dev_count):
    exc, phi_local, boxes, width = top_adj.shape
    mid_phi, mids = level1_adj.shape[1:3]
    per_dest = boxes // dev_count
    block = 8
    dests = block // per_dest
    tiles = phi_local * per_dest * (width // LANES) + mid_phi * 4 * per_dest
    return pl.pallas_call(
        lambda *refs: pack_kernel(dests, per_dest, *refs),
        grid=(boxes // block,),
        in_specs=[
            pl.BlockSpec((exc, phi_local, block, LANES), lambda g: (0, 0, g, 0)),
            pl.BlockSpec((exc, phi_local, block, LANES), lambda g: (0, 0, g, 1)),
            pl.BlockSpec((exc, mid_phi, 4 * block, LANES), lambda g: (0, 0, g, 0)),
        ],
        out_specs=pl.BlockSpec((dests, tiles, exc, LANES), lambda g: (g, 0, 0, 0)),
        out_shape=jax.ShapeDtypeStruct((dev_count, tiles, exc, LANES), jnp.float32),
        compiler_params=pltpu.CompilerParams(vmem_limit_bytes=8 << 20),
        name="pack",
    )(top_adj, top_adj, level1_adj)


def theta_block(index_ref, weight_ref, columns):
    samples = index_ref.shape[1]
    rows = lax.broadcasted_iota(jnp.int32, (columns, samples), 0)
    total = jnp.zeros((columns, samples), jnp.float32)
    for s in range(3):
        hit = rows == index_ref[s : s + 1, :]
        total = total + jnp.where(hit, weight_ref[s : s + 1, :], 0.0)
    return total


def coef_kernel(
    sizes,
    where_ref,
    inc_ref,
    child_ref,
    phi_top_ref,
    phi_mid_ref,
    img_ref,
    index_top_ref,
    weight_top_ref,
    index_mid_ref,
    weight_mid_ref,
    w_ref,
    pw2_ref,
    pw1_ref,
    m2_ref,
    m1_ref,
    tc_ref,
    ts_ref,
    dir_ref,
    ph_ref,
    ob_ref,
):
    exc, np2, np1, nt2, images, per_dev = sizes
    nt1, nt0 = nt2 // 2, nt2 // 4
    half = np2 // 2
    first_box = where_ref[0] * per_dev
    first_exc = where_ref[1] * exc

    def splat_top(p):
        for s in range(3):
            pw2_ref[p * 3 + s] = jnp.full((exc, LANES), phi_top_ref[s, p], jnp.float32)

    def splat_mid(p):
        for s in range(3):
            pw1_ref[p * 3 + s] = jnp.full((exc, LANES), phi_mid_ref[s, p], jnp.float32)

    loop(np2, splat_top)
    loop(np1, splat_mid)

    m2_ref[...] = jnp.zeros(m2_ref.shape, jnp.float32)
    m1_ref[...] = jnp.zeros(m1_ref.shape, jnp.float32)
    theta_top = theta_block(index_top_ref, weight_top_ref, nt1)
    theta_mid = theta_block(index_mid_ref, weight_mid_ref, nt0)
    for part in range(2):
        m2_ref[part * nt1 : (part + 1) * nt1, part * nt2 : (part + 1) * nt2] = theta_top
    for part in range(4):
        m1_ref[part * nt0 : (part + 1) * nt0, part * nt1 : (part + 1) * nt1] = theta_mid

    mx, my, mz = directions((np1, LANES), nt1, np1)
    sxs, sxc = sincos(PHASE_MID * mx)
    sys_, syc = sincos(PHASE_MID * my)
    szs, szc = sincos(PHASE_MID * mz)
    lane = lax.broadcasted_iota(jnp.int32, (np1, LANES), 1)
    sign = jnp.where(lane < nt1, -1.0, 1.0)
    for octant in range(4):
        fx = 2.0 * (octant % 2) - 1.0
        fy = 2.0 * (octant // 2) - 1.0
        re, im = cmul(sxc, fx * sxs, syc, fy * sys_)
        re, im = cmul(re, im, szc, -szs)
        tc_ref[octant * np1 : (octant + 1) * np1, :] = re
        ts_ref[octant * np1 : (octant + 1) * np1, :] = im * sign

    ux, uy, uz = directions((np2, LANES), nt2, np2)
    dir_ref[0] = ux
    dir_ref[1] = uy
    axs, axc = sincos(PHASE_TOP * ux)
    ays, ayc = sincos(PHASE_TOP * uy)
    azs, azc = sincos(PHASE_TOP * uz)
    for box in range(per_dev):
        for slot in range(4):
            fx = jnp.float32(0.0)
            fy = jnp.float32(0.0)
            for octant in range(4):
                hit = child_ref[first_box + box, octant] == 4 * (first_box + box) + slot
                fx = fx + jnp.where(hit, jnp.float32(2.0 * (octant % 2) - 1.0), jnp.float32(0.0))
                fy = fy + jnp.where(hit, jnp.float32(2.0 * (octant // 2) - 1.0), jnp.float32(0.0))
            re, im = cmul(axc, fx * axs, ayc, fy * ays)
            re, im = cmul(re, im, azc, -azs)
            ph_ref[box * 8 + slot * 2] = re
            ph_ref[box * 8 + slot * 2 + 1] = im

    image = img_ref[...]
    ox, oy, wt = image[0:1, :], image[1:2, :], image[2:3, :]
    excs = lax.broadcasted_iota(jnp.int32, (exc, LANES), 0)
    kx = jnp.zeros((exc, LANES), jnp.float32)
    ky = jnp.zeros((exc, LANES), jnp.float32)
    for e in range(exc):
        kx = jnp.where(excs == e, inc_ref[0, first_exc + e], kx)
        ky = jnp.where(excs == e, inc_ref[1, first_exc + e], ky)
    fs, fc = sincos(LATTICE * (ox * kx + oy * ky))
    wc = (wt * fc)[:, :images]
    ws = (wt * fs)[:, :images]
    left_c = jnp.concatenate([wc, -ws, wc, -ws], axis=0)
    left_s = jnp.concatenate([ws, wc, -ws, -wc], axis=0)
    ob_ref[0] = jnp.transpose(jnp.broadcast_to(LATTICE * ox, (LANES, LANES)))[:images]
    ob_ref[1] = jnp.transpose(jnp.broadcast_to(LATTICE * oy, (LANES, LANES)))[:images]

    def lattice(p):
        ux_row = dir_ref[0, pl.ds(p, 1), :]
        uy_row = dir_ref[1, pl.ds(p, 1), :]
        sb, cb = sincos(ob_ref[0] * ux_row + ob_ref[1] * uy_row)
        total = jnp.dot(
            left_c, cb, precision=HIGHEST, preferred_element_type=jnp.float32
        ) + jnp.dot(left_s, sb, precision=HIGHEST, preferred_element_type=jnp.float32)
        for mirror in range(2):
            sr = total[(2 * mirror) * exc : (2 * mirror + 1) * exc]
            si = total[(2 * mirror + 1) * exc : (2 * mirror + 2) * exc]
            q = p + mirror * half
            for tile in range(4 * per_dev):
                pr = ph_ref[2 * tile, pl.ds(q, 1), :]
                pi = ph_ref[2 * tile + 1, pl.ds(q, 1), :]
                re, im = cmul(pr, pi, sr, -si)
                w_ref[q, 2 * tile] = re
                w_ref[q, 2 * tile + 1] = im

    loop(half, lattice)


def coefficients(where, inc, child, phi_top, phi_mid, img, tit, twt, tim, twm, exc, nt2, images):
    np2, np1 = phi_top.shape[1], phi_mid.shape[1]
    nt1 = nt2 // 2
    per_dev = images[1]
    sizes = (exc, np2, np1, nt2, images[0], per_dev)
    f32 = jnp.float32
    return pl.pallas_call(
        lambda *refs: coef_kernel(sizes, *refs),
        in_specs=[SMEM] * 5 + [VMEM] * 5,
        out_specs=[VMEM] * 7,
        out_shape=[
            jax.ShapeDtypeStruct((np2, 8 * per_dev, exc, LANES), f32),
            jax.ShapeDtypeStruct((np2 * 3, exc, LANES), f32),
            jax.ShapeDtypeStruct((np1 * 3, exc, LANES), f32),
            jax.ShapeDtypeStruct((LANES, 2 * nt2), f32),
            jax.ShapeDtypeStruct((LANES, 4 * nt1), f32),
            jax.ShapeDtypeStruct((4 * np1, LANES), f32),
            jax.ShapeDtypeStruct((4 * np1, LANES), f32),
        ],
        scratch_shapes=[
            pltpu.VMEM((2, np2, LANES), f32),
            pltpu.VMEM((8 * per_dev, np2, LANES), f32),
            pltpu.VMEM((2, images[0], LANES), f32),
        ],
        compiler_params=pltpu.CompilerParams(vmem_limit_bytes=32 << 20),
        name="coefficients",
    )(where, inc, child, phi_top, phi_mid, img, tit, twt, tim, twm)


def phi_pass(count, contribution, emit):
    first = contribution(count - 1)
    second = contribution(0)
    carry = [x + y for x, y in zip(first[2], second[1])], list(second[2])

    def step(q, carry):
        here, after = carry
        new = contribution((q + 1) % count if isinstance(q, int) else lax.rem(q + 1, count))
        emit(q, [x + y for x, y in zip(here, new[0])])
        return [x + y for x, y in zip(after, new[1])], list(new[2])

    if count <= 16:
        for q in range(count):
            carry = step(q, carry)
    else:
        lax.fori_loop(0, count, step, carry)


def main_kernel(
    sizes,
    r_ref,
    w_ref,
    pw2_ref,
    pw1_ref,
    m2_ref,
    m1_ref,
    tc_ref,
    ts_ref,
    o_ref,
    x_ref,
    g_ref,
    h_ref,
    y_ref,
    z_ref,
):
    exc, np2, np1, nt2, phi_local, per_dev = sizes
    np0 = np1 // 2
    mid_local = phi_local // 2
    base = phi_local * per_dev * 2
    mids = 4 * per_dev
    nt = (((1,), (1,)), ((), ()))

    for box in range(per_dev):

        def top(m, box=box):
            out = [[None] * 8 for _ in range(3)]
            for parity in range(2):
                p = 2 * m + parity
                tile = ((p % phi_local) * per_dev + box) * 2
                ar = r_ref[p // phi_local, tile]
                ai = r_ref[p // phi_local, tile + 1]
                weights = [pw2_ref[3 * p + s] for s in range(3)]
                for slot in range(4):
                    wr = w_ref[p, box * 8 + slot * 2]
                    wi = w_ref[p, box * 8 + slot * 2 + 1]
                    for c, value in enumerate(cmul(ar, ai, wr, wi)):
                        for s in range(3):
                            term = weights[s] * value
                            k = slot * 2 + c
                            out[s][k] = term if out[s][k] is None else out[s][k] + term
            return out

        def keep(q, values):
            for slot in range(4):
                for c in range(2):
                    x_ref[
                        pl.ds((q * 4 + slot) * exc, exc), c * LANES : (c + 1) * LANES
                    ] = values[slot * 2 + c]

        phi_pass(np1, top, keep)
        rows = x_ref.shape[0]
        block = min(rows, 512)

        def theta(part, box=box):
            done = lax.dot_general(
                x_ref[pl.ds(part * block, block), :],
                m2_ref[...],
                nt,
                precision=HIGHEST,
                preferred_element_type=jnp.float32,
            )
            per_block = block // (4 * exc)
            for n in range(per_block):
                q = part * per_block + n
                for slot in range(4):
                    row = (n * 4 + slot) * exc
                    mid = box * 4 + slot
                    value = (
                        done[row : row + exc]
                        + r_ref[q // mid_local, base + (q % mid_local) * mids + mid]
                    )
                    g_ref[q, mid] = value
                    h_ref[q, mid] = pltpu.roll(value, LANES // 2, 1)

        loop(rows // block, theta)

    o_rows = o_ref.reshape(exc * 4 * mids, o_ref.shape[2])

    for octant in range(4):
        for box in range(per_dev):

            def middle(m, octant=octant, box=box):
                out = [[None] * 4 for _ in range(3)]
                for parity in range(2):
                    q = 2 * m + parity
                    cosine = tc_ref[pl.ds(octant * np1 + q, 1), :]
                    sine = ts_ref[pl.ds(octant * np1 + q, 1), :]
                    weights = [pw1_ref[3 * q + s] for s in range(3)]
                    for slot in range(4):
                        value = (
                            g_ref[q, box * 4 + slot] * cosine + h_ref[q, box * 4 + slot] * sine
                        )
                        for s in range(3):
                            term = weights[s] * value
                            out[s][slot] = term if out[s][slot] is None else out[s][slot] + term
                return out

            def keep_low(q, values, octant=octant, box=box):
                for slot in range(4):
                    k = (box * 4 + slot) * 4 + octant
                    y_ref[q // 2, pl.ds(k * exc, exc), pl.ds((q % 2) * LANES, LANES)] = values[
                        slot
                    ]

            phi_pass(np0, middle, keep_low)

    def finish(pair):
        done = lax.dot_general(
            y_ref[pair],
            m1_ref[...],
            nt,
            precision=HIGHEST,
            preferred_element_type=jnp.float32,
        )
        start = pair * LANES
        lanes = pl.ds(start if isinstance(pair, int) else pl.multiple_of(start, LANES), LANES)
        for k in range(4 * mids):
            z_ref[pl.ds(k, exc, stride=4 * mids), :] = done[k * exc : (k + 1) * exc]
        o_rows[:, lanes] = z_ref[...]

    loop(np0 // 2, finish)


def main(received, coefs, exc, np2, np1, nt2, phi_local, per_dev):
    mids = 4 * per_dev
    np0 = np1 // 2
    f32 = jnp.float32
    sizes = (exc, np2, np1, nt2, phi_local, per_dev)
    return pl.pallas_call(
        lambda *refs: main_kernel(sizes, *refs),
        in_specs=[VMEM] * 8,
        out_specs=VMEM,
        out_shape=jax.ShapeDtypeStruct((exc, 4 * mids, np0 * (nt2 // 2)), f32),
        scratch_shapes=[
            pltpu.VMEM((np1 * 4 * exc, 2 * LANES), f32),
            pltpu.VMEM((np1, mids, exc, LANES), f32),
            pltpu.VMEM((np1, mids, exc, LANES), f32),
            pltpu.VMEM((np0 // 2, 4 * mids * exc, 2 * LANES), f32),
            pltpu.VMEM((4 * mids * exc, LANES), f32),
        ],
        compiler_params=pltpu.CompilerParams(vmem_limit_bytes=56 << 20),
        name="levels",
    )(received, *coefs)


def local(
    top_adj,
    level1_adj,
    image_offsets,
    image_weights,
    incidence,
    child_list,
    theta_index_top,
    theta_weight_top,
    phi_weight_top,
    theta_index_mid,
    theta_weight_mid,
    phi_weight_mid,
):
    dev_count = lax.axis_size("dev")
    rhs_count = lax.axis_size("rhs")
    exc, phi_local, top_boxes, top_width = top_adj.shape
    per_dev = top_boxes // dev_count
    nt2 = top_width // 2
    np2 = phi_local * dev_count
    np1 = np2 // 2
    images = image_offsets.shape[0] * rhs_count

    packed = pack(top_adj, level1_adj, dev_count)
    received = lax.all_to_all(packed, "dev", split_axis=0, concat_axis=0, tiled=True)

    own = jnp.concatenate(
        [
            image_offsets.T.astype(jnp.float32),
            image_weights[None] * float(images) ** (-0.5),
        ],
        axis=0,
    )
    parts = [own]
    for shift in range(1, rhs_count):
        parts.append(
            lax.ppermute(own, "rhs", [(i, (i + shift) % rhs_count) for i in range(rhs_count)])
        )
    img = jnp.concatenate(parts + [jnp.zeros((3, LANES - images), jnp.float32)], axis=1)
    where = jnp.stack([lax.axis_index("dev"), lax.axis_index("rhs")]).astype(jnp.int32)
    coefs = coefficients(
        where,
        incidence.T,
        child_list,
        phi_weight_top.T,
        phi_weight_mid.T,
        img,
        theta_index_top.T,
        theta_weight_top.T,
        theta_index_mid.T,
        theta_weight_mid.T,
        exc,
        nt2,
        (images, per_dev),
    )
    return main(received, coefs, exc, np2, np1, nt2, phi_local, per_dev)


def solution(mesh):
    placed = (
        P("rhs", "dev", None, None),
        P("rhs", "dev", None, None),
        P("rhs", None),
        P("rhs"),
        P(),
        P(),
        P(),
        P(),
        P(),
        P(),
        P(),
        P(),
    )
    return jax.shard_map(
        local, mesh=mesh, in_specs=placed, out_specs=P("rhs", "dev", None), check_vma=False
    )
```

time: 58.9 us -> 29.9 us (0.51)
  matrix products: 10.7 us -> 0 us
  blocking collectives: 9.94 us -> 0 us
  other arithmetic: 9.84 us -> 0.17 us
  waiting for transfers between devices: 11.6 us -> 2.83 us
  Pallas kernels: 0 us -> 7.61 us
  local copies, waits for them, and re-layouts: 5.15 us -> 9.74 us
  starting transfers between devices: 10.2 us -> 9.1 us
  between operations: 1.03 us -> 0.1 us
    dot_general x11 -> x0, matrix products: 10.7 us -> none  [the longest x4 4.54 us: upper_level(): jnp.einsum('...pbu,pq->...qbu', theta_done, phi_map, precision=lax.Precis...]
    unnamed x1 -> x0, blocking collectives: 9.94 us -> none
    unnamed x13 -> x41, local copies, waits for them, and re-layouts: 1.29 us -> 9.66 us
    all_to_all x1, waiting for transfers between devices: 9.69 us -> 1.59 us  [local(): lax.all_to_all(packed, 'dev', split_axis=0, concat_axis=0, tiled=True)]
    pallas_call x0 -> x3, Pallas kernels: none -> 7.61 us  [the longest x1 3.99 us: main(): pl.pallas_call(lambda *refs: main_kernel(sizes, *refs), in_specs=[VMEM] *...]
    reduce_sum x4 -> x0, other arithmetic: 3.09 us -> none  [the longest x1 2.35 us: lattice_sum(): jnp.sum(weighted[:, None, None, None] * jnp.cos(phase_arg), axis=0)]
    ppermute x2 -> x1, starting transfers between devices: 4.49 us -> 1.55 us  [local(): lax.ppermute(own, 'rhs', [(i, (i + shift) % rhs_count) for i in range(rhs...]
    add x3 -> x0, other arithmetic: 2.41 us -> none  [the longest x1 1.01 us: local(): sum_real * top_real + sum_imag * top_imag]
  transfers between devices with their start and end apart: 3 -> 2, of which waited for: 2 -> 2; matrix products, arithmetic and copies ran while one was open for 4% -> 1% of each run, Pallas kernels for 0% -> 9%
where the time goes in v1:
time: 29.9 us; the launch traced here: 29.5 us
  local copies, waits for them, and re-layouts  9.74 us (33%)
  starting transfers between devices  9.1 us (30%)
  Pallas kernels  7.61 us (25%)
  waiting for transfers between devices  2.83 us (9%)
    unnamed x41, local copies, waits for them, and re-layouts  9.66 us
    all_to_all x1, starting transfers between devices, local(): lax.all_to_all(packed, 'dev', split_axis=0, concat_axis=0, tiled=True)  7.55 us
    pallas_call x1, Pallas kernels, main(): pl.pallas_call(lambda *refs: main_kernel(sizes, *refs), in_specs=[VMEM] *...  3.99 us
    pallas_call x1, Pallas kernels, coefficients(): pl.pallas_call(lambda *refs: coef_kernel(sizes, *refs), in_specs=[SMEM] *...  2.6 us
    all_to_all x1, waiting for transfers between devices, local(): lax.all_to_all(packed, 'dev', split_axis=0, concat_axis=0, tiled=True)  1.59 us
    ppermute x1, starting transfers between devices, local(): lax.ppermute(own, 'rhs', [(i, (i + shift) % rhs_count) for i in range(rhs...  1.55 us
    ppermute x1, waiting for transfers between devices, local(): lax.ppermute(own, 'rhs', [(i, (i + shift) % rhs_count) for i in range(rhs...  1.24 us
    pallas_call x1, Pallas kernels, pack(): pl.pallas_call(lambda *refs: pack_kernel(dests, per_dest, *refs), grid=(b...  1.02 us
  transfers between devices with their start and end apart: 2, of which 2 were waited for; matrix products, arithmetic and copies ran while one was open for 1% of the time, Pallas kernels for 9%

profile of v1, /device:TPU:0, one launch (start us, length us, event | category | flops | bytes accessed | tf_op | source)
XLA Modules:
  0.0 29.5 jit_solution(14182780559761073177)
XLA Ops:
  0.0 0.9 %copy-done = f32[8,2,16,256]{3,2,1,0:T(8,128)S(1)} copy-done((f32[8,2,16,256]{3,2,1,0:T(8,128)S(1)}, f32[8,2,16,256]{3,2,1,0:T(8,128)}, u32[]{:S(2)}) %copy-start) | copy-done | bytes 262168
  1.0 0.9 %copy-done.3 = f32[8,1,64,128]{3,2,1,0:T(8,128)S(1)} copy-done((f32[8,1,64,128]{3,2,1,0:T(8,128)S(1)}, f32[8,1,64,128]{3,2,1,0:T(8,128)}, u32[]{:S(2)}) %copy-start.3) | copy-done | bytes 262168
  1.9 1.0 %pack.1 = f32[16,8,8,128]{3,2,1,0:T(8,128)} custom-call(f32[8,2,16,256]{3,2,1,0:T(8,128)S(1)} %copy-done, f32[8,2,16,256]{3,2,1,0:T(8,128)S(1)} %copy-done, f32[8,1,64,128]{3,2,1,0:T(8,128)S(1)} %copy-done.3), custom_call_target="tpu_custom_call" | custom-call | tf_op jit(solution)/shard_map/pack/pallas_call | solution.py:87
  2.9 7.5 %all-to-all-start = ((f32[16,8,8,128]{3,2,1,0:T(8,128)}), f32[16,8,8,128]{3,2,1,0:T(8,128)S(1)}, u32[]{:S(2)}, u32[]{:S(2)}) async-start(f32[16,8,8,128]{3,2,1,0:T(8,128)} %pack.1), calls=%async_computation | async-start | bytes 1048576 | tf_op jit(solution)/shard_map/all_to_all | solution.py:449
  10.5 0.7 %copy-done.18 = s32[32,2]{0,1:T(2,128)S(1)} copy-done((s32[32,2]{0,1:T(2,128)S(1)}, s32[32,2]{0,1:T(2,128)}, u32[]{:S(2)}) %copy-start.18) | copy-done | bytes 280
  11.2 1.6 %collective-permute-start = (f32[3,32]{1,0:T(4,128)S(1)}, f32[3,32]{1,0:T(4,128)S(1)}, u32[]{:S(2)}, u32[]{:S(2)}) collective-permute-start(f32[3,32]{1,0:T(4,128)S(1)} %pad_maximum_fusion), channel_id=1, source_target_pairs={{0,1},{1,0},{2,3},{3,2},{4,5},{5,4},{6,7},{7,6},{8,9},{9,8},{10,11... | collective-permute-start | bytes 1160 | tf_op jit(solution)/shard_map/ppermute | solution.py:461
  12.7 0.1 pad_add_fusion.refs_0_
  12.8 0.6 %copy-done.17 = s32[16,4]{0,1:T(4,128)S(1)} copy-done((s32[16,4]{0,1:T(4,128)S(1)}, s32[16,4]{0,1:T(4,128)}, u32[]{:S(2)}) %copy-start.17) | copy-done | bytes 280
  13.4 0.1 copy.13.refs_2_
  13.5 0.1 pad.3.clone
  13.6 1.2 %collective-permute-done = f32[3,32]{1,0:T(4,128)S(1)} collective-permute-done((f32[3,32]{1,0:T(4,128)S(1)}, f32[3,32]{1,0:T(4,128)S(1)}, u32[]{:S(2)}, u32[]{:S(2)}) %collective-permute-start) | collective-permute-done | bytes 416 | tf_op jit(solution)/shard_map/ppermute | solution.py:461
  14.8 0.1 maximum_maximum_fusion.refs_5_
  15.0 0.6 %copy-done.10 = f32[16,3]{0,1:T(4,128)S(1)} copy-done((f32[16,3]{0,1:T(4,128)S(1)}, f32[16,3]{0,1:T(4,128)}, u32[]{:S(2)}) %copy-start.10) | copy-done | bytes 216
  15.6 2.6 %coefficients.1 = (f32[32,8,8,128]{3,2,1,0:T(8,128)S(1)}, f32[96,8,128]{2,1,0:T(8,128)S(1)}, f32[48,8,128]{2,1,0:T(8,128)S(1)}, f32[128,256]{1,0:T(8,128)S(1)}, ...) custom-call(s32[2]{0:T(128)S(1)} %pad_add_fusion.refs_0_, f32[2,16]{1,0:T(2,128)S(1)} %bitcast.19, ...), custom_call_target="tpu_custom_call" | custom-call | tf_op jit(solution)/shard_map/coefficients/pallas_call | solution.py:237
  18.2 1.0 %copy-done.1 = f32[32,8,8,128]{3,2,1,0:T(8,128)} copy-done((f32[32,8,8,128]{3,2,1,0:T(8,128)}, f32[32,8,8,128]{3,2,1,0:T(8,128)S(1)}, u32[]{:S(2)}) %copy-start.1) | copy-done | bytes 1048600
  19.2 0.8 %copy-done.2 = f32[96,8,128]{2,1,0:T(8,128)} copy-done((f32[96,8,128]{2,1,0:T(8,128)}, f32[96,8,128]{2,1,0:T(8,128)S(1)}, u32[]{:S(2)}) %copy-start.2) | copy-done | bytes 393240
  20.0 0.7 %copy-done.4 = f32[48,8,128]{2,1,0:T(8,128)} copy-done((f32[48,8,128]{2,1,0:T(8,128)}, f32[48,8,128]{2,1,0:T(8,128)S(1)}, u32[]{:S(2)}) %copy-start.4) | copy-done | bytes 196632
  20.7 0.6 %copy-done.5 = f32[128,256]{1,0:T(8,128)} copy-done((f32[128,256]{1,0:T(8,128)}, f32[128,256]{1,0:T(8,128)S(1)}, u32[]{:S(2)}) %copy-start.5) | copy-done | bytes 131096
  21.3 0.6 %copy-done.6 = f32[128,256]{1,0:T(8,128)} copy-done((f32[128,256]{1,0:T(8,128)}, f32[128,256]{1,0:T(8,128)S(1)}, u32[]{:S(2)}) %copy-start.6) | copy-done | bytes 131096
  21.9 0.6 %copy-done.7 = f32[64,128]{1,0:T(8,128)} copy-done((f32[64,128]{1,0:T(8,128)}, f32[64,128]{1,0:T(8,128)S(1)}, u32[]{:S(2)}) %copy-start.7) | copy-done | bytes 32792
  22.6 0.6 %copy-done.8 = f32[64,128]{1,0:T(8,128)} copy-done((f32[64,128]{1,0:T(8,128)}, f32[64,128]{1,0:T(8,128)S(1)}, u32[]{:S(2)}) %copy-start.8) | copy-done | bytes 32792
  23.2 1.6 %all-to-all-done.refs_0_ = f32[16,8,8,128]{3,2,1,0:T(8,128)S(1)} async-done(((f32[16,8,8,128]{3,2,1,0:T(8,128)}), f32[16,8,8,128]{3,2,1,0:T(8,128)S(1)}, u32[]{:S(2)}, u32[]{:S(2)}) %all-to-all-start) | async-done | bytes 524320 | tf_op jit(solution)/shard_map/all_to_all | solution.py:449
  24.8 0.8 %copy-done.16 = f32[16,8,8,128]{3,2,1,0:T(8,128)} copy-done((f32[16,8,8,128]{3,2,1,0:T(8,128)}, f32[16,8,8,128]{3,2,1,0:T(8,128)S(1)}, u32[]{:S(2)}) %copy-start.16) | copy-done | bytes 524312
  25.6 4.0 %levels.1 = f32[8,16,512]{2,1,0:T(8,128)} custom-call(f32[16,8,8,128]{3,2,1,0:T(8,128)} %copy-done.16, f32[32,8,8,128]{3,2,1,0:T(8,128)} %copy-done.1, f32[96,8,128]{2,1,0:T(8,128)} %copy-done.2, f32[48,8,128]{2,1,0:T(8,128)} %copy-done.4, f32[128,256]{1,0:T(8,128)} %copy-done.5, f32[128,256]{1,0:T(8,128)} %copy-done.6, f32[64,128]{1,0:T(8,128)} %copy-done.7, ...), custom_call_target="tpu_custom_call" | custom-call | tf_op jit(solution)/shard_map/levels/pallas_call | solution.py:408
  (31 shorter events, 0.1 us)
Async XLA Ops:
  0.0 0.9 %copy-start = (f32[8,2,16,256]{3,2,1,0:T(8,128)S(1)}, f32[8,2,16,256]{3,2,1,0:T(8,128)}, u32[]{:S(2)}) copy-start(f32[8,2,16,256]{3,2,1,0:T(8,128)} %refs_1_.1) | copy-start | bytes 786436
  1.0 0.9 %copy-start.3 = (f32[8,1,64,128]{3,2,1,0:T(8,128)S(1)}, f32[8,1,64,128]{3,2,1,0:T(8,128)}, u32[]{:S(2)}) copy-start(f32[8,1,64,128]{3,2,1,0:T(8,128)} %refs_2_.2) | copy-start | bytes 786436
  2.9 7.6 %copy-start.19 = (f32[32]{0:T(128)S(1)}, f32[32]{0:T(128)}, u32[]{:S(2)}) copy-start(f32[32]{0:T(128)} %param.15) | copy-start | bytes 388
  2.9 21.8 %all-to-all-start = ((f32[16,8,8,128]{3,2,1,0:T(8,128)}), f32[16,8,8,128]{3,2,1,0:T(8,128)S(1)}, u32[]{:S(2)}, u32[]{:S(2)}) async-start(f32[16,8,8,128]{3,2,1,0:T(8,128)} %pack.1), calls=%async_computation | async-start | bytes 1048576 | tf_op jit(solution)/shard_map/all_to_all | solution.py:449
  10.5 0.7 %copy-start.18 = (s32[32,2]{0,1:T(2,128)S(1)}, s32[32,2]{0,1:T(2,128)}, u32[]{:S(2)}) copy-start(s32[32,2]{0,1:T(2,128)} %param.14) | copy-start | bytes 772
  11.2 3.6 %collective-permute-start = (f32[3,32]{1,0:T(4,128)S(1)}, f32[3,32]{1,0:T(4,128)S(1)}, u32[]{:S(2)}, u32[]{:S(2)}) collective-permute-start(f32[3,32]{1,0:T(4,128)S(1)} %pad_maximum_fusion), channel_id=1, source_target_pairs={{0,1},{1,0},{2,3},{3,2},{4,5},{5,4},{6,7},{7,6},{8,9},{9,8},{10,11... | collective-permute-start | bytes 1160 | tf_op jit(solution)/shard_map/ppermute | solution.py:461
  12.7 0.7 %copy-start.17 = (s32[16,4]{0,1:T(4,128)S(1)}, s32[16,4]{0,1:T(4,128)}, u32[]{:S(2)}) copy-start(s32[16,4]{0,1:T(4,128)} %param.17) | copy-start | bytes 772
  13.4 1.5 %copy-start.11 = (s32[128,3]{0,1:T(4,128)S(1)}, s32[128,3]{0,1:T(4,128)}, u32[]{:S(2)}) copy-start(s32[128,3]{0,1:T(4,128)} %param.18) | copy-start | bytes 4612
  13.4 1.5 %copy-start.12 = (f32[128,3]{0,1:T(4,128)S(1)}, f32[128,3]{0,1:T(4,128)}, u32[]{:S(2)}) copy-start(f32[128,3]{0,1:T(4,128)} %param.19) | copy-start | bytes 4612
  13.4 1.5 %copy-start.13 = (s32[64,3]{0,1:T(4,128)S(1)}, s32[64,3]{0,1:T(4,128)}, u32[]{:S(2)}) copy-start(s32[64,3]{0,1:T(4,128)} %param.21) | copy-start | bytes 2308
  13.4 1.5 %copy-start.14 = (f32[64,3]{0,1:T(4,128)S(1)}, f32[64,3]{0,1:T(4,128)}, u32[]{:S(2)}) copy-start(f32[64,3]{0,1:T(4,128)} %param.22) | copy-start | bytes 2308
  14.9 0.7 %copy-start.10 = (f32[16,3]{0,1:T(4,128)S(1)}, f32[16,3]{0,1:T(4,128)}, u32[]{:S(2)}) copy-start(f32[16,3]{0,1:T(4,128)} %param.23) | copy-start | bytes 580
  14.9 0.7 %copy-start.9 = (f32[32,3]{0,1:T(4,128)S(1)}, f32[32,3]{0,1:T(4,128)}, u32[]{:S(2)}) copy-start(f32[32,3]{0,1:T(4,128)} %param.20) | copy-start | bytes 1156
  14.9 0.7 %copy-start.15 = (f32[16,2]{0,1:T(2,128)S(1)}, f32[16,2]{0,1:T(2,128)}, u32[]{:S(2)}) copy-start(f32[16,2]{0,1:T(2,128)} %param.16) | copy-start | bytes 388
  18.2 1.0 %copy-start.1 = (f32[32,8,8,128]{3,2,1,0:T(8,128)}, f32[32,8,8,128]{3,2,1,0:T(8,128)S(1)}, u32[]{:S(2)}) copy-start(f32[32,8,8,128]{3,2,1,0:T(8,128)S(1)} %get-tuple-element.12.refs_1_) | copy-start | bytes 3145732
  19.2 0.8 %copy-start.2 = (f32[96,8,128]{2,1,0:T(8,128)}, f32[96,8,128]{2,1,0:T(8,128)S(1)}, u32[]{:S(2)}) copy-start(f32[96,8,128]{2,1,0:T(8,128)S(1)} %get-tuple-element.13.refs_2_) | copy-start | bytes 1179652
  20.0 0.7 %copy-start.4 = (f32[48,8,128]{2,1,0:T(8,128)}, f32[48,8,128]{2,1,0:T(8,128)S(1)}, u32[]{:S(2)}) copy-start(f32[48,8,128]{2,1,0:T(8,128)S(1)} %get-tuple-element.14.refs_3_) | copy-start | bytes 589828
  20.7 0.6 %copy-start.5 = (f32[128,256]{1,0:T(8,128)}, f32[128,256]{1,0:T(8,128)S(1)}, u32[]{:S(2)}) copy-start(f32[128,256]{1,0:T(8,128)S(1)} %get-tuple-element.15.refs_4_) | copy-start | bytes 393220
  21.3 0.6 %copy-start.6 = (f32[128,256]{1,0:T(8,128)}, f32[128,256]{1,0:T(8,128)S(1)}, u32[]{:S(2)}) copy-start(f32[128,256]{1,0:T(8,128)S(1)} %get-tuple-element.16.refs_5_) | copy-start | bytes 393220
  21.9 0.6 %copy-start.7 = (f32[64,128]{1,0:T(8,128)}, f32[64,128]{1,0:T(8,128)S(1)}, u32[]{:S(2)}) copy-start(f32[64,128]{1,0:T(8,128)S(1)} %get-tuple-element.17.refs_6_) | copy-start | bytes 98308
  22.6 0.6 %copy-start.8 = (f32[64,128]{1,0:T(8,128)}, f32[64,128]{1,0:T(8,128)S(1)}, u32[]{:S(2)}) copy-start(f32[64,128]{1,0:T(8,128)S(1)} %get-tuple-element.18.refs_7_) | copy-start | bytes 98308
  24.7 0.8 %copy-start.16 = (f32[16,8,8,128]{3,2,1,0:T(8,128)}, f32[16,8,8,128]{3,2,1,0:T(8,128)S(1)}, u32[]{:S(2)}) copy-start(f32[16,8,8,128]{3,2,1,0:T(8,128)S(1)} %all-to-all-done.refs_0_) | copy-start | bytes 1572868

commit v2 on v1

--- a/solution.py
+++ b/solution.py
@@ -56,47 +56,77 @@
         lax.fori_loop(0, count, lambda step, carry: (body(step), carry)[1], 0)
 
 
-def pack_kernel(dests, per_dest, re_ref, im_ref, l_ref, o_ref):
+def pack_kernel(per_dest, a_hbm, l_hbm, o_hbm, re_ref, im_ref, mid_ref, top_out, mid_out, sems):
     exc, phi_local, boxes, _ = re_ref.shape
-    mids = l_ref.shape[2]
-    mid_phi = l_ref.shape[1]
-    a_rows = [ref.reshape(exc * phi_local * boxes, LANES) for ref in (re_ref, im_ref)]
-    l_rows = l_ref.reshape(exc * mid_phi * mids, LANES)
-    for dest in range(dests):
-        tile = 0
-        for phi in range(phi_local):
-            for box in range(per_dest):
-                row = phi * boxes + dest * per_dest + box
-                for part in range(2):
-                    o_ref[dest, tile] = a_rows[part][pl.ds(row, exc, stride=phi_local * boxes), :]
-                    tile += 1
+    mid_phi, mids = mid_ref.shape[1:3]
+    copies = [
+        pltpu.make_async_copy(a_hbm.at[:, :, :, pl.ds(0, LANES)], re_ref, sems.at[0]),
+        pltpu.make_async_copy(a_hbm.at[:, :, :, pl.ds(LANES, LANES)], im_ref, sems.at[1]),
+        pltpu.make_async_copy(l_hbm, mid_ref, sems.at[2]),
+    ]
+    for copy in copies:
+        copy.start()
+    top_tiles = top_out.shape[1]
+    mid_tiles = mid_out.shape[1]
+
+    for part, ref in enumerate((re_ref, im_ref)):
+        rows = ref.reshape(exc * phi_local * boxes, LANES)
+        copies[part].wait()
+
+        def top(dest, rows=rows, part=part):
+            for phi in range(phi_local):
+                for box in range(per_dest):
+                    row = phi * boxes + dest * per_dest + box
+                    tile = (phi * per_dest + box) * 2 + part
+                    top_out[dest, tile] = rows[pl.ds(row, exc, stride=phi_local * boxes), :]
+
+        loop(boxes // per_dest, top)
+
+    leave = [
+        pltpu.make_async_copy(top_out, o_hbm.at[:, pl.ds(0, top_tiles)], sems.at[3]),
+        pltpu.make_async_copy(mid_out, o_hbm.at[:, pl.ds(top_tiles, mid_tiles)], sems.at[4]),
+    ]
+    leave[0].start()
+    mid_rows = mid_ref.reshape(exc * mid_phi * mids, LANES)
+    copies[2].wait()
+
+    def middle(dest):
         for phi in range(mid_phi):
             for mid in range(4 * per_dest):
                 row = phi * mids + dest * 4 * per_dest + mid
-                o_ref[dest, tile] = l_rows[pl.ds(row, exc, stride=mid_phi * mids), :]
-                tile += 1
+                tile = phi * 4 * per_dest + mid
+                mid_out[dest, tile] = mid_rows[pl.ds(row, exc, stride=mid_phi * mids), :]
+
+    loop(boxes // per_dest, middle)
+    leave[1].start()
+    for copy in leave:
+        copy.wait()
 
 
 def pack(top_adj, level1_adj, dev_count):
-    exc, phi_local, boxes, width = top_adj.shape
+    exc, phi_local, boxes, _ = top_adj.shape
     mid_phi, mids = level1_adj.shape[1:3]
     per_dest = boxes // dev_count
-    block = 8
-    dests = block // per_dest
-    tiles = phi_local * per_dest * (width // LANES) + mid_phi * 4 * per_dest
+    top_tiles = phi_local * per_dest * 2
+    mid_tiles = mid_phi * 4 * per_dest
+    f32 = jnp.float32
+    hbm = pl.BlockSpec(memory_space=pltpu.HBM)
     return pl.pallas_call(
-        lambda *refs: pack_kernel(dests, per_dest, *refs),
-        grid=(boxes // block,),
-        in_specs=[
-            pl.BlockSpec((exc, phi_local, block, LANES), lambda g: (0, 0, g, 0)),
-            pl.BlockSpec((exc, phi_local, block, LANES), lambda g: (0, 0, g, 1)),
-            pl.BlockSpec((exc, mid_phi, 4 * block, LANES), lambda g: (0, 0, g, 0)),
+        lambda *refs: pack_kernel(per_dest, *refs),
+        in_specs=[hbm] * 2,
+        out_specs=hbm,
+        out_shape=jax.ShapeDtypeStruct((dev_count, top_tiles + mid_tiles, exc, LANES), f32),
+        scratch_shapes=[
+            pltpu.VMEM((exc, phi_local, boxes, LANES), f32),
+            pltpu.VMEM((exc, phi_local, boxes, LANES), f32),
+            pltpu.VMEM((exc, mid_phi, mids, LANES), f32),
+            pltpu.VMEM((dev_count, top_tiles, exc, LANES), f32),
+            pltpu.VMEM((dev_count, mid_tiles, exc, LANES), f32),
+            pltpu.SemaphoreType.DMA((5,)),
         ],
-        out_specs=pl.BlockSpec((dests, tiles, exc, LANES), lambda g: (g, 0, 0, 0)),
-        out_shape=jax.ShapeDtypeStruct((dev_count, tiles, exc, LANES), jnp.float32),
-        compiler_params=pltpu.CompilerParams(vmem_limit_bytes=8 << 20),
+        compiler_params=pltpu.CompilerParams(vmem_limit_bytes=67043328),
         name="pack",
-    )(top_adj, top_adj, level1_adj)
+    )(top_adj, level1_adj)
 
 
 def theta_block(index_ref, weight_ref, columns):
@@ -131,6 +161,7 @@
     dir_ref,
     ph_ref,
     ob_ref,
+    fm_ref,
 ):
     exc, np2, np1, nt2, images, per_dev = sizes
     nt1, nt0 = nt2 // 2, nt2 // 4
@@ -149,14 +180,17 @@
     loop(np2, splat_top)
     loop(np1, splat_mid)
 
-    m2_ref[...] = jnp.zeros(m2_ref.shape, jnp.float32)
-    m1_ref[...] = jnp.zeros(m1_ref.shape, jnp.float32)
     theta_top = theta_block(index_top_ref, weight_top_ref, nt1)
     theta_mid = theta_block(index_mid_ref, weight_mid_ref, nt0)
-    for part in range(2):
-        m2_ref[part * nt1 : (part + 1) * nt1, part * nt2 : (part + 1) * nt2] = theta_top
-    for part in range(4):
-        m1_ref[part * nt0 : (part + 1) * nt0, part * nt1 : (part + 1) * nt1] = theta_mid
+    for parts, block, m_ref in ((2, theta_top, m2_ref), (4, theta_mid, m1_ref)):
+        high, width = block.shape
+        fm_ref[...] = jnp.zeros(fm_ref.shape, jnp.float32)
+        for part in range(parts):
+            fm_ref[part * high : (part + 1) * high, part * width : (part + 1) * width] = block
+        full = jnp.transpose(fm_ref[...])
+        coarse = full.astype(jnp.bfloat16)
+        m_ref[:, :LANES] = coarse
+        m_ref[:, LANES:] = (full - coarse.astype(jnp.float32)).astype(jnp.bfloat16)
 
     mx, my, mz = directions((np1, LANES), nt1, np1)
     sxs, sxc = sincos(PHASE_MID * mx)
@@ -242,8 +276,8 @@
             jax.ShapeDtypeStruct((np2, 8 * per_dev, exc, LANES), f32),
             jax.ShapeDtypeStruct((np2 * 3, exc, LANES), f32),
             jax.ShapeDtypeStruct((np1 * 3, exc, LANES), f32),
-            jax.ShapeDtypeStruct((LANES, 2 * nt2), f32),
-            jax.ShapeDtypeStruct((LANES, 4 * nt1), f32),
+            jax.ShapeDtypeStruct((2 * nt2, 2 * LANES), jnp.bfloat16),
+            jax.ShapeDtypeStruct((4 * nt1, 2 * LANES), jnp.bfloat16),
             jax.ShapeDtypeStruct((4 * np1, LANES), f32),
             jax.ShapeDtypeStruct((4 * np1, LANES), f32),
         ],
@@ -251,10 +285,19 @@
             pltpu.VMEM((2, np2, LANES), f32),
             pltpu.VMEM((8 * per_dev, np2, LANES), f32),
             pltpu.VMEM((2, images[0], LANES), f32),
+            pltpu.VMEM((LANES, 2 * nt2), f32),
         ],
-        compiler_params=pltpu.CompilerParams(vmem_limit_bytes=32 << 20),
+        compiler_params=pltpu.CompilerParams(vmem_limit_bytes=(8 << 20) + np2 * (96 << 10)),
         name="coefficients",
     )(where, inc, child, phi_top, phi_mid, img, tit, twt, tim, twm)
+
+
+def split_dot(x, m_ref):
+    high = x.astype(jnp.bfloat16)
+    low = (x - high.astype(jnp.float32)).astype(jnp.bfloat16)
+    wide = jnp.dot(high, m_ref[...], preferred_element_type=jnp.float32)
+    rest = jnp.dot(low, m_ref[:, :LANES], preferred_element_type=jnp.float32)
+    return wide[:, :LANES] + (wide[:, LANES:] + rest)
 
 
 def phi_pass(count, contribution, emit):
@@ -297,7 +340,6 @@
     mid_local = phi_local // 2
     base = phi_local * per_dev * 2
     mids = 4 * per_dev
-    nt = (((1,), (1,)), ((), ()))
 
     for box in range(per_dev):
 
@@ -331,13 +373,7 @@
         block = min(rows, 512)
 
         def theta(part, box=box):
-            done = lax.dot_general(
-                x_ref[pl.ds(part * block, block), :],
-                m2_ref[...],
-                nt,
-                precision=HIGHEST,
-                preferred_element_type=jnp.float32,
-            )
+            done = split_dot(x_ref[pl.ds(part * block, block), :], m2_ref)
             per_block = block // (4 * exc)
             for n in range(per_block):
                 q = part * per_block + n
@@ -384,13 +420,7 @@
             phi_pass(np0, middle, keep_low)
 
     def finish(pair):
-        done = lax.dot_general(
-            y_ref[pair],
-            m1_ref[...],
-            nt,
-            precision=HIGHEST,
-            preferred_element_type=jnp.float32,
-        )
+        done = split_dot(y_ref[pair], m1_ref)
         start = pair * LANES
         lanes = pl.ds(start if isinstance(pair, int) else pl.multiple_of(start, LANES), LANES)
         for k in range(4 * mids):
@@ -417,7 +447,7 @@
             pltpu.VMEM((np0 // 2, 4 * mids * exc, 2 * LANES), f32),
             pltpu.VMEM((4 * mids * exc, LANES), f32),
         ],
-        compiler_params=pltpu.CompilerParams(vmem_limit_bytes=56 << 20),
+        compiler_params=pltpu.CompilerParams(vmem_limit_bytes=(8 << 20) + np2 * (144 << 10)),
         name="levels",
     )(received, *coefs)
 

time: 29.9 us -> 25.8 us (0.86)
  local copies, waits for them, and re-layouts: 9.74 us -> 2.15 us
  waiting for transfers between devices: 2.83 us -> 7.77 us
  Pallas kernels: 7.61 us -> 6.34 us
    unnamed x41 -> x21, local copies, waits for them, and re-layouts: 9.66 us -> 2.07 us
    all_to_all x1, waiting for transfers between devices: 1.59 us -> 6.52 us  [local(): lax.all_to_all(packed, 'dev', split_axis=0, concat_axis=0, tiled=True)]
    pallas_call x1, Pallas kernels: 3.99 us -> 1.76 us  [main(): pl.pallas_call(lambda *refs: main_kernel(sizes, *refs), in_specs=[VMEM] *...]
    pallas_call x1, Pallas kernels: 1.02 us -> 2 us  [pack(): pl.pallas_call(lambda *refs: pack_kernel(per_dest, *refs), in_specs=[hbm]...]
  transfers between devices with their start and end apart: 2 -> 2, of which waited for: 2 -> 2; matrix products, arithmetic and copies ran while one was open for 1% -> 1% of each run, Pallas kernels for 9% -> 10%
where the time goes in v2:
time: 25.8 us; the launch traced here: 25.5 us
  starting transfers between devices  8.98 us (35%)
  waiting for transfers between devices  7.77 us (30%)
  Pallas kernels  6.34 us (25%)
  local copies, waits for them, and re-layouts  2.15 us (8%)
    all_to_all x1, starting transfers between devices, local(): lax.all_to_all(packed, 'dev', split_axis=0, concat_axis=0, tiled=True)  7.43 us
    all_to_all x1, waiting for transfers between devices, local(): lax.all_to_all(packed, 'dev', split_axis=0, concat_axis=0, tiled=True)  6.52 us
    pallas_call x1, Pallas kernels, coefficients(): pl.pallas_call(lambda *refs: coef_kernel(sizes, *refs), in_specs=[SMEM] *...  2.58 us
    unnamed x21, local copies, waits for them, and re-layouts  2.07 us
    pallas_call x1, Pallas kernels, pack(): pl.pallas_call(lambda *refs: pack_kernel(per_dest, *refs), in_specs=[hbm]...  2 us
    pallas_call x1, Pallas kernels, main(): pl.pallas_call(lambda *refs: main_kernel(sizes, *refs), in_specs=[VMEM] *...  1.76 us
    ppermute x1, starting transfers between devices, local(): lax.ppermute(own, 'rhs', [(i, (i + shift) % rhs_count) for i in range(rhs...  1.55 us
    ppermute x1, waiting for transfers between devices, local(): lax.ppermute(own, 'rhs', [(i, (i + shift) % rhs_count) for i in range(rhs...  1.25 us
  transfers between devices with their start and end apart: 2, of which 2 were waited for; matrix products, arithmetic and copies ran while one was open for 1% of the time, Pallas kernels for 10%

profile of v2, /device:TPU:0, one launch (start us, length us, event | category | flops | bytes accessed | tf_op | source)
XLA Modules:
  0.0 25.5 jit_solution(15740774871609339894)
XLA Ops:
  0.0 2.0 %pack.1 = f32[16,8,8,128]{3,2,1,0:T(8,128)} custom-call(f32[8,2,16,256]{3,2,1,0:T(8,128)} %refs_0_.1, f32[8,1,64,128]{3,2,1,0:T(8,128)} %refs_1_.1), custom_call_target="tpu_custom_call" | custom-call | tf_op jit(solution)/shard_map/pack/pallas_call | solution.py:114
  2.0 0.0 copy-start.9
  2.0 7.4 %all-to-all-start = ((f32[16,8,8,128]{3,2,1,0:T(8,128)}), f32[16,8,8,128]{3,2,1,0:T(8,128)S(1)}, u32[]{:S(2)}, u32[]{:S(2)}) async-start(f32[16,8,8,128]{3,2,1,0:T(8,128)} %pack.1), calls=%async_computation | async-start | bytes 1048576 | tf_op jit(solution)/shard_map/all_to_all | solution.py:479
  9.5 0.0 copy-done.9
  9.5 0.0 copy-start.8
  9.5 0.7 %copy-done.8 = s32[32,2]{0,1:T(2,128)S(1)} copy-done((s32[32,2]{0,1:T(2,128)S(1)}, s32[32,2]{0,1:T(2,128)}, u32[]{:S(2)}) %copy-start.8) | copy-done | bytes 280
  10.2 1.6 %collective-permute-start = (f32[3,32]{1,0:T(4,128)S(1)}, f32[3,32]{1,0:T(4,128)S(1)}, u32[]{:S(2)}, u32[]{:S(2)}) collective-permute-start(f32[3,32]{1,0:T(4,128)S(1)} %pad_maximum_fusion), channel_id=1, source_target_pairs={{0,1},{1,0},{2,3},{3,2},{4,5},{5,4},{6,7},{7,6},{8,9},{9,8},{10,11... | collective-permute-start | bytes 1160 | tf_op jit(solution)/shard_map/ppermute | solution.py:491
  11.7 0.0 copy-start.7
  11.7 0.1 pad_add_fusion.refs_0_
  11.8 0.6 %copy-done.7 = s32[16,4]{0,1:T(4,128)S(1)} copy-done((s32[16,4]{0,1:T(4,128)S(1)}, s32[16,4]{0,1:T(4,128)}, u32[]{:S(2)}) %copy-start.7) | copy-done | bytes 280
  12.4 0.1 copy.13.refs_2_
  12.5 0.1 pad.3.clone
  12.6 1.2 %collective-permute-done = f32[3,32]{1,0:T(4,128)S(1)} collective-permute-done((f32[3,32]{1,0:T(4,128)S(1)}, f32[3,32]{1,0:T(4,128)S(1)}, u32[]{:S(2)}, u32[]{:S(2)}) %collective-permute-start) | collective-permute-done | bytes 416 | tf_op jit(solution)/shard_map/ppermute | solution.py:491
  13.8 0.1 maximum_maximum_fusion.refs_5_
  13.9 0.6 %copy-done.2 = s32[128,3]{0,1:T(4,128)S(1)} copy-done((s32[128,3]{0,1:T(4,128)S(1)}, s32[128,3]{0,1:T(4,128)}, u32[]{:S(2)}) %copy-start.2) | copy-done | bytes 1560
  14.5 0.0 copy-done.3
  14.5 0.0 copy-done.4
  14.5 0.0 copy-done.5
  14.5 0.0 copy-done.1
  14.6 0.0 copy-done
  14.6 0.0 copy-done.6
  14.6 2.6 %coefficients.1 = (f32[32,8,8,128]{3,2,1,0:T(8,128)S(1)}, f32[96,8,128]{2,1,0:T(8,128)S(1)}, f32[48,8,128]{2,1,0:T(8,128)S(1)}, bf16[256,256]{1,0:T(8,128)(2,1)S...) custom-call(s32[2]{0:T(128)S(1)} %pad_add_fusion.refs_0_, f32[2,16]{1,0:T(2,128)S(1)} %bitcast.19, ...), custom_call_target="tpu_custom_call" | custom-call | tf_op jit(solution)/shard_map/coefficients/pallas_call | solution.py:271
  17.2 6.5 %all-to-all-done.refs_0_ = f32[16,8,8,128]{3,2,1,0:T(8,128)S(1)} async-done(((f32[16,8,8,128]{3,2,1,0:T(8,128)}), f32[16,8,8,128]{3,2,1,0:T(8,128)S(1)}, u32[]{:S(2)}, u32[]{:S(2)}) %all-to-all-start) | async-done | bytes 524320 | tf_op jit(solution)/shard_map/all_to_all | solution.py:479
  23.7 1.8 %levels.1 = f32[8,16,512]{2,1,0:T(8,128)} custom-call(f32[16,8,8,128]{3,2,1,0:T(8,128)S(1)} %all-to-all-done.refs_0_, f32[32,8,8,128]{3,2,1,0:T(8,128)S(1)} %get-tuple-element.12.refs_1_, f32[96,8,128]{2,1,0:T(8,128)S(1)} %get-tuple-element.13.refs_2_, f32[48,8,128]{2,1,0:T(8,128)S(1)} %get-tuple-element.14.refs_3_, ...), custom_call_target="tpu_custom_call" | custom-call | tf_op jit(solution)/shard_map/levels/pallas_call | solution.py:438
  (11 shorter events, 0.0 us)
Async XLA Ops:
  2.0 7.4 %copy-start.9 = (f32[32]{0:T(128)S(1)}, f32[32]{0:T(128)}, u32[]{:S(2)}) copy-start(f32[32]{0:T(128)} %param.15) | copy-start | bytes 388
  2.0 21.7 %all-to-all-start = ((f32[16,8,8,128]{3,2,1,0:T(8,128)}), f32[16,8,8,128]{3,2,1,0:T(8,128)S(1)}, u32[]{:S(2)}, u32[]{:S(2)}) async-start(f32[16,8,8,128]{3,2,1,0:T(8,128)} %pack.1), calls=%async_computation | async-start | bytes 1048576 | tf_op jit(solution)/shard_map/all_to_all | solution.py:479
  9.5 0.7 %copy-start.8 = (s32[32,2]{0,1:T(2,128)S(1)}, s32[32,2]{0,1:T(2,128)}, u32[]{:S(2)}) copy-start(s32[32,2]{0,1:T(2,128)} %param.14) | copy-start | bytes 772
  10.2 3.6 %collective-permute-start = (f32[3,32]{1,0:T(4,128)S(1)}, f32[3,32]{1,0:T(4,128)S(1)}, u32[]{:S(2)}, u32[]{:S(2)}) collective-permute-start(f32[3,32]{1,0:T(4,128)S(1)} %pad_maximum_fusion), channel_id=1, source_target_pairs={{0,1},{1,0},{2,3},{3,2},{4,5},{5,4},{6,7},{7,6},{8,9},{9,8},{10,11... | collective-permute-start | bytes 1160 | tf_op jit(solution)/shard_map/ppermute | solution.py:491
  11.7 0.7 %copy-start.7 = (s32[16,4]{0,1:T(4,128)S(1)}, s32[16,4]{0,1:T(4,128)}, u32[]{:S(2)}) copy-start(s32[16,4]{0,1:T(4,128)} %param.17) | copy-start | bytes 772
  13.8 0.7 %copy-start.2 = (s32[128,3]{0,1:T(4,128)S(1)}, s32[128,3]{0,1:T(4,128)}, u32[]{:S(2)}) copy-start(s32[128,3]{0,1:T(4,128)} %param.18) | copy-start | bytes 4612
  13.8 0.7 %copy-start.3 = (f32[128,3]{0,1:T(4,128)S(1)}, f32[128,3]{0,1:T(4,128)}, u32[]{:S(2)}) copy-start(f32[128,3]{0,1:T(4,128)} %param.19) | copy-start | bytes 4612
  13.8 0.7 %copy-start.4 = (s32[64,3]{0,1:T(4,128)S(1)}, s32[64,3]{0,1:T(4,128)}, u32[]{:S(2)}) copy-start(s32[64,3]{0,1:T(4,128)} %param.21) | copy-start | bytes 2308
  13.8 0.7 %copy-start.5 = (f32[64,3]{0,1:T(4,128)S(1)}, f32[64,3]{0,1:T(4,128)}, u32[]{:S(2)}) copy-start(f32[64,3]{0,1:T(4,128)} %param.22) | copy-start | bytes 2308
  13.9 0.7 %copy-start.1 = (f32[16,3]{0,1:T(4,128)S(1)}, f32[16,3]{0,1:T(4,128)}, u32[]{:S(2)}) copy-start(f32[16,3]{0,1:T(4,128)} %param.23) | copy-start | bytes 580
  13.9 0.7 %copy-start = (f32[32,3]{0,1:T(4,128)S(1)}, f32[32,3]{0,1:T(4,128)}, u32[]{:S(2)}) copy-start(f32[32,3]{0,1:T(4,128)} %param.20) | copy-start | bytes 1156
  13.9 0.7 %copy-start.6 = (f32[16,2]{0,1:T(2,128)S(1)}, f32[16,2]{0,1:T(2,128)}, u32[]{:S(2)}) copy-start(f32[16,2]{0,1:T(2,128)} %param.16) | copy-start | bytes 388

commit v3 on v2

--- a/solution.py
+++ b/solution.py
@@ -59,46 +59,51 @@
 def pack_kernel(per_dest, a_hbm, l_hbm, o_hbm, re_ref, im_ref, mid_ref, top_out, mid_out, sems):
     exc, phi_local, boxes, _ = re_ref.shape
     mid_phi, mids = mid_ref.shape[1:3]
-    copies = [
+    arrive = [
         pltpu.make_async_copy(a_hbm.at[:, :, :, pl.ds(0, LANES)], re_ref, sems.at[0]),
         pltpu.make_async_copy(a_hbm.at[:, :, :, pl.ds(LANES, LANES)], im_ref, sems.at[1]),
         pltpu.make_async_copy(l_hbm, mid_ref, sems.at[2]),
     ]
-    for copy in copies:
+    for copy in arrive:
         copy.start()
-    top_tiles = top_out.shape[1]
-    mid_tiles = mid_out.shape[1]
+    group = 8
+    leave = []
+
+    def scatter(source, target, dests):
+        count, width, _ = source.shape
+        rows = target.reshape(width * count, LANES)
+
+        def one(g):
+            for e in range(count):
+                start = g * group * count + e
+                rows[pl.ds(start, group, stride=count), :] = source[e, pl.ds(g * group, group), :]
+
+        loop(width // group, one)
+        split = target.reshape(width // len(dests), len(dests), count, LANES)
+        for n, tile in enumerate(dests):
+            copy = pltpu.make_async_copy(
+                split.at[:, n], o_hbm.at[:, tile], sems.at[3 + len(leave)]
+            )
+            copy.start()
+            leave.append(copy)
 
     for part, ref in enumerate((re_ref, im_ref)):
-        rows = ref.reshape(exc * phi_local * boxes, LANES)
-        copies[part].wait()
-
-        def top(dest, rows=rows, part=part):
-            for phi in range(phi_local):
-                for box in range(per_dest):
-                    row = phi * boxes + dest * per_dest + box
-                    tile = (phi * per_dest + box) * 2 + part
-                    top_out[dest, tile] = rows[pl.ds(row, exc, stride=phi_local * boxes), :]
-
-        loop(boxes // per_dest, top)
-
-    leave = [
-        pltpu.make_async_copy(top_out, o_hbm.at[:, pl.ds(0, top_tiles)], sems.at[3]),
-        pltpu.make_async_copy(mid_out, o_hbm.at[:, pl.ds(top_tiles, mid_tiles)], sems.at[4]),
-    ]
-    leave[0].start()
-    mid_rows = mid_ref.reshape(exc * mid_phi * mids, LANES)
-    copies[2].wait()
-
-    def middle(dest):
-        for phi in range(mid_phi):
-            for mid in range(4 * per_dest):
-                row = phi * mids + dest * 4 * per_dest + mid
-                tile = phi * 4 * per_dest + mid
-                mid_out[dest, tile] = mid_rows[pl.ds(row, exc, stride=mid_phi * mids), :]
-
-    loop(boxes // per_dest, middle)
-    leave[1].start()
+        arrive[part].wait()
+        for phi in range(phi_local):
+            k = phi * 2 + part
+            scatter(
+                ref.at[:, phi],
+                top_out.at[k],
+                [box * phi_local * 2 + k for box in range(per_dest)],
+            )
+    arrive[2].wait()
+    first = per_dest * phi_local * 2
+    for phi in range(mid_phi):
+        scatter(
+            mid_ref.at[:, phi],
+            mid_out.at[phi],
+            [first + mid * mid_phi + phi for mid in range(4 * per_dest)],
+        )
     for copy in leave:
         copy.wait()
 
@@ -107,22 +112,21 @@
     exc, phi_local, boxes, _ = top_adj.shape
     mid_phi, mids = level1_adj.shape[1:3]
     per_dest = boxes // dev_count
-    top_tiles = phi_local * per_dest * 2
-    mid_tiles = mid_phi * 4 * per_dest
+    tiles = (phi_local * 2 + mid_phi * 4) * per_dest
     f32 = jnp.float32
     hbm = pl.BlockSpec(memory_space=pltpu.HBM)
     return pl.pallas_call(
         lambda *refs: pack_kernel(per_dest, *refs),
         in_specs=[hbm] * 2,
         out_specs=hbm,
-        out_shape=jax.ShapeDtypeStruct((dev_count, top_tiles + mid_tiles, exc, LANES), f32),
+        out_shape=jax.ShapeDtypeStruct((dev_count, tiles, exc, LANES), f32),
         scratch_shapes=[
             pltpu.VMEM((exc, phi_local, boxes, LANES), f32),
             pltpu.VMEM((exc, phi_local, boxes, LANES), f32),
             pltpu.VMEM((exc, mid_phi, mids, LANES), f32),
-            pltpu.VMEM((dev_count, top_tiles, exc, LANES), f32),
-            pltpu.VMEM((dev_count, mid_tiles, exc, LANES), f32),
-            pltpu.SemaphoreType.DMA((5,)),
+            pltpu.VMEM((phi_local * 2, boxes, exc, LANES), f32),
+            pltpu.VMEM((mid_phi, mids, exc, LANES), f32),
+            pltpu.SemaphoreType.DMA((3 + tiles,)),
         ],
         compiler_params=pltpu.CompilerParams(vmem_limit_bytes=67043328),
         name="pack",
@@ -300,22 +304,35 @@
     return wide[:, :LANES] + (wide[:, LANES:] + rest)
 
 
-def phi_pass(count, contribution, emit):
+def phi_pass(count, contribution, emit, origin=0):
+    if count <= 16:
+        first = contribution(origin % count)
+        here, after = first[1], first[2]
+        held = None
+        for m in range(1, count):
+            new = contribution((m + origin) % count)
+            ready = [x + y for x, y in zip(here, new[0])]
+            if m == 1:
+                held = ready
+            else:
+                emit((m - 1 + origin) % count, ready)
+            here, after = [x + y for x, y in zip(after, new[1])], new[2]
+        emit((count - 1 + origin) % count, [x + y for x, y in zip(here, first[0])])
+        emit(origin % count, [x + y for x, y in zip(held, after)])
+        return
+
     first = contribution(count - 1)
     second = contribution(0)
-    carry = [x + y for x, y in zip(first[2], second[1])], list(second[2])
 
     def step(q, carry):
         here, after = carry
-        new = contribution((q + 1) % count if isinstance(q, int) else lax.rem(q + 1, count))
+        new = contribution(lax.rem(q + 1, count))
         emit(q, [x + y for x, y in zip(here, new[0])])
         return [x + y for x, y in zip(after, new[1])], list(new[2])
 
-    if count <= 16:
-        for q in range(count):
-            carry = step(q, carry)
-    else:
-        lax.fori_loop(0, count, step, carry)
+    lax.fori_loop(
+        0, count, step, ([x + y for x, y in zip(first[2], second[1])], list(second[2]))
+    )
 
 
 def main_kernel(
@@ -334,6 +351,7 @@
     h_ref,
     y_ref,
     z_ref,
+    sems,
 ):
     exc, np2, np1, nt2, phi_local, per_dev = sizes
     np0 = np1 // 2
@@ -347,7 +365,7 @@
             out = [[None] * 8 for _ in range(3)]
             for parity in range(2):
                 p = 2 * m + parity
-                tile = ((p % phi_local) * per_dev + box) * 2
+                tile = (box * phi_local + p % phi_local) * 2
                 ar = r_ref[p // phi_local, tile]
                 ai = r_ref[p // phi_local, tile + 1]
                 weights = [pw2_ref[3 * p + s] for s in range(3)]
@@ -361,35 +379,41 @@
                             out[s][k] = term if out[s][k] is None else out[s][k] + term
             return out
 
-        def keep(q, values):
-            for slot in range(4):
-                for c in range(2):
-                    x_ref[
-                        pl.ds((q * 4 + slot) * exc, exc), c * LANES : (c + 1) * LANES
-                    ] = values[slot * 2 + c]
-
-        phi_pass(np1, top, keep)
-        rows = x_ref.shape[0]
-        block = min(rows, 512)
+        chunk = min(np1, 4)
 
         def theta(part, box=box):
-            done = split_dot(x_ref[pl.ds(part * block, block), :], m2_ref)
-            per_block = block // (4 * exc)
-            for n in range(per_block):
-                q = part * per_block + n
+            done = split_dot(x_ref[pl.ds(part * chunk * 4 * exc, chunk * 4 * exc), :], m2_ref)
+            for n in range(chunk):
+                q = (part * chunk + n + 1) % np1
                 for slot in range(4):
                     row = (n * 4 + slot) * exc
                     mid = box * 4 + slot
                     value = (
                         done[row : row + exc]
-                        + r_ref[q // mid_local, base + (q % mid_local) * mids + mid]
+                        + r_ref[q // mid_local, base + mid * mid_local + q % mid_local]
                     )
                     g_ref[q, mid] = value
                     h_ref[q, mid] = pltpu.roll(value, LANES // 2, 1)
 
-        loop(rows // block, theta)
+        static = np1 <= 16
+
+        def keep(q, values):
+            place = (q + np1 - 1) % np1
+            for slot in range(4):
+                for c in range(2):
+                    x_ref[
+                        pl.ds((place * 4 + slot) * exc, exc), c * LANES : (c + 1) * LANES
+                    ] = values[slot * 2 + c]
+            if static and place % chunk == chunk - 1:
+                theta(place // chunk)
+
+        phi_pass(np1, top, keep)
+        if not static:
+            loop(np1 // chunk, theta)
 
     o_rows = o_ref.reshape(exc * 4 * mids, o_ref.shape[2])
+
+    pairs = np0 // 2
 
     for octant in range(4):
         for box in range(per_dev):
@@ -410,24 +434,37 @@
                             out[s][slot] = term if out[s][slot] is None else out[s][slot] + term
                 return out
 
-            def keep_low(q, values, octant=octant, box=box):
+            buffer = y_ref.at[octant % 2]
+
+            def keep_low(q, values, buffer=buffer):
                 for slot in range(4):
-                    k = (box * 4 + slot) * 4 + octant
-                    y_ref[q // 2, pl.ds(k * exc, exc), pl.ds((q % 2) * LANES, LANES)] = values[
-                        slot
-                    ]
-
-            phi_pass(np0, middle, keep_low)
-
-    def finish(pair):
-        done = split_dot(y_ref[pair], m1_ref)
+                    buffer[q // 2, pl.ds(slot * exc, exc), pl.ds((q % 2) * LANES, LANES)] = (
+                        values[slot]
+                    )
+
+            phi_pass(np0, middle, keep_low, 1)
+
+            def finish(part, octant=octant, box=box, buffer=buffer):
+                step = min(pairs, 4)
+                tile = buffer[pl.ds(part * step, step)].reshape(step * 4 * exc, 2 * LANES)
+                done = split_dot(tile, m1_ref)
+                for n in range(step):
+                    for slot in range(4):
+                        k = (box * 4 + slot) * 4 + octant
+                        row = (n * 4 + slot) * exc
+                        z_ref[part * step + n, pl.ds(k, exc, stride=4 * mids), :] = done[
+                            row : row + exc
+                        ]
+
+            loop(pairs // min(pairs, 4), finish)
+
+    def leave(pair):
         start = pair * LANES
         lanes = pl.ds(start if isinstance(pair, int) else pl.multiple_of(start, LANES), LANES)
-        for k in range(4 * mids):
-            z_ref[pl.ds(k, exc, stride=4 * mids), :] = done[k * exc : (k + 1) * exc]
-        o_rows[:, lanes] = z_ref[...]
-
-    loop(np0 // 2, finish)
+        return pltpu.make_async_copy(z_ref.at[pair], o_rows.at[:, lanes], sems.at[pair])
+
+    loop(pairs, lambda pair: leave(pair).start())
+    loop(pairs, lambda pair: leave(pair).wait())
 
 
 def main(received, coefs, exc, np2, np1, nt2, phi_local, per_dev):
@@ -438,14 +475,15 @@
     return pl.pallas_call(
         lambda *refs: main_kernel(sizes, *refs),
         in_specs=[VMEM] * 8,
-        out_specs=VMEM,
+        out_specs=pl.BlockSpec(memory_space=pltpu.HBM),
         out_shape=jax.ShapeDtypeStruct((exc, 4 * mids, np0 * (nt2 // 2)), f32),
         scratch_shapes=[
             pltpu.VMEM((np1 * 4 * exc, 2 * LANES), f32),
             pltpu.VMEM((np1, mids, exc, LANES), f32),
             pltpu.VMEM((np1, mids, exc, LANES), f32),
-            pltpu.VMEM((np0 // 2, 4 * mids * exc, 2 * LANES), f32),
-            pltpu.VMEM((4 * mids * exc, LANES), f32),
+            pltpu.VMEM((2, np0 // 2, 4 * exc, 2 * LANES), f32),
+            pltpu.VMEM((np0 // 2, 4 * mids * exc, LANES), f32),
+            pltpu.SemaphoreType.DMA((np0 // 2,)),
         ],
         compiler_params=pltpu.CompilerParams(vmem_limit_bytes=(8 << 20) + np2 * (144 << 10)),
         name="levels",

time: 25.8 us -> 25.6 us (level)
  no operation moved by 1% of the time
where the time goes in v3:
time: 25.6 us; the launch traced here: 25.3 us
  starting transfers between devices  8.98 us (35%)
  waiting for transfers between devices  7.77 us (30%)
  Pallas kernels  6.21 us (24%)
  local copies, waits for them, and re-layouts  2.15 us (8%)
    all_to_all x1, starting transfers between devices, local(): lax.all_to_all(packed, 'dev', split_axis=0, concat_axis=0, tiled=True)  7.43 us
    all_to_all x1, waiting for transfers between devices, local(): lax.all_to_all(packed, 'dev', split_axis=0, concat_axis=0, tiled=True)  6.52 us
    pallas_call x1, Pallas kernels, coefficients(): pl.pallas_call(lambda *refs: coef_kernel(sizes, *refs), in_specs=[SMEM] *...  2.59 us
    unnamed x21, local copies, waits for them, and re-layouts  2.07 us
    pallas_call x1, Pallas kernels, pack(): pl.pallas_call(lambda *refs: pack_kernel(per_dest, *refs), in_specs=[hbm]...  1.95 us
    pallas_call x1, Pallas kernels, main(): pl.pallas_call(lambda *refs: main_kernel(sizes, *refs), in_specs=[VMEM] *...  1.67 us
    ppermute x1, starting transfers between devices, local(): lax.ppermute(own, 'rhs', [(i, (i + shift) % rhs_count) for i in range(rhs...  1.55 us
    ppermute x1, waiting for transfers between devices, local(): lax.ppermute(own, 'rhs', [(i, (i + shift) % rhs_count) for i in range(rhs...  1.25 us
  transfers between devices with their start and end apart: 2, of which 2 were waited for; matrix products, arithmetic and copies ran while one was open for 1% of the time, Pallas kernels for 10%

profile of v3, /device:TPU:0, one launch (start us, length us, event | category | flops | bytes accessed | tf_op | source)
XLA Modules:
  0.0 25.3 jit_solution(1421555532973181893)
XLA Ops:
  0.0 1.9 %pack.1 = f32[16,8,8,128]{3,2,1,0:T(8,128)} custom-call(f32[8,2,16,256]{3,2,1,0:T(8,128)} %refs_0_.1, f32[8,1,64,128]{3,2,1,0:T(8,128)} %refs_1_.1), custom_call_target="tpu_custom_call" | custom-call | tf_op jit(solution)/shard_map/pack/pallas_call | solution.py:118
  2.0 0.0 copy-start.9
  2.0 7.4 %all-to-all-start = ((f32[16,8,8,128]{3,2,1,0:T(8,128)}), f32[16,8,8,128]{3,2,1,0:T(8,128)S(1)}, u32[]{:S(2)}, u32[]{:S(2)}) async-start(f32[16,8,8,128]{3,2,1,0:T(8,128)} %pack.1), calls=%async_computation | async-start | bytes 1048576 | tf_op jit(solution)/shard_map/all_to_all | solution.py:517
  9.4 0.0 copy-done.9
  9.4 0.0 copy-start.8
  9.4 0.7 %copy-done.8 = s32[32,2]{0,1:T(2,128)S(1)} copy-done((s32[32,2]{0,1:T(2,128)S(1)}, s32[32,2]{0,1:T(2,128)}, u32[]{:S(2)}) %copy-start.8) | copy-done | bytes 280
  10.1 1.6 %collective-permute-start = (f32[3,32]{1,0:T(4,128)S(1)}, f32[3,32]{1,0:T(4,128)S(1)}, u32[]{:S(2)}, u32[]{:S(2)}) collective-permute-start(f32[3,32]{1,0:T(4,128)S(1)} %pad_maximum_fusion), channel_id=1, source_target_pairs={{0,1},{1,0},{2,3},{3,2},{4,5},{5,4},{6,7},{7,6},{8,9},{9,8},{10,11... | collective-permute-start | bytes 1160 | tf_op jit(solution)/shard_map/ppermute | solution.py:529
  11.7 0.0 copy-start.7
  11.7 0.1 pad_add_fusion.refs_0_
  11.7 0.6 %copy-done.7 = s32[16,4]{0,1:T(4,128)S(1)} copy-done((s32[16,4]{0,1:T(4,128)S(1)}, s32[16,4]{0,1:T(4,128)}, u32[]{:S(2)}) %copy-start.7) | copy-done | bytes 280
  12.3 0.1 copy.13.refs_2_
  12.4 0.1 pad.3.clone
  12.5 1.2 %collective-permute-done = f32[3,32]{1,0:T(4,128)S(1)} collective-permute-done((f32[3,32]{1,0:T(4,128)S(1)}, f32[3,32]{1,0:T(4,128)S(1)}, u32[]{:S(2)}, u32[]{:S(2)}) %collective-permute-start) | collective-permute-done | bytes 416 | tf_op jit(solution)/shard_map/ppermute | solution.py:529
  13.8 0.1 maximum_maximum_fusion.refs_5_
  13.9 0.6 %copy-done.2 = s32[128,3]{0,1:T(4,128)S(1)} copy-done((s32[128,3]{0,1:T(4,128)S(1)}, s32[128,3]{0,1:T(4,128)}, u32[]{:S(2)}) %copy-start.2) | copy-done | bytes 1560
  14.4 0.0 copy-done.3
  14.5 0.0 copy-done.4
  14.5 0.0 copy-done.5
  14.5 0.0 copy-done.1
  14.5 0.0 copy-done
  14.5 0.0 copy-done.6
  14.6 2.6 %coefficients.1 = (f32[32,8,8,128]{3,2,1,0:T(8,128)S(1)}, f32[96,8,128]{2,1,0:T(8,128)S(1)}, f32[48,8,128]{2,1,0:T(8,128)S(1)}, bf16[256,256]{1,0:T(8,128)(2,1)S...) custom-call(s32[2]{0:T(128)S(1)} %pad_add_fusion.refs_0_, f32[2,16]{1,0:T(2,128)S(1)} %bitcast.19, ...), custom_call_target="tpu_custom_call" | custom-call | tf_op jit(solution)/shard_map/coefficients/pallas_call | solution.py:275
  17.2 6.5 %all-to-all-done.refs_0_ = f32[16,8,8,128]{3,2,1,0:T(8,128)S(1)} async-done(((f32[16,8,8,128]{3,2,1,0:T(8,128)}), f32[16,8,8,128]{3,2,1,0:T(8,128)S(1)}, u32[]{:S(2)}, u32[]{:S(2)}) %all-to-all-start) | async-done | bytes 524320 | tf_op jit(solution)/shard_map/all_to_all | solution.py:517
  23.7 1.7 %levels.1 = f32[8,16,512]{2,1,0:T(8,128)} custom-call(f32[16,8,8,128]{3,2,1,0:T(8,128)S(1)} %all-to-all-done.refs_0_, f32[32,8,8,128]{3,2,1,0:T(8,128)S(1)} %get-tuple-element.12.refs_1_, f32[96,8,128]{2,1,0:T(8,128)S(1)} %get-tuple-element.13.refs_2_, f32[48,8,128]{2,1,0:T(8,128)S(1)} %get-tuple-element.14.refs_3_, ...), custom_call_target="tpu_custom_call" | custom-call | tf_op jit(solution)/shard_map/levels/pallas_call | solution.py:475
  (11 shorter events, 0.0 us)
Async XLA Ops:
  2.0 7.4 %copy-start.9 = (f32[32]{0:T(128)S(1)}, f32[32]{0:T(128)}, u32[]{:S(2)}) copy-start(f32[32]{0:T(128)} %param.15) | copy-start | bytes 388
  2.0 21.7 %all-to-all-start = ((f32[16,8,8,128]{3,2,1,0:T(8,128)}), f32[16,8,8,128]{3,2,1,0:T(8,128)S(1)}, u32[]{:S(2)}, u32[]{:S(2)}) async-start(f32[16,8,8,128]{3,2,1,0:T(8,128)} %pack.1), calls=%async_computation | async-start | bytes 1048576 | tf_op jit(solution)/shard_map/all_to_all | solution.py:517
  9.4 0.7 %copy-start.8 = (s32[32,2]{0,1:T(2,128)S(1)}, s32[32,2]{0,1:T(2,128)}, u32[]{:S(2)}) copy-start(s32[32,2]{0,1:T(2,128)} %param.14) | copy-start | bytes 772
  10.1 3.6 %collective-permute-start = (f32[3,32]{1,0:T(4,128)S(1)}, f32[3,32]{1,0:T(4,128)S(1)}, u32[]{:S(2)}, u32[]{:S(2)}) collective-permute-start(f32[3,32]{1,0:T(4,128)S(1)} %pad_maximum_fusion), channel_id=1, source_target_pairs={{0,1},{1,0},{2,3},{3,2},{4,5},{5,4},{6,7},{7,6},{8,9},{9,8},{10,11... | collective-permute-start | bytes 1160 | tf_op jit(solution)/shard_map/ppermute | solution.py:529
  11.7 0.7 %copy-start.7 = (s32[16,4]{0,1:T(4,128)S(1)}, s32[16,4]{0,1:T(4,128)}, u32[]{:S(2)}) copy-start(s32[16,4]{0,1:T(4,128)} %param.17) | copy-start | bytes 772
  13.8 0.7 %copy-start.2 = (s32[128,3]{0,1:T(4,128)S(1)}, s32[128,3]{0,1:T(4,128)}, u32[]{:S(2)}) copy-start(s32[128,3]{0,1:T(4,128)} %param.18) | copy-start | bytes 4612
  13.8 0.7 %copy-start.3 = (f32[128,3]{0,1:T(4,128)S(1)}, f32[128,3]{0,1:T(4,128)}, u32[]{:S(2)}) copy-start(f32[128,3]{0,1:T(4,128)} %param.19) | copy-start | bytes 4612
  13.8 0.7 %copy-start.4 = (s32[64,3]{0,1:T(4,128)S(1)}, s32[64,3]{0,1:T(4,128)}, u32[]{:S(2)}) copy-start(s32[64,3]{0,1:T(4,128)} %param.21) | copy-start | bytes 2308
  13.8 0.7 %copy-start.5 = (f32[64,3]{0,1:T(4,128)S(1)}, f32[64,3]{0,1:T(4,128)}, u32[]{:S(2)}) copy-start(f32[64,3]{0,1:T(4,128)} %param.22) | copy-start | bytes 2308
  13.8 0.7 %copy-start.1 = (f32[16,3]{0,1:T(4,128)S(1)}, f32[16,3]{0,1:T(4,128)}, u32[]{:S(2)}) copy-start(f32[16,3]{0,1:T(4,128)} %param.23) | copy-start | bytes 580
  13.9 0.7 %copy-start = (f32[32,3]{0,1:T(4,128)S(1)}, f32[32,3]{0,1:T(4,128)}, u32[]{:S(2)}) copy-start(f32[32,3]{0,1:T(4,128)} %param.20) | copy-start | bytes 1156
  13.9 0.7 %copy-start.6 = (f32[16,2]{0,1:T(2,128)S(1)}, f32[16,2]{0,1:T(2,128)}, u32[]{:S(2)}) copy-start(f32[16,2]{0,1:T(2,128)} %param.16) | copy-start | bytes 388

commit v4 on v3

--- a/solution.py
+++ b/solution.py
@@ -7,40 +7,40 @@
 from jax.experimental.pallas import tpu as pltpu
 from jax.sharding import PartitionSpec as P
 
+
 PHASE_TOP = 18.85
 PHASE_MID = 9.42
 LATTICE = 12.57
 LANES = 128
-HIGHEST = lax.Precision.HIGHEST
 VMEM = pl.BlockSpec(memory_space=pltpu.VMEM)
 SMEM = pl.BlockSpec(memory_space=pltpu.SMEM)
 
 
+SINE = (3.141592502593994, -5.1677069664001465, 2.5500314235687256, -0.5980451703071594, 0.0772201269865036)
+COSINE = (1.0, -4.934802055358887, 4.058709144592285, -1.3352121114730835, 0.23493756353855133, -0.024396715685725212)
+
+
+def horner(z, factors):
+    total = factors[-1]
+    for factor in factors[-2::-1]:
+        total = total * z + factor
+    return total
+
+
 def sincos(x):
-    n = jnp.floor(x * (2.0 / math.pi) + 0.5)
-    r = x - n * 1.5703125
-    r = r - n * 4.837512969970703125e-4
-    r = r - n * 7.54978995489188216e-8
-    z = r * r
-    s = r + r * z * (-1.6666654611e-1 + z * (8.3321608736e-3 - z * 1.9515295891e-4))
-    c = (1.0 - 0.5 * z) + z * z * (
-        4.166664568298827e-2 + z * (-1.388731625493765e-3 + z * 2.443315711809948e-5)
-    )
-    quadrant = n.astype(jnp.int32)
-    swap = (quadrant & 1) == 1
-    sine = jnp.where(swap, c, s)
-    cosine = jnp.where(swap, s, c)
-    sine = jnp.where((quadrant & 2) == 2, -sine, sine)
-    cosine = jnp.where(((quadrant + 1) & 2) == 2, -cosine, cosine)
-    return sine, cosine
-
-
-def directions(shape, theta_count, phi_count, row0=0):
-    rows = lax.broadcasted_iota(jnp.int32, shape, 0).astype(jnp.float32) + row0
+    n = jnp.floor(x + 0.5)
+    f = x - n
+    z = f * f
+    sign = jnp.where((n.astype(jnp.int32) & 1) == 1, -1.0, 1.0)
+    return sign * f * horner(z, SINE), sign * horner(z, COSINE)
+
+
+def directions(shape, theta_count, phi_count):
+    rows = lax.broadcasted_iota(jnp.int32, shape, 0).astype(jnp.float32)
     cols = lax.broadcasted_iota(jnp.int32, shape, 1)
-    theta = math.pi / theta_count * ((cols % theta_count).astype(jnp.float32) + 0.5)
+    theta = ((cols % theta_count).astype(jnp.float32) + 0.5) / theta_count
     sin_theta, cos_theta = sincos(theta)
-    sin_phi, cos_phi = sincos(2.0 * math.pi / phi_count * rows)
+    sin_phi, cos_phi = sincos(2.0 / phi_count * rows)
     return cos_phi * sin_theta, sin_phi * sin_theta, cos_theta
 
 
@@ -56,9 +56,17 @@
         lax.fori_loop(0, count, lambda step, carry: (body(step), carry)[1], 0)
 
 
-def pack_kernel(per_dest, a_hbm, l_hbm, o_hbm, re_ref, im_ref, mid_ref, top_out, mid_out, sems):
+def factors(dev_count):
+    inner = 1 << ((dev_count.bit_length() - 1) // 2)
+    return dev_count // inner, inner
+
+
+def pack_kernel(per_dest, outer, inner, a_hbm, l_hbm, mid_hbm, *refs):
+    top_hbm = refs[:outer]
+    re_ref, im_ref, mid_ref, top_out, mid_out, sems = refs[outer:]
     exc, phi_local, boxes, _ = re_ref.shape
-    mid_phi, mids = mid_ref.shape[1:3]
+    mid_phi, _ = mid_ref.shape[1:3]
+    plane = lax.axis_index("dev") // inner
     arrive = [
         pltpu.make_async_copy(a_hbm.at[:, :, :, pl.ds(0, LANES)], re_ref, sems.at[0]),
         pltpu.make_async_copy(a_hbm.at[:, :, :, pl.ds(LANES, LANES)], im_ref, sems.at[1]),
@@ -69,7 +77,7 @@
     group = 8
     leave = []
 
-    def scatter(source, target, dests):
+    def scatter(source, target):
         count, width, _ = source.shape
         rows = target.reshape(width * count, LANES)
 
@@ -79,31 +87,30 @@
                 rows[pl.ds(start, group, stride=count), :] = source[e, pl.ds(g * group, group), :]
 
         loop(width // group, one)
-        split = target.reshape(width // len(dests), len(dests), count, LANES)
-        for n, tile in enumerate(dests):
-            copy = pltpu.make_async_copy(
-                split.at[:, n], o_hbm.at[:, tile], sems.at[3 + len(leave)]
-            )
-            copy.start()
-            leave.append(copy)
+
+    def send(source, target):
+        copy = pltpu.make_async_copy(source, target, sems.at[3 + len(leave)])
+        copy.start()
+        leave.append(copy)
 
     for part, ref in enumerate((re_ref, im_ref)):
         arrive[part].wait()
         for phi in range(phi_local):
             k = phi * 2 + part
-            scatter(
-                ref.at[:, phi],
-                top_out.at[k],
-                [box * phi_local * 2 + k for box in range(per_dest)],
-            )
+            scatter(ref.at[:, phi], top_out.at[k])
+            split = top_out.at[k].reshape(boxes // per_dest, per_dest, exc, LANES)
+            for other in range(outer):
+                for box in range(per_dest):
+                    send(
+                        split.at[pl.ds((plane ^ other) * inner, inner), box],
+                        top_hbm[other].at[:, box * phi_local * 2 + k],
+                    )
     arrive[2].wait()
-    first = per_dest * phi_local * 2
     for phi in range(mid_phi):
-        scatter(
-            mid_ref.at[:, phi],
-            mid_out.at[phi],
-            [first + mid * mid_phi + phi for mid in range(4 * per_dest)],
-        )
+        scatter(mid_ref.at[:, phi], mid_out.at[phi])
+        split = mid_out.at[phi].reshape(boxes // per_dest, 4 * per_dest, exc, LANES)
+        for mid in range(4 * per_dest):
+            send(split.at[:, mid], mid_hbm.at[:, mid * mid_phi + phi])
     for copy in leave:
         copy.wait()
 
@@ -112,21 +119,23 @@
     exc, phi_local, boxes, _ = top_adj.shape
     mid_phi, mids = level1_adj.shape[1:3]
     per_dest = boxes // dev_count
-    tiles = (phi_local * 2 + mid_phi * 4) * per_dest
+    outer, inner = factors(dev_count)
+    tops = phi_local * 2 * per_dest
     f32 = jnp.float32
     hbm = pl.BlockSpec(memory_space=pltpu.HBM)
     return pl.pallas_call(
-        lambda *refs: pack_kernel(per_dest, *refs),
+        lambda *refs: pack_kernel(per_dest, outer, inner, *refs),
         in_specs=[hbm] * 2,
-        out_specs=hbm,
-        out_shape=jax.ShapeDtypeStruct((dev_count, tiles, exc, LANES), f32),
+        out_specs=[hbm] * (1 + outer),
+        out_shape=[jax.ShapeDtypeStruct((dev_count, 4 * per_dest * mid_phi, exc, LANES), f32)]
+        + [jax.ShapeDtypeStruct((inner, tops, exc, LANES), f32)] * outer,
         scratch_shapes=[
             pltpu.VMEM((exc, phi_local, boxes, LANES), f32),
             pltpu.VMEM((exc, phi_local, boxes, LANES), f32),
             pltpu.VMEM((exc, mid_phi, mids, LANES), f32),
             pltpu.VMEM((phi_local * 2, boxes, exc, LANES), f32),
             pltpu.VMEM((mid_phi, mids, exc, LANES), f32),
-            pltpu.SemaphoreType.DMA((3 + tiles,)),
+            pltpu.SemaphoreType.DMA((3 + outer * tops + 4 * per_dest * mid_phi,)),
         ],
         compiler_params=pltpu.CompilerParams(vmem_limit_bytes=67043328),
         name="pack",
@@ -143,19 +152,16 @@
     return total
 
 
-def coef_kernel(
+def table_kernel(
     sizes,
     where_ref,
-    inc_ref,
     child_ref,
     phi_top_ref,
     phi_mid_ref,
-    img_ref,
     index_top_ref,
     weight_top_ref,
     index_mid_ref,
     weight_mid_ref,
-    w_ref,
     pw2_ref,
     pw1_ref,
     m2_ref,
@@ -164,14 +170,11 @@
     ts_ref,
     dir_ref,
     ph_ref,
-    ob_ref,
     fm_ref,
 ):
-    exc, np2, np1, nt2, images, per_dev = sizes
+    exc, np2, np1, nt2, per_dev = sizes
     nt1, nt0 = nt2 // 2, nt2 // 4
-    half = np2 // 2
     first_box = where_ref[0] * per_dev
-    first_exc = where_ref[1] * exc
 
     def splat_top(p):
         for s in range(3):
@@ -197,9 +200,9 @@
         m_ref[:, LANES:] = (full - coarse.astype(jnp.float32)).astype(jnp.bfloat16)
 
     mx, my, mz = directions((np1, LANES), nt1, np1)
-    sxs, sxc = sincos(PHASE_MID * mx)
-    sys_, syc = sincos(PHASE_MID * my)
-    szs, szc = sincos(PHASE_MID * mz)
+    sxs, sxc = sincos(PHASE_MID / math.pi * mx)
+    sys_, syc = sincos(PHASE_MID / math.pi * my)
+    szs, szc = sincos(PHASE_MID / math.pi * mz)
     lane = lax.broadcasted_iota(jnp.int32, (np1, LANES), 1)
     sign = jnp.where(lane < nt1, -1.0, 1.0)
     for octant in range(4):
@@ -213,9 +216,9 @@
     ux, uy, uz = directions((np2, LANES), nt2, np2)
     dir_ref[0] = ux
     dir_ref[1] = uy
-    axs, axc = sincos(PHASE_TOP * ux)
-    ays, ayc = sincos(PHASE_TOP * uy)
-    azs, azc = sincos(PHASE_TOP * uz)
+    axs, axc = sincos(PHASE_TOP / math.pi * ux)
+    ays, ayc = sincos(PHASE_TOP / math.pi * uy)
+    azs, azc = sincos(PHASE_TOP / math.pi * uz)
     for box in range(per_dev):
         for slot in range(4):
             fx = jnp.float32(0.0)
@@ -229,6 +232,14 @@
             ph_ref[box * 8 + slot * 2] = re
             ph_ref[box * 8 + slot * 2 + 1] = im
 
+
+def lattice_kernel(
+    sizes, where_ref, inc_ref, img_ref, dir_ref, ph_ref, w_ref, ob_ref
+):
+    exc, np2, images, per_dev = sizes
+    half = np2 // 2
+    first_exc = where_ref[1] * exc
+
     image = img_ref[...]
     ox, oy, wt = image[0:1, :], image[1:2, :], image[2:3, :]
     excs = lax.broadcasted_iota(jnp.int32, (exc, LANES), 0)
@@ -237,21 +248,32 @@
     for e in range(exc):
         kx = jnp.where(excs == e, inc_ref[0, first_exc + e], kx)
         ky = jnp.where(excs == e, inc_ref[1, first_exc + e], ky)
-    fs, fc = sincos(LATTICE * (ox * kx + oy * ky))
+    fs, fc = sincos(LATTICE / math.pi * (ox * kx + oy * ky))
     wc = (wt * fc)[:, :images]
     ws = (wt * fs)[:, :images]
-    left_c = jnp.concatenate([wc, -ws, wc, -ws], axis=0)
-    left_s = jnp.concatenate([ws, wc, -ws, -wc], axis=0)
-    ob_ref[0] = jnp.transpose(jnp.broadcast_to(LATTICE * ox, (LANES, LANES)))[:images]
-    ob_ref[1] = jnp.transpose(jnp.broadcast_to(LATTICE * oy, (LANES, LANES)))[:images]
-
-    def lattice(p):
+    left = jnp.concatenate(
+        [
+            jnp.concatenate([wc, -ws, wc, -ws], axis=0),
+            jnp.concatenate([ws, wc, -ws, -wc], axis=0),
+        ],
+        axis=1,
+    )
+    left_high = left.astype(jnp.bfloat16)
+    left_low = (left - left_high.astype(jnp.float32)).astype(jnp.bfloat16)
+    left_both = jnp.concatenate([left_high, left_low], axis=0)
+    ob_ref[0] = jnp.transpose(jnp.broadcast_to(LATTICE / math.pi * ox, (LANES, LANES)))[:images]
+    ob_ref[1] = jnp.transpose(jnp.broadcast_to(LATTICE / math.pi * oy, (LANES, LANES)))[:images]
+
+    def sample(p):
         ux_row = dir_ref[0, pl.ds(p, 1), :]
         uy_row = dir_ref[1, pl.ds(p, 1), :]
         sb, cb = sincos(ob_ref[0] * ux_row + ob_ref[1] * uy_row)
-        total = jnp.dot(
-            left_c, cb, precision=HIGHEST, preferred_element_type=jnp.float32
-        ) + jnp.dot(left_s, sb, precision=HIGHEST, preferred_element_type=jnp.float32)
+        basis = jnp.concatenate([cb, sb], axis=0)
+        high = basis.astype(jnp.bfloat16)
+        low = (basis - high.astype(jnp.float32)).astype(jnp.bfloat16)
+        both = jnp.dot(left_both, high, preferred_element_type=jnp.float32)
+        rest = jnp.dot(left_high, low, preferred_element_type=jnp.float32)
+        total = both[: 4 * exc] + (both[4 * exc :] + rest)
         for mirror in range(2):
             sr = total[(2 * mirror) * exc : (2 * mirror + 1) * exc]
             si = total[(2 * mirror + 1) * exc : (2 * mirror + 2) * exc]
@@ -263,37 +285,46 @@
                 w_ref[q, 2 * tile] = re
                 w_ref[q, 2 * tile + 1] = im
 
-    loop(half, lattice)
-
-
-def coefficients(where, inc, child, phi_top, phi_mid, img, tit, twt, tim, twm, exc, nt2, images):
+    loop(half, sample)
+
+
+def tables(where, child, phi_top, phi_mid, tit, twt, tim, twm, exc, nt2, per_dev):
     np2, np1 = phi_top.shape[1], phi_mid.shape[1]
-    nt1 = nt2 // 2
-    per_dev = images[1]
-    sizes = (exc, np2, np1, nt2, images[0], per_dev)
+    sizes = (exc, np2, np1, nt2, per_dev)
     f32 = jnp.float32
     return pl.pallas_call(
-        lambda *refs: coef_kernel(sizes, *refs),
-        in_specs=[SMEM] * 5 + [VMEM] * 5,
-        out_specs=[VMEM] * 7,
+        lambda *refs: table_kernel(sizes, *refs),
+        in_specs=[SMEM] * 4 + [VMEM] * 4,
+        out_specs=[VMEM] * 8,
         out_shape=[
-            jax.ShapeDtypeStruct((np2, 8 * per_dev, exc, LANES), f32),
             jax.ShapeDtypeStruct((np2 * 3, exc, LANES), f32),
             jax.ShapeDtypeStruct((np1 * 3, exc, LANES), f32),
             jax.ShapeDtypeStruct((2 * nt2, 2 * LANES), jnp.bfloat16),
-            jax.ShapeDtypeStruct((4 * nt1, 2 * LANES), jnp.bfloat16),
+            jax.ShapeDtypeStruct((2 * nt2, 2 * LANES), jnp.bfloat16),
             jax.ShapeDtypeStruct((4 * np1, LANES), f32),
             jax.ShapeDtypeStruct((4 * np1, LANES), f32),
+            jax.ShapeDtypeStruct((2, np2, LANES), f32),
+            jax.ShapeDtypeStruct((8 * per_dev, np2, LANES), f32),
         ],
-        scratch_shapes=[
-            pltpu.VMEM((2, np2, LANES), f32),
-            pltpu.VMEM((8 * per_dev, np2, LANES), f32),
-            pltpu.VMEM((2, images[0], LANES), f32),
-            pltpu.VMEM((LANES, 2 * nt2), f32),
-        ],
-        compiler_params=pltpu.CompilerParams(vmem_limit_bytes=(8 << 20) + np2 * (96 << 10)),
-        name="coefficients",
-    )(where, inc, child, phi_top, phi_mid, img, tit, twt, tim, twm)
+        scratch_shapes=[pltpu.VMEM((LANES, 2 * nt2), f32)],
+        compiler_params=pltpu.CompilerParams(vmem_limit_bytes=(8 << 20) + np2 * (64 << 10)),
+        name="tables",
+    )(where, child, phi_top, phi_mid, tit, twt, tim, twm)
+
+
+def lattice(where, inc, img, places, phases, exc, images):
+    np2 = places.shape[1]
+    per_dev = phases.shape[0] // 8
+    f32 = jnp.float32
+    return pl.pallas_call(
+        lambda *refs: lattice_kernel((exc, np2, images, per_dev), *refs),
+        in_specs=[SMEM] * 2 + [VMEM] * 3,
+        out_specs=VMEM,
+        out_shape=jax.ShapeDtypeStruct((np2, 8 * per_dev, exc, LANES), f32),
+        scratch_shapes=[pltpu.VMEM((2, images, LANES), f32)],
+        compiler_params=pltpu.CompilerParams(vmem_limit_bytes=(8 << 20) + np2 * (64 << 10)),
+        name="lattice",
+    )(where, inc, img, places, phases)
 
 
 def split_dot(x, m_ref):
@@ -335,29 +366,18 @@
     )
 
 
-def main_kernel(
-    sizes,
-    r_ref,
-    w_ref,
-    pw2_ref,
-    pw1_ref,
-    m2_ref,
-    m1_ref,
-    tc_ref,
-    ts_ref,
-    o_ref,
-    x_ref,
-    g_ref,
-    h_ref,
-    y_ref,
-    z_ref,
-    sems,
-):
-    exc, np2, np1, nt2, phi_local, per_dev = sizes
-    np0 = np1 // 2
-    mid_local = phi_local // 2
-    base = phi_local * per_dev * 2
-    mids = 4 * per_dev
+def upper_kernel(sizes, *refs):
+    exc, _, np1, _, phi_local, per_dev, outer, inner = sizes
+    parts = refs[:inner]
+    w_ref, pw2_ref, m2_ref, u_ref, r_ref, x_ref = refs[inner:]
+    me = lax.axis_index("dev")
+    for j in range(inner):
+
+        def place(k, j=j):
+            source = ((me // inner) ^ k) * inner + ((me % inner) ^ j)
+            r_ref[source] = parts[j][k]
+
+        loop(outer, place)
 
     for box in range(per_dev):
 
@@ -388,12 +408,7 @@
                 for slot in range(4):
                     row = (n * 4 + slot) * exc
                     mid = box * 4 + slot
-                    value = (
-                        done[row : row + exc]
-                        + r_ref[q // mid_local, base + mid * mid_local + q % mid_local]
-                    )
-                    g_ref[q, mid] = value
-                    h_ref[q, mid] = pltpu.roll(value, LANES // 2, 1)
+                    u_ref[q, mid] = done[row : row + exc]
 
         static = np1 <= 16
 
@@ -411,6 +426,22 @@
         if not static:
             loop(np1 // chunk, theta)
 
+
+def lower_kernel(
+    sizes, l_ref, u_ref, pw1_ref, m1_ref, tc_ref, ts_ref, o_ref, g_ref, h_ref, y_ref, z_ref, sems
+):
+    exc, np1, phi_local, per_dev = sizes
+    np0 = np1 // 2
+    mid_local = phi_local // 2
+    mids = 4 * per_dev
+
+    def join(q):
+        for mid in range(mids):
+            value = u_ref[q, mid] + l_ref[q // mid_local, mid * mid_local + q % mid_local]
+            g_ref[q, mid] = value
+            h_ref[q, mid] = pltpu.roll(value, LANES // 2, 1)
+
+    loop(np1, join)
     o_rows = o_ref.reshape(exc * 4 * mids, o_ref.shape[2])
 
     pairs = np0 // 2
@@ -467,27 +498,44 @@
     loop(pairs, lambda pair: leave(pair).wait())
 
 
-def main(received, coefs, exc, np2, np1, nt2, phi_local, per_dev):
+def upper(parts, coefs, exc, np2, np1, nt2, phi_local, per_dev, outer, inner):
+    f32 = jnp.float32
+    sizes = (exc, np2, np1, nt2, phi_local, per_dev, outer, inner)
+    tops = phi_local * 2 * per_dev
+    return pl.pallas_call(
+        lambda *refs: upper_kernel(sizes, *refs),
+        in_specs=[VMEM] * (inner + 3),
+        out_specs=VMEM,
+        out_shape=jax.ShapeDtypeStruct((np1, 4 * per_dev, exc, LANES), f32),
+        scratch_shapes=[
+            pltpu.VMEM((outer * inner, tops, exc, LANES), f32),
+            pltpu.VMEM((np1 * 4 * exc, 2 * LANES), f32),
+        ],
+        compiler_params=pltpu.CompilerParams(vmem_limit_bytes=(8 << 20) + np2 * (112 << 10)),
+        name="upper",
+    )(*parts, *coefs)
+
+
+def lower(received, above, coefs, exc, np1, nt2, phi_local, per_dev):
     mids = 4 * per_dev
     np0 = np1 // 2
     f32 = jnp.float32
-    sizes = (exc, np2, np1, nt2, phi_local, per_dev)
+    sizes = (exc, np1, phi_local, per_dev)
     return pl.pallas_call(
-        lambda *refs: main_kernel(sizes, *refs),
-        in_specs=[VMEM] * 8,
+        lambda *refs: lower_kernel(sizes, *refs),
+        in_specs=[VMEM] * 6,
         out_specs=pl.BlockSpec(memory_space=pltpu.HBM),
         out_shape=jax.ShapeDtypeStruct((exc, 4 * mids, np0 * (nt2 // 2)), f32),
         scratch_shapes=[
-            pltpu.VMEM((np1 * 4 * exc, 2 * LANES), f32),
             pltpu.VMEM((np1, mids, exc, LANES), f32),
             pltpu.VMEM((np1, mids, exc, LANES), f32),
             pltpu.VMEM((2, np0 // 2, 4 * exc, 2 * LANES), f32),
             pltpu.VMEM((np0 // 2, 4 * mids * exc, LANES), f32),
             pltpu.SemaphoreType.DMA((np0 // 2,)),
         ],
-        compiler_params=pltpu.CompilerParams(vmem_limit_bytes=(8 << 20) + np2 * (144 << 10)),
-        name="levels",
-    )(received, *coefs)
+        compiler_params=pltpu.CompilerParams(vmem_limit_bytes=(8 << 20) + np1 * (192 << 10)),
+        name="lower",
+    )(received, above, *coefs)
 
 
 def local(
@@ -513,8 +561,32 @@
     np1 = np2 // 2
     images = image_offsets.shape[0] * rhs_count
 
-    packed = pack(top_adj, level1_adj, dev_count)
-    received = lax.all_to_all(packed, "dev", split_axis=0, concat_axis=0, tiled=True)
+    outer, inner = factors(dev_count)
+    me = lax.axis_index("dev")
+    mids_out, *tops_out = pack(top_adj, level1_adj, dev_count)
+    planes = {0: tops_out[0]}
+    for k in order(outer):
+        planes[k] = lax.ppermute(
+            tops_out[k],
+            "dev",
+            [(s, ((s // inner) ^ k) * inner + s % inner) for s in range(dev_count)],
+        )
+    received = lax.all_to_all(mids_out, "dev", split_axis=0, concat_axis=0, tiled=True)
+    parts = []
+    for j in range(inner):
+        block = jnp.stack(
+            [
+                lax.dynamic_index_in_dim(planes[k], (me % inner) ^ j, 0, keepdims=False)
+                for k in range(outer)
+            ]
+        )
+        if j:
+            block = lax.ppermute(
+                block,
+                "dev",
+                [(s, s // inner * inner + ((s % inner) ^ j)) for s in range(dev_count)],
+            )
+        parts.append(block)
 
     own = jnp.concatenate(
         [
@@ -523,29 +595,36 @@
         ],
         axis=0,
     )
-    parts = [own]
+    images_of = [own]
     for shift in range(1, rhs_count):
-        parts.append(
+        images_of.append(
             lax.ppermute(own, "rhs", [(i, (i + shift) % rhs_count) for i in range(rhs_count)])
         )
-    img = jnp.concatenate(parts + [jnp.zeros((3, LANES - images), jnp.float32)], axis=1)
+    img = jnp.concatenate(images_of + [jnp.zeros((3, LANES - images), jnp.float32)], axis=1)
     where = jnp.stack([lax.axis_index("dev"), lax.axis_index("rhs")]).astype(jnp.int32)
-    coefs = coefficients(
+    pw2, pw1, m2, m1, tc, ts, places, phases = tables(
         where,
-        incidence.T,
         child_list,
         phi_weight_top.T,
         phi_weight_mid.T,
-        img,
         theta_index_top.T,
         theta_weight_top.T,
         theta_index_mid.T,
         theta_weight_mid.T,
         exc,
         nt2,
-        (images, per_dev),
+        per_dev,
     )
-    return main(received, coefs, exc, np2, np1, nt2, phi_local, per_dev)
+    w = lattice(where, incidence.T, img, places, phases, exc, images)
+    above = upper(
+        parts, (w, pw2, m2), exc, np2, np1, nt2, phi_local, per_dev, outer, inner
+    )
+    return lower(received, above, (pw1, m1, tc, ts), exc, np1, nt2, phi_local, per_dev)
+
+
+def order(count):
+    steps = list(range(1, count))
+    return steps[count // 2 - 1 :] + steps[: count // 2 - 1]
 
 
 def solution(mesh):

time: 25.6 us -> 35.3 us (1.38)
  starting transfers between devices: 8.98 us -> 15.4 us
  other arithmetic: 0.17 us -> 2.12 us
  waiting for transfers between devices: 7.77 us -> 8.35 us
  Pallas kernels: 6.21 us -> 6.65 us
    ppermute x0 -> x6, waiting for transfers between devices: none -> 8.34 us  [the longest x3 4.59 us: local(): lax.ppermute(tops_out[k], 'dev', [(s, (s // inner ^ k) * inner + s % inne...]
    all_to_all x1, waiting for transfers between devices: 6.52 us -> 0.01 us  [local(): lax.all_to_all(mids_out, 'dev', split_axis=0, concat_axis=0, tiled=True)]
    ppermute x0 -> x6, starting transfers between devices: none -> 6.36 us  [the longest x3 4.45 us: local(): lax.ppermute(tops_out[k], 'dev', [(s, (s // inner ^ k) * inner + s % inne...]
    ppermute x1, starting transfers between devices: 1.55 us -> 2.97 us  [local(): lax.ppermute(own, 'rhs', [(i, (i + shift) % rhs_count) for i in range(rhs...]
    all_to_all x1, starting transfers between devices: 7.43 us -> 6.08 us  [local(): lax.all_to_all(mids_out, 'dev', split_axis=0, concat_axis=0, tiled=True)]
    ppermute x1, waiting for transfers between devices: 1.25 us -> 0.01 us  [local(): lax.ppermute(own, 'rhs', [(i, (i + shift) % rhs_count) for i in range(rhs...]
    concatenate x1, other arithmetic: 0.08 us -> 0.75 us  [local(): jnp.concatenate(images_of + [jnp.zeros((3, LANES - images), jnp.float32)]...]
    mul x1, other arithmetic: 0.01 us -> 0.67 us  [local(): image_weights[None] * float(images) ** (-0.5)]
  transfers between devices with their start and end apart: 2 -> 8, of which waited for: 2 -> 3; matrix products, arithmetic and copies ran while one was open for 1% -> 3% of each run, Pallas kernels for 10% -> 15%
where the time goes in v4:
time: 35.3 us; the launch traced here: 35 us
  starting transfers between devices  15.4 us (44%)
  waiting for transfers between devices  8.35 us (24%)
  Pallas kernels  6.65 us (19%)
  local copies, waits for them, and re-layouts  2.21 us (6%)
  other arithmetic  2.12 us (6%)
    all_to_all x1, starting transfers between devices, local(): lax.all_to_all(mids_out, 'dev', split_axis=0, concat_axis=0, tiled=True)  6.08 us
    ppermute x3, waiting for transfers between devices, local(): lax.ppermute(tops_out[k], 'dev', [(s, (s // inner ^ k) * inner + s % inne...  4.59 us
    ppermute x3, starting transfers between devices, local(): lax.ppermute(tops_out[k], 'dev', [(s, (s // inner ^ k) * inner + s % inne...  4.45 us
    ppermute x3, waiting for transfers between devices, local(): lax.ppermute(block, 'dev', [(s, s // inner * inner + (s % inner ^ j)) for...  3.75 us
    ppermute x1, starting transfers between devices, local(): lax.ppermute(own, 'rhs', [(i, (i + shift) % rhs_count) for i in range(rhs...  2.97 us
    unnamed x35, local copies, waits for them, and re-layouts  2.08 us
    pallas_call x1, Pallas kernels, pack(): pl.pallas_call(lambda *refs: pack_kernel(per_dest, outer, inner, *refs),...  2.02 us
    ppermute x3, starting transfers between devices, local(): lax.ppermute(block, 'dev', [(s, s // inner * inner + (s % inner ^ j)) for...  1.91 us
  transfers between devices with their start and end apart: 8, of which 3 were waited for; matrix products, arithmetic and copies ran while one was open for 3% of the time, Pallas kernels for 15%

profile of v4, /device:TPU:0, one launch (start us, length us, event | category | flops | bytes accessed | tf_op | source)
XLA Modules:
  0.0 35.0 jit_solution(11840752465471874409)
XLA Ops:
  0.0 0.7 %multiply_bitcast_fusion = f32[1,32]{1,0:T(1,128)S(1)} fusion(f32[32]{0:T(128)} %param.15), kind=kLoop, calls=%fused_computation.24 | loop fusion | flops 32 | bytes 256 | tf_op jit(solution)/shard_map/mul | solution.py:594
  0.7 0.6 %copy-done.11 = f32[1,32]{1,0:T(1,128)} copy-done((f32[1,32]{1,0:T(1,128)}, f32[1,32]{1,0:T(1,128)S(1)}, u32[]{:S(2)}) %copy-start.11) | copy-done | bytes 152
  1.3 0.6 %pad_maximum_fusion.4 = f32[3,32]{1,0:T(4,128)} fusion(f32[1,32]{1,0:T(1,128)S(1)} %multiply_bitcast_fusion, f32[2,32]{1,0:T(2,128)S(1)} %convert_bitcast_fusion), kind=kLoop, calls=%fused_computation.20 | loop fusion | flops 96 | bytes 768 | tf_op jit(solution)/shard_map/concatenate | solution.py:591
  1.9 3.0 %collective-permute-start.6 = (f32[3,32]{1,0:T(4,128)}, f32[3,32]{1,0:T(4,128)}, u32[]{:S(2)}, u32[]{:S(2)}) collective-permute-start(f32[3,32]{1,0:T(4,128)} %pad_maximum_fusion.4), channel_id=1, source_target_pairs={{0,1},{1,0},{2,3},{3,2},{4,5},{5,4},{6,7},{7,6},{8,9},{9,8},{10,11... | collective-permute-start | bytes 1160 | tf_op jit(solution)/shard_map/ppermute | solution.py:601
  4.8 2.0 %pack.1 = (f32[16,4,8,128]{3,2,1,0:T(8,128)}, f32[4,4,8,128]{3,2,1,0:T(8,128)}, f32[4,4,8,128]{3,2,1,0:T(8,128)}, f32[4,4,8,128]{3,2,1,0:T(8,128)}, f32[4,4,8,128]{3,2,1,0:T(8,128)}) custom-call(f32[8,2,16,256]{3,2,1,0:T(8,128)} %refs_0_.1, f32[8,1,64,128]{3,2,1,0:T(8,128)} %refs_1_.2), custom_call_target="tpu_custom_call" | custom-call | tf_op jit(solution)/shard_map/pack/pallas_call | solution.py:126
  6.9 6.1 %all-to-all-start = ((f32[16,4,8,128]{3,2,1,0:T(8,128)}), f32[16,4,8,128]{3,2,1,0:T(8,128)S(1)}, u32[]{:S(2)}, u32[]{:S(2)}) async-start(f32[16,4,8,128]{3,2,1,0:T(8,128)} %get-tuple-element.18), calls=%async_computation | async-start | bytes 524288 | tf_op jit(solution)/shard_map/all_to_all | solution.py:574
  13.0 2.0 %collective-permute-start = (f32[4,4,8,128]{3,2,1,0:T(8,128)S(1)}, f32[4,4,8,128]{3,2,1,0:T(8,128)S(1)}, u32[]{:S(2)}, u32[]{:S(2)}) collective-permute-start(f32[4,4,8,128]{3,2,1,0:T(8,128)S(1)} %copy-done.16), channel_id=1, source_target_pairs={{0,8},{2,10},{4,12},{6,14},{8,0},{10,2},{12,4},{14,6},{16,24},{18,... | collective-permute-start | bytes 196616 | tf_op jit(solution)/shard_map/ppermute | solution.py:569
  15.0 2.4 %collective-permute-start.1 = (f32[4,4,8,128]{3,2,1,0:T(8,128)S(1)}, f32[4,4,8,128]{3,2,1,0:T(8,128)S(1)}, u32[]{:S(2)}, u32[]{:S(2)}) collective-permute-start(f32[4,4,8,128]{3,2,1,0:T(8,128)S(1)} %copy-done.15), channel_id=1, source_target_pairs={{0,16},{2,18},{4,20},{6,22},{8,24},{10,26},{12,28},{14,30},{16,0},... | collective-permute-start | bytes 196616 | tf_op jit(solution)/shard_map/ppermute | solution.py:569
  17.4 0.1 collective-permute-start.2
  17.5 0.1 copy.13.refs_1_
  17.5 0.1 pad_add_fusion.refs_0_
  17.6 0.1 pad.3.clone
  17.8 0.6 %copy-done.2 = s32[128,3]{0,1:T(4,128)S(1)} copy-done((s32[128,3]{0,1:T(4,128)S(1)}, s32[128,3]{0,1:T(4,128)}, u32[]{:S(2)}) %copy-start.2) | copy-done | bytes 1560
  18.5 1.3 %tables.1 = (f32[96,8,128]{2,1,0:T(8,128)S(1)}, f32[48,8,128]{2,1,0:T(8,128)S(1)}, bf16[256,256]{1,0:T(8,128)(2,1)S(1)}, bf16[256,256]{1,0:T(8,128)(2,1)S(1)}, f...) custom-call(s32[2]{0:T(128)S(1)} %pad_add_fusion.refs_0_, ...), custom_call_target="tpu_custom_call" | custom-call | tf_op jit(solution)/shard_map/tables/pallas_call | solution.py:295
  19.8 0.8 %maximum_maximum_fusion.refs_2_ = f32[3,128]{1,0:T(4,128)S(1)} fusion(f32[3,32]{1,0:T(4,128)} %collective-permute-done.6, f32[1,32]{1,0:T(1,128)S(1)} %copy-done.12, f32[2,32]{1,0:T(2,128)S(1)} %copy-done.9, f32[128]{0:T(128)S(1)} %pad.3.clone), kind=kLoop, calls=%fused_computation.21 | loop fusion | flops 1152 | bytes 2816 | tf_op jit(solution)/shard_map/concatenate | solution.py:603
  20.5 0.7 %copy-done.6 = f32[16,2]{0,1:T(2,128)S(1)} copy-done((f32[16,2]{0,1:T(2,128)S(1)}, f32[16,2]{0,1:T(2,128)}, u32[]{:S(2)}) %copy-start.6) | copy-done | bytes 152
  21.2 1.6 %lattice.1.refs_4_ = f32[32,8,8,128]{3,2,1,0:T(8,128)S(1)} custom-call(s32[2]{0:T(128)S(1)} %pad_add_fusion.refs_0_, f32[2,16]{1,0:T(2,128)S(1)} %bitcast.19, f32[3,128]{1,0:T(4,128)S(1)} %maximum_maximum_fusion.refs_2_, f32[2,32,128]{2,1,0:T(8,128)S(1)} %get-tuple-element.23.refs_3_, f32[8,32,128]{2,1,0:T(8,128)S(1)} %get-tuple-element.24.refs_4_), custom_call_target="tpu_custom_call" | custom-call | tf_op jit(solution)/shard_map/lattice/pallas_call | solution.py:319
  22.8 4.6 %collective-permute-done.1 = f32[4,4,8,128]{3,2,1,0:T(8,128)S(1)} collective-permute-done((f32[4,4,8,128]{3,2,1,0:T(8,128)S(1)}, f32[4,4,8,128]{3,2,1,0:T(8,128)S(1)}, u32[]{:S(2)}, u32[]{:S(2)}) %collective-permute-start.1) | collective-permute-done | bytes 65568 | tf_op jit(solution)/shard_map/ppermute | solution.py:569
  27.5 1.5 %collective-permute-start.4 = (f32[4,4,8,128]{3,2,1,0:T(8,128)S(1)}, f32[4,4,8,128]{3,2,1,0:T(8,128)S(1)}, u32[]{:S(2)}, u32[]{:S(2)}) collective-permute-start(f32[4,4,8,128]{3,2,1,0:T(8,128)S(1)} %pad_maximum_fusion.2), channel_id=1, source_target_pairs={{0,4},{2,6},{4,0},{6,2},{8,12},{10,14},{12,8},{14,10},{16,20},{18,... | collective-permute-start | bytes 196616 | tf_op jit(solution)/shard_map/ppermute | solution.py:584
  29.1 0.3 collective-permute-start.5
  29.4 2.6 %collective-permute-done.4.refs_2_ = f32[4,4,8,128]{3,2,1,0:T(8,128)S(1)} collective-permute-done((f32[4,4,8,128]{3,2,1,0:T(8,128)S(1)}, f32[4,4,8,128]{3,2,1,0:T(8,128)S(1)}, u32[]{:S(2)}, u32[]{:S(2)}) %collective-permute-start.4) | collective-permute-done | bytes 65568 | tf_op jit(solution)/shard_map/ppermute | solution.py:584
  32.0 1.1 %collective-permute-done.5.refs_3_ = f32[4,4,8,128]{3,2,1,0:T(8,128)S(1)} collective-permute-done((f32[4,4,8,128]{3,2,1,0:T(8,128)S(1)}, f32[4,4,8,128]{3,2,1,0:T(8,128)S(1)}, u32[]{:S(2)}, u32[]{:S(2)}) %collective-permute-start.5) | collective-permute-done | bytes 65568 | tf_op jit(solution)/shard_map/ppermute | solution.py:584
  33.1 0.5 %upper.1.refs_1_ = f32[16,4,8,128]{3,2,1,0:T(8,128)S(1)} custom-call(f32[4,4,8,128]{3,2,1,0:T(8,128)S(1)} %pad_maximum_fusion.refs_0_, f32[4,4,8,128]{3,2,1,0:T(8,128)S(1)} %collective-permute-done.3.refs_1_, f32[4,4,8,128]{3,2,1,0:T(8,128)S(1)} %collective-permute-done.4.refs_2_, f32[4,4,8,128]{3,2,1,0:T(8,128)S(1)} %collective-permute-done.5.refs_3_, ...), custom_call_target="tpu_custom_call" | custom-call | tf_op jit(solution)/shard_map/upper/pallas_call | solution.py:505
  33.7 1.3 %lower.1 = f32[8,16,512]{2,1,0:T(8,128)} custom-call(f32[16,4,8,128]{3,2,1,0:T(8,128)S(1)} %all-to-all-done.refs_0_, f32[16,4,8,128]{3,2,1,0:T(8,128)S(1)} %upper.1.refs_1_, f32[48,8,128]{2,1,0:T(8,128)S(1)} %get-tuple-element.27.refs_2_, bf16[256,256]{1,0:T(8,128)(2,1)S(1)} %get-tuple-element.28.refs_3_, f32[64,128]{1,0:T(8,128)S(1)} %get-tuple-element.29.refs_4_, ...), custom_call_target="tpu_custom_call" | custom-call | tf_op jit(solution)/shard_map/lower/pallas_call | solution.py:524
  (47 shorter events, 0.3 us)
Async XLA Ops:
  0.0 0.7 %copy-start.13 = (s32[32,2]{0,1:T(2,128)S(1)}, s32[32,2]{0,1:T(2,128)}, u32[]{:S(2)}) copy-start(s32[32,2]{0,1:T(2,128)} %param.14) | copy-start | bytes 772
  1.3 0.6 %copy-start.8 = (f32[2,32]{1,0:T(2,128)}, f32[2,32]{1,0:T(2,128)S(1)}, u32[]{:S(2)}) copy-start(f32[2,32]{1,0:T(2,128)S(1)} %convert_bitcast_fusion) | copy-start | bytes 772
  1.9 17.9 %collective-permute-start.6 = (f32[3,32]{1,0:T(4,128)}, f32[3,32]{1,0:T(4,128)}, u32[]{:S(2)}, u32[]{:S(2)}) collective-permute-start(f32[3,32]{1,0:T(4,128)} %pad_maximum_fusion.4), channel_id=1, source_target_pairs={{0,1},{1,0},{2,3},{3,2},{4,5},{5,4},{6,7},{7,6},{8,9},{9,8},{10,11... | collective-permute-start | bytes 1160 | tf_op jit(solution)/shard_map/ppermute | solution.py:601
  6.8 6.1 %copy-start.16 = (f32[4,4,8,128]{3,2,1,0:T(8,128)S(1)}, f32[4,4,8,128]{3,2,1,0:T(8,128)}, u32[]{:S(2)}) copy-start(f32[4,4,8,128]{3,2,1,0:T(8,128)} %get-tuple-element.20) | copy-start | bytes 196612
  6.9 8.1 %copy-start.15 = (f32[4,4,8,128]{3,2,1,0:T(8,128)S(1)}, f32[4,4,8,128]{3,2,1,0:T(8,128)}, u32[]{:S(2)}) copy-start(f32[4,4,8,128]{3,2,1,0:T(8,128)} %get-tuple-element.21) | copy-start | bytes 196612
  6.9 10.5 %copy-start.14 = (f32[4,4,8,128]{3,2,1,0:T(8,128)S(1)}, f32[4,4,8,128]{3,2,1,0:T(8,128)}, u32[]{:S(2)}) copy-start(f32[4,4,8,128]{3,2,1,0:T(8,128)} %get-tuple-element.22) | copy-start | bytes 196612
  6.9 10.6 %copy-start.10 = (s32[16,4]{0,1:T(4,128)S(1)}, s32[16,4]{0,1:T(4,128)}, u32[]{:S(2)}) copy-start(s32[16,4]{0,1:T(4,128)} %param.17) | copy-start | bytes 772
  6.9 26.8 %all-to-all-start = ((f32[16,4,8,128]{3,2,1,0:T(8,128)}), f32[16,4,8,128]{3,2,1,0:T(8,128)S(1)}, u32[]{:S(2)}, u32[]{:S(2)}) async-start(f32[16,4,8,128]{3,2,1,0:T(8,128)} %get-tuple-element.18), calls=%async_computation | async-start | bytes 524288 | tf_op jit(solution)/shard_map/all_to_all | solution.py:574
  13.0 4.7 %copy-start.7 = (f32[4,4,8,128]{3,2,1,0:T(8,128)S(1)}, f32[4,4,8,128]{3,2,1,0:T(8,128)}, u32[]{:S(2)}) copy-start(f32[4,4,8,128]{3,2,1,0:T(8,128)} %get-tuple-element.19) | copy-start | bytes 196612
  13.0 9.8 %collective-permute-start = (f32[4,4,8,128]{3,2,1,0:T(8,128)S(1)}, f32[4,4,8,128]{3,2,1,0:T(8,128)S(1)}, u32[]{:S(2)}, u32[]{:S(2)}) collective-permute-start(f32[4,4,8,128]{3,2,1,0:T(8,128)S(1)} %copy-done.16), channel_id=1, source_target_pairs={{0,8},{2,10},{4,12},{6,14},{8,0},{10,2},{12,4},{14,6},{16,24},{18,... | collective-permute-start | bytes 196616 | tf_op jit(solution)/shard_map/ppermute | solution.py:569
  15.0 12.4 %collective-permute-start.1 = (f32[4,4,8,128]{3,2,1,0:T(8,128)S(1)}, f32[4,4,8,128]{3,2,1,0:T(8,128)S(1)}, u32[]{:S(2)}, u32[]{:S(2)}) collective-permute-start(f32[4,4,8,128]{3,2,1,0:T(8,128)S(1)} %copy-done.15), channel_id=1, source_target_pairs={{0,16},{2,18},{4,20},{6,22},{8,24},{10,26},{12,28},{14,30},{16,0},... | collective-permute-start | bytes 196616 | tf_op jit(solution)/shard_map/ppermute | solution.py:569
  17.4 10.0 %collective-permute-start.2 = (f32[4,4,8,128]{3,2,1,0:T(8,128)S(1)}, f32[4,4,8,128]{3,2,1,0:T(8,128)S(1)}, u32[]{:S(2)}, u32[]{:S(2)}) collective-permute-start(f32[4,4,8,128]{3,2,1,0:T(8,128)S(1)} %copy-done.14), channel_id=1, source_target_pairs={{0,24},{2,26},{4,28},{6,30},{8,16},{10,18},{12,20},{14,22},{16,8},... | collective-permute-start | bytes 196616 | tf_op jit(solution)/shard_map/ppermute | solution.py:569
  17.7 0.7 %copy-start.2 = (s32[128,3]{0,1:T(4,128)S(1)}, s32[128,3]{0,1:T(4,128)}, u32[]{:S(2)}) copy-start(s32[128,3]{0,1:T(4,128)} %param.18) | copy-start | bytes 4612
  17.7 0.7 %copy-start.3 = (f32[128,3]{0,1:T(4,128)S(1)}, f32[128,3]{0,1:T(4,128)}, u32[]{:S(2)}) copy-start(f32[128,3]{0,1:T(4,128)} %param.19) | copy-start | bytes 4612
  17.7 0.7 %copy-start.4 = (s32[64,3]{0,1:T(4,128)S(1)}, s32[64,3]{0,1:T(4,128)}, u32[]{:S(2)}) copy-start(s32[64,3]{0,1:T(4,128)} %param.21) | copy-start | bytes 2308
  17.7 0.7 %copy-start.5 = (f32[64,3]{0,1:T(4,128)S(1)}, f32[64,3]{0,1:T(4,128)}, u32[]{:S(2)}) copy-start(f32[64,3]{0,1:T(4,128)} %param.22) | copy-start | bytes 2308
  17.7 0.7 %copy-start.1 = (f32[16,3]{0,1:T(4,128)S(1)}, f32[16,3]{0,1:T(4,128)}, u32[]{:S(2)}) copy-start(f32[16,3]{0,1:T(4,128)} %param.23) | copy-start | bytes 580
  17.8 0.7 %copy-start = (f32[32,3]{0,1:T(4,128)S(1)}, f32[32,3]{0,1:T(4,128)}, u32[]{:S(2)}) copy-start(f32[32,3]{0,1:T(4,128)} %param.20) | copy-start | bytes 1156
  18.5 1.3 %copy-start.9 = (f32[2,32]{1,0:T(2,128)S(1)}, f32[2,32]{1,0:T(2,128)}, u32[]{:S(2)}) copy-start(f32[2,32]{1,0:T(2,128)} %copy-done.8) | copy-start | bytes 772
  18.5 1.3 %copy-start.12 = (f32[1,32]{1,0:T(1,128)S(1)}, f32[1,32]{1,0:T(1,128)}, u32[]{:S(2)}) copy-start(f32[1,32]{1,0:T(1,128)} %copy-done.11) | copy-start | bytes 388
  20.5 0.7 %copy-start.6 = (f32[16,2]{0,1:T(2,128)S(1)}, f32[16,2]{0,1:T(2,128)}, u32[]{:S(2)}) copy-start(f32[16,2]{0,1:T(2,128)} %param.16) | copy-start | bytes 388
  27.4 1.9 %collective-permute-start.3 = (f32[4,4,8,128]{3,2,1,0:T(8,128)S(1)}, f32[4,4,8,128]{3,2,1,0:T(8,128)S(1)}, u32[]{:S(2)}, u32[]{:S(2)}) collective-permute-start(f32[4,4,8,128]{3,2,1,0:T(8,128)S(1)} %pad_maximum_fusion.1), channel_id=1, source_target_pairs={{0,2},{2,0},{4,6},{6,4},{8,10},{10,8},{12,14},{14,12},{16,18},{18,... | collective-permute-start | bytes 196616 | tf_op jit(solution)/shard_map/ppermute | solution.py:584
  27.5 4.5 %collective-permute-start.4 = (f32[4,4,8,128]{3,2,1,0:T(8,128)S(1)}, f32[4,4,8,128]{3,2,1,0:T(8,128)S(1)}, u32[]{:S(2)}, u32[]{:S(2)}) collective-permute-start(f32[4,4,8,128]{3,2,1,0:T(8,128)S(1)} %pad_maximum_fusion.2), channel_id=1, source_target_pairs={{0,4},{2,6},{4,0},{6,2},{8,12},{10,14},{12,8},{14,10},{16,20},{18,... | collective-permute-start | bytes 196616 | tf_op jit(solution)/shard_map/ppermute | solution.py:584
  29.1 4.1 %collective-permute-start.5 = (f32[4,4,8,128]{3,2,1,0:T(8,128)S(1)}, f32[4,4,8,128]{3,2,1,0:T(8,128)S(1)}, u32[]{:S(2)}, u32[]{:S(2)}) collective-permute-start(f32[4,4,8,128]{3,2,1,0:T(8,128)S(1)} %pad_maximum_fusion.3), channel_id=1, source_target_pairs={{0,6},{2,4},{4,2},{6,0},{8,14},{10,12},{12,10},{14,8},{16,22},{18,... | collective-permute-start | bytes 196616 | tf_op jit(solution)/shard_map/ppermute | solution.py:584
  (1 other events, 0.6 us)

commit v5 on v4

--- a/solution.py
+++ b/solution.py
@@ -12,6 +12,7 @@
 PHASE_MID = 9.42
 LATTICE = 12.57
 LANES = 128
+MOVED = 1
 VMEM = pl.BlockSpec(memory_space=pltpu.VMEM)
 SMEM = pl.BlockSpec(memory_space=pltpu.SMEM)
 
@@ -110,7 +111,17 @@
         scatter(mid_ref.at[:, phi], mid_out.at[phi])
         split = mid_out.at[phi].reshape(boxes // per_dest, 4 * per_dest, exc, LANES)
         for mid in range(4 * per_dest):
-            send(split.at[:, mid], mid_hbm.at[:, mid * mid_phi + phi])
+            box, slot = divmod(mid, 4)
+            if slot < MOVED:
+                tile = (2 * phi_local * per_dest) + (box * MOVED + slot) * mid_phi + phi
+                for other in range(outer):
+                    send(
+                        split.at[pl.ds((plane ^ other) * inner, inner), mid],
+                        top_hbm[other].at[:, tile],
+                    )
+            else:
+                tile = (box * (4 - MOVED) + slot - MOVED) * mid_phi + phi
+                send(split.at[:, mid], mid_hbm.at[:, tile])
     for copy in leave:
         copy.wait()
 
@@ -120,14 +131,15 @@
     mid_phi, mids = level1_adj.shape[1:3]
     per_dest = boxes // dev_count
     outer, inner = factors(dev_count)
-    tops = phi_local * 2 * per_dest
+    tops = (phi_local * 2 + MOVED * mid_phi) * per_dest
+    rest = (4 - MOVED) * per_dest * mid_phi
     f32 = jnp.float32
     hbm = pl.BlockSpec(memory_space=pltpu.HBM)
     return pl.pallas_call(
         lambda *refs: pack_kernel(per_dest, outer, inner, *refs),
         in_specs=[hbm] * 2,
         out_specs=[hbm] * (1 + outer),
-        out_shape=[jax.ShapeDtypeStruct((dev_count, 4 * per_dest * mid_phi, exc, LANES), f32)]
+        out_shape=[jax.ShapeDtypeStruct((dev_count, rest, exc, LANES), f32)]
         + [jax.ShapeDtypeStruct((inner, tops, exc, LANES), f32)] * outer,
         scratch_shapes=[
             pltpu.VMEM((exc, phi_local, boxes, LANES), f32),
@@ -135,7 +147,7 @@
             pltpu.VMEM((exc, mid_phi, mids, LANES), f32),
             pltpu.VMEM((phi_local * 2, boxes, exc, LANES), f32),
             pltpu.VMEM((mid_phi, mids, exc, LANES), f32),
-            pltpu.SemaphoreType.DMA((3 + outer * tops + 4 * per_dest * mid_phi,)),
+            pltpu.SemaphoreType.DMA((3 + outer * tops + rest,)),
         ],
         compiler_params=pltpu.CompilerParams(vmem_limit_bytes=67043328),
         name="pack",
@@ -154,7 +166,6 @@
 
 def table_kernel(
     sizes,
-    where_ref,
     child_ref,
     phi_top_ref,
     phi_mid_ref,
@@ -162,6 +173,7 @@
     weight_top_ref,
     index_mid_ref,
     weight_mid_ref,
+    inc_ref,
     pw2_ref,
     pw1_ref,
     m2_ref,
@@ -170,11 +182,19 @@
     ts_ref,
     dir_ref,
     ph_ref,
+    kk_ref,
     fm_ref,
 ):
     exc, np2, np1, nt2, per_dev = sizes
     nt1, nt0 = nt2 // 2, nt2 // 4
-    first_box = where_ref[0] * per_dev
+    first_box = lax.axis_index("dev") * per_dev
+
+    lanes = lax.broadcasted_iota(jnp.int32, (exc, inc_ref.shape[1]), 1)
+    rows = lax.broadcasted_iota(jnp.int32, (exc, inc_ref.shape[1]), 0)
+    own = lanes == rows + lax.axis_index("rhs") * exc
+    for axis in range(2):
+        value = jnp.sum(jnp.where(own, inc_ref[axis : axis + 1, :], 0.0), axis=1, keepdims=True)
+        kk_ref[axis] = jnp.broadcast_to(value, (exc, LANES))
 
     def splat_top(p):
         for s in range(3):
@@ -224,7 +244,7 @@
             fx = jnp.float32(0.0)
             fy = jnp.float32(0.0)
             for octant in range(4):
-                hit = child_ref[first_box + box, octant] == 4 * (first_box + box) + slot
+                hit = child_ref[octant, first_box + box] == 4 * (first_box + box) + slot
                 fx = fx + jnp.where(hit, jnp.float32(2.0 * (octant % 2) - 1.0), jnp.float32(0.0))
                 fy = fy + jnp.where(hit, jnp.float32(2.0 * (octant // 2) - 1.0), jnp.float32(0.0))
             re, im = cmul(axc, fx * axs, ayc, fy * ays)
@@ -233,21 +253,16 @@
             ph_ref[box * 8 + slot * 2 + 1] = im
 
 
-def lattice_kernel(
-    sizes, where_ref, inc_ref, img_ref, dir_ref, ph_ref, w_ref, ob_ref
-):
+def lattice_kernel(sizes, inc_ref, img_ref, dir_ref, ph_ref, w_ref, ob_ref):
     exc, np2, images, per_dev = sizes
     half = np2 // 2
-    first_exc = where_ref[1] * exc
+
+    def column(row):
+        return jnp.transpose(jnp.broadcast_to(row, (LANES, LANES)))
 
     image = img_ref[...]
     ox, oy, wt = image[0:1, :], image[1:2, :], image[2:3, :]
-    excs = lax.broadcasted_iota(jnp.int32, (exc, LANES), 0)
-    kx = jnp.zeros((exc, LANES), jnp.float32)
-    ky = jnp.zeros((exc, LANES), jnp.float32)
-    for e in range(exc):
-        kx = jnp.where(excs == e, inc_ref[0, first_exc + e], kx)
-        ky = jnp.where(excs == e, inc_ref[1, first_exc + e], ky)
+    kx, ky = inc_ref[0], inc_ref[1]
     fs, fc = sincos(LATTICE / math.pi * (ox * kx + oy * ky))
     wc = (wt * fc)[:, :images]
     ws = (wt * fs)[:, :images]
@@ -261,8 +276,8 @@
     left_high = left.astype(jnp.bfloat16)
     left_low = (left - left_high.astype(jnp.float32)).astype(jnp.bfloat16)
     left_both = jnp.concatenate([left_high, left_low], axis=0)
-    ob_ref[0] = jnp.transpose(jnp.broadcast_to(LATTICE / math.pi * ox, (LANES, LANES)))[:images]
-    ob_ref[1] = jnp.transpose(jnp.broadcast_to(LATTICE / math.pi * oy, (LANES, LANES)))[:images]
+    ob_ref[0] = column(LATTICE / math.pi * ox)[:images]
+    ob_ref[1] = column(LATTICE / math.pi * oy)[:images]
 
     def sample(p):
         ux_row = dir_ref[0, pl.ds(p, 1), :]
@@ -288,14 +303,14 @@
     loop(half, sample)
 
 
-def tables(where, child, phi_top, phi_mid, tit, twt, tim, twm, exc, nt2, per_dev):
+def tables(child, phi_top, phi_mid, tit, twt, tim, twm, inc, exc, nt2, per_dev):
     np2, np1 = phi_top.shape[1], phi_mid.shape[1]
     sizes = (exc, np2, np1, nt2, per_dev)
     f32 = jnp.float32
     return pl.pallas_call(
         lambda *refs: table_kernel(sizes, *refs),
-        in_specs=[SMEM] * 4 + [VMEM] * 4,
-        out_specs=[VMEM] * 8,
+        in_specs=[SMEM] * 3 + [VMEM] * 5,
+        out_specs=[VMEM] * 9,
         out_shape=[
             jax.ShapeDtypeStruct((np2 * 3, exc, LANES), f32),
             jax.ShapeDtypeStruct((np1 * 3, exc, LANES), f32),
@@ -305,26 +320,27 @@
             jax.ShapeDtypeStruct((4 * np1, LANES), f32),
             jax.ShapeDtypeStruct((2, np2, LANES), f32),
             jax.ShapeDtypeStruct((8 * per_dev, np2, LANES), f32),
+            jax.ShapeDtypeStruct((2, exc, LANES), f32),
         ],
         scratch_shapes=[pltpu.VMEM((LANES, 2 * nt2), f32)],
         compiler_params=pltpu.CompilerParams(vmem_limit_bytes=(8 << 20) + np2 * (64 << 10)),
         name="tables",
-    )(where, child, phi_top, phi_mid, tit, twt, tim, twm)
-
-
-def lattice(where, inc, img, places, phases, exc, images):
+    )(child, phi_top, phi_mid, tit, twt, tim, twm, inc)
+
+
+def lattice(inc, img, places, phases, exc, images):
     np2 = places.shape[1]
     per_dev = phases.shape[0] // 8
     f32 = jnp.float32
     return pl.pallas_call(
         lambda *refs: lattice_kernel((exc, np2, images, per_dev), *refs),
-        in_specs=[SMEM] * 2 + [VMEM] * 3,
+        in_specs=[VMEM] * 4,
         out_specs=VMEM,
         out_shape=jax.ShapeDtypeStruct((np2, 8 * per_dev, exc, LANES), f32),
         scratch_shapes=[pltpu.VMEM((2, images, LANES), f32)],
         compiler_params=pltpu.CompilerParams(vmem_limit_bytes=(8 << 20) + np2 * (64 << 10)),
         name="lattice",
-    )(where, inc, img, places, phases)
+    )(inc, img, places, phases)
 
 
 def split_dot(x, m_ref):
@@ -370,6 +386,8 @@
     exc, _, np1, _, phi_local, per_dev, outer, inner = sizes
     parts = refs[:inner]
     w_ref, pw2_ref, m2_ref, u_ref, r_ref, x_ref = refs[inner:]
+    mid_local = phi_local // 2
+    tops = phi_local * 2 * per_dev
     me = lax.axis_index("dev")
     for j in range(inner):
 
@@ -408,7 +426,11 @@
                 for slot in range(4):
                     row = (n * 4 + slot) * exc
                     mid = box * 4 + slot
-                    u_ref[q, mid] = done[row : row + exc]
+                    value = done[row : row + exc]
+                    if slot < MOVED:
+                        tile = tops + (box * MOVED + slot) * mid_local + q % mid_local
+                        value = value + r_ref[q // mid_local, tile]
+                    u_ref[q, mid] = value
 
         static = np1 <= 16
 
@@ -437,7 +459,11 @@
 
     def join(q):
         for mid in range(mids):
-            value = u_ref[q, mid] + l_ref[q // mid_local, mid * mid_local + q % mid_local]
+            value = u_ref[q, mid]
+            box, slot = divmod(mid, 4)
+            if slot >= MOVED:
+                tile = (box * (4 - MOVED) + slot - MOVED) * mid_local + q % mid_local
+                value = value + l_ref[q // mid_local, tile]
             g_ref[q, mid] = value
             h_ref[q, mid] = pltpu.roll(value, LANES // 2, 1)
 
@@ -501,7 +527,7 @@
 def upper(parts, coefs, exc, np2, np1, nt2, phi_local, per_dev, outer, inner):
     f32 = jnp.float32
     sizes = (exc, np2, np1, nt2, phi_local, per_dev, outer, inner)
-    tops = phi_local * 2 * per_dev
+    tops = parts[0].shape[1]
     return pl.pallas_call(
         lambda *refs: upper_kernel(sizes, *refs),
         in_specs=[VMEM] * (inner + 3),
@@ -601,21 +627,20 @@
             lax.ppermute(own, "rhs", [(i, (i + shift) % rhs_count) for i in range(rhs_count)])
         )
     img = jnp.concatenate(images_of + [jnp.zeros((3, LANES - images), jnp.float32)], axis=1)
-    where = jnp.stack([lax.axis_index("dev"), lax.axis_index("rhs")]).astype(jnp.int32)
-    pw2, pw1, m2, m1, tc, ts, places, phases = tables(
-        where,
-        child_list,
+    pw2, pw1, m2, m1, tc, ts, places, phases, incident = tables(
+        child_list.T,
         phi_weight_top.T,
         phi_weight_mid.T,
         theta_index_top.T,
         theta_weight_top.T,
         theta_index_mid.T,
         theta_weight_mid.T,
+        incidence.T,
         exc,
         nt2,
         per_dev,
     )
-    w = lattice(where, incidence.T, img, places, phases, exc, images)
+    w = lattice(incident, img, places, phases, exc, images)
     above = upper(
         parts, (w, pw2, m2), exc, np2, np1, nt2, phi_local, per_dev, outer, inner
     )

time: 35.3 us -> 35.6 us (level)
  waiting for transfers between devices: 8.35 us -> 10.1 us
  local copies, waits for them, and re-layouts: 2.21 us -> 1.44 us
  Pallas kernels: 6.65 us -> 6.09 us
    ppermute x3, waiting for transfers between devices: 4.59 us -> 5.7 us  [local(): lax.ppermute(tops_out[k], 'dev', [(s, (s // inner ^ k) * inner + s % inne...]
    unnamed x35 -> x34, local copies, waits for them, and re-layouts: 2.08 us -> 1.33 us
    ppermute x3, waiting for transfers between devices: 3.75 us -> 4.42 us  [local(): lax.ppermute(block, 'dev', [(s, s // inner * inner + (s % inner ^ j)) for...]
    pallas_call x1, Pallas kernels: 1.55 us -> 1 us  [lattice(): pl.pallas_call(lambda *refs: lattice_kernel((exc, np2, images, per_dev),...]
  transfers between devices with their start and end apart: 8 -> 8, of which waited for: 3 -> 3; matrix products, arithmetic and copies ran while one was open for 3% -> 3% of each run, Pallas kernels for 15% -> 14%
where the time goes in v5:
time: 35.6 us; the launch traced here: 35.3 us
  starting transfers between devices  15.4 us (43%)
  waiting for transfers between devices  10.1 us (28%)
  Pallas kernels  6.09 us (17%)
  other arithmetic  2.04 us (6%)
  local copies, waits for them, and re-layouts  1.44 us (4%)
    all_to_all x1, starting transfers between devices, local(): lax.all_to_all(mids_out, 'dev', split_axis=0, concat_axis=0, tiled=True)  6.08 us
    ppermute x3, waiting for transfers between devices, local(): lax.ppermute(tops_out[k], 'dev', [(s, (s // inner ^ k) * inner + s % inne...  5.7 us
    ppermute x3, starting transfers between devices, local(): lax.ppermute(tops_out[k], 'dev', [(s, (s // inner ^ k) * inner + s % inne...  4.45 us
    ppermute x3, waiting for transfers between devices, local(): lax.ppermute(block, 'dev', [(s, s // inner * inner + (s % inner ^ j)) for...  4.42 us
    ppermute x1, starting transfers between devices, local(): lax.ppermute(own, 'rhs', [(i, (i + shift) % rhs_count) for i in range(rhs...  2.97 us
    pallas_call x1, Pallas kernels, pack(): pl.pallas_call(lambda *refs: pack_kernel(per_dest, outer, inner, *refs),...  2.05 us
    ppermute x3, starting transfers between devices, local(): lax.ppermute(block, 'dev', [(s, s // inner * inner + (s % inner ^ j)) for...  1.91 us
    unnamed x34, local copies, waits for them, and re-layouts  1.33 us
  transfers between devices with their start and end apart: 8, of which 3 were waited for; matrix products, arithmetic and copies ran while one was open for 3% of the time, Pallas kernels for 14%

profile of v5, /device:TPU:0, one launch (start us, length us, event | category | flops | bytes accessed | tf_op | source)
XLA Modules:
  0.0 35.3 jit_solution(11164597165629069279)
XLA Ops:
  0.0 0.7 %multiply_bitcast_fusion = f32[1,32]{1,0:T(1,128)S(1)} fusion(f32[32]{0:T(128)} %param.15), kind=kLoop, calls=%fused_computation.23 | loop fusion | flops 32 | bytes 256 | tf_op jit(solution)/shard_map/mul | solution.py:620
  0.7 0.6 %copy-done.11 = f32[1,32]{1,0:T(1,128)} copy-done((f32[1,32]{1,0:T(1,128)}, f32[1,32]{1,0:T(1,128)S(1)}, u32[]{:S(2)}) %copy-start.11) | copy-done | bytes 152
  1.3 0.6 %pad_maximum_fusion.4 = f32[3,32]{1,0:T(4,128)} fusion(f32[1,32]{1,0:T(1,128)S(1)} %multiply_bitcast_fusion, f32[2,32]{1,0:T(2,128)S(1)} %convert_bitcast_fusion), kind=kLoop, calls=%fused_computation.20 | loop fusion | flops 96 | bytes 768 | tf_op jit(solution)/shard_map/concatenate | solution.py:617
  1.8 3.0 %collective-permute-start.6 = (f32[3,32]{1,0:T(4,128)}, f32[3,32]{1,0:T(4,128)}, u32[]{:S(2)}, u32[]{:S(2)}) collective-permute-start(f32[3,32]{1,0:T(4,128)} %pad_maximum_fusion.4), channel_id=1, source_target_pairs={{0,1},{1,0},{2,3},{3,2},{4,5},{5,4},{6,7},{7,6},{8,9},{9,8},{10,11... | collective-permute-start | bytes 1160 | tf_op jit(solution)/shard_map/ppermute | solution.py:627
  4.8 2.0 %pack.1 = (f32[16,3,8,128]{3,2,1,0:T(8,128)}, f32[4,5,8,128]{3,2,1,0:T(8,128)}, f32[4,5,8,128]{3,2,1,0:T(8,128)}, f32[4,5,8,128]{3,2,1,0:T(8,128)}, f32[4,5,8,128]{3,2,1,0:T(8,128)}) custom-call(f32[8,2,16,256]{3,2,1,0:T(8,128)} %refs_0_.1, f32[8,1,64,128]{3,2,1,0:T(8,128)} %refs_1_.1), custom_call_target="tpu_custom_call" | custom-call | tf_op jit(solution)/shard_map/pack/pallas_call | solution.py:138
  6.9 6.1 %all-to-all-start = ((f32[16,3,8,128]{3,2,1,0:T(8,128)}), f32[16,3,8,128]{3,2,1,0:T(8,128)S(1)}, u32[]{:S(2)}, u32[]{:S(2)}) async-start(f32[16,3,8,128]{3,2,1,0:T(8,128)} %get-tuple-element.19), calls=%async_computation | async-start | bytes 393216 | tf_op jit(solution)/shard_map/all_to_all | solution.py:600
  13.0 2.0 %collective-permute-start = (f32[4,5,8,128]{3,2,1,0:T(8,128)S(1)}, f32[4,5,8,128]{3,2,1,0:T(8,128)S(1)}, u32[]{:S(2)}, u32[]{:S(2)}) collective-permute-start(f32[4,5,8,128]{3,2,1,0:T(8,128)S(1)} %copy-done.16), channel_id=1, source_target_pairs={{0,8},{2,10},{4,12},{6,14},{8,0},{10,2},{12,4},{14,6},{16,24},{18,... | collective-permute-start | bytes 245768 | tf_op jit(solution)/shard_map/ppermute | solution.py:595
  15.0 2.4 %collective-permute-start.1 = (f32[4,5,8,128]{3,2,1,0:T(8,128)S(1)}, f32[4,5,8,128]{3,2,1,0:T(8,128)S(1)}, u32[]{:S(2)}, u32[]{:S(2)}) collective-permute-start(f32[4,5,8,128]{3,2,1,0:T(8,128)S(1)} %copy-done.15), channel_id=1, source_target_pairs={{0,16},{2,18},{4,20},{6,22},{8,24},{10,26},{12,28},{14,30},{16,0},... | collective-permute-start | bytes 245768 | tf_op jit(solution)/shard_map/ppermute | solution.py:595
  17.4 0.1 collective-permute-start.2
  17.5 0.1 pad.3.clone
  17.6 0.6 %copy-done.6 = f32[64,3]{0,1:T(4,128)S(1)} copy-done((f32[64,3]{0,1:T(4,128)S(1)}, f32[64,3]{0,1:T(4,128)}, u32[]{:S(2)}) %copy-start.6) | copy-done | bytes 792
  18.3 0.0 copy-done.5
  18.3 1.2 %tables.1 = (f32[96,8,128]{2,1,0:T(8,128)S(1)}, f32[48,8,128]{2,1,0:T(8,128)S(1)}, bf16[256,256]{1,0:T(8,128)(2,1)S(1)}, bf16[256,256]{1,0:T(8,128)(2,1)S(1)}, f...) custom-call(s32[4,16]{1,0:T(4,128)S(1)} %bitcast.12, ...), custom_call_target="tpu_custom_call" | custom-call | tf_op jit(solution)/shard_map/tables/pallas_call | solution.py:310
  19.6 0.7 %maximum_maximum_fusion.refs_1_ = f32[3,128]{1,0:T(4,128)S(1)} fusion(f32[3,32]{1,0:T(4,128)} %collective-permute-done.6, f32[1,32]{1,0:T(1,128)S(1)} %copy-done.12, f32[2,32]{1,0:T(2,128)S(1)} %copy-done.10, f32[128]{0:T(128)S(1)} %pad.3.clone), kind=kLoop, calls=%fused_computation.21 | loop fusion | flops 1152 | bytes 2816 | tf_op jit(solution)/shard_map/concatenate | solution.py:629
  20.3 1.0 %lattice.1.refs_4_ = f32[32,8,8,128]{3,2,1,0:T(8,128)S(1)} custom-call(f32[2,8,128]{2,1,0:T(8,128)S(1)} %get-tuple-element.24.refs_0_, f32[3,128]{1,0:T(4,128)S(1)} %maximum_maximum_fusion.refs_1_, f32[2,32,128]{2,1,0:T(8,128)S(1)} %get-tuple-element.25.refs_2_, f32[8,32,128]{2,1,0:T(8,128)S(1)} %get-tuple-element.26.refs_3_), custom_call_target="tpu_custom_call" | custom-call | tf_op jit(solution)/shard_map/lattice/pallas_call | solution.py:335
  21.3 0.0 collective-permute-done
  21.4 5.7 %collective-permute-done.1 = f32[4,5,8,128]{3,2,1,0:T(8,128)S(1)} collective-permute-done((f32[4,5,8,128]{3,2,1,0:T(8,128)S(1)}, f32[4,5,8,128]{3,2,1,0:T(8,128)S(1)}, u32[]{:S(2)}, u32[]{:S(2)}) %collective-permute-start.1) | collective-permute-done | bytes 81952 | tf_op jit(solution)/shard_map/ppermute | solution.py:595
  27.1 0.1 collective-permute-start.3
  27.2 1.5 %collective-permute-start.4 = (f32[4,5,8,128]{3,2,1,0:T(8,128)S(1)}, f32[4,5,8,128]{3,2,1,0:T(8,128)S(1)}, u32[]{:S(2)}, u32[]{:S(2)}) collective-permute-start(f32[4,5,8,128]{3,2,1,0:T(8,128)S(1)} %pad_maximum_fusion.2), channel_id=1, source_target_pairs={{0,4},{2,6},{4,0},{6,2},{8,12},{10,14},{12,8},{14,10},{16,20},{18,... | collective-permute-start | bytes 245768 | tf_op jit(solution)/shard_map/ppermute | solution.py:610
  28.7 0.3 collective-permute-start.5
  29.1 3.3 %collective-permute-done.4.refs_2_ = f32[4,5,8,128]{3,2,1,0:T(8,128)S(1)} collective-permute-done((f32[4,5,8,128]{3,2,1,0:T(8,128)S(1)}, f32[4,5,8,128]{3,2,1,0:T(8,128)S(1)}, u32[]{:S(2)}, u32[]{:S(2)}) %collective-permute-start.4) | collective-permute-done | bytes 81952 | tf_op jit(solution)/shard_map/ppermute | solution.py:610
  32.3 1.1 %collective-permute-done.5.refs_3_ = f32[4,5,8,128]{3,2,1,0:T(8,128)S(1)} collective-permute-done((f32[4,5,8,128]{3,2,1,0:T(8,128)S(1)}, f32[4,5,8,128]{3,2,1,0:T(8,128)S(1)}, u32[]{:S(2)}, u32[]{:S(2)}) %collective-permute-start.5) | collective-permute-done | bytes 81952 | tf_op jit(solution)/shard_map/ppermute | solution.py:610
  33.5 0.5 %upper.1.refs_1_ = f32[16,4,8,128]{3,2,1,0:T(8,128)S(1)} custom-call(f32[4,5,8,128]{3,2,1,0:T(8,128)S(1)} %pad_maximum_fusion.refs_0_, f32[4,5,8,128]{3,2,1,0:T(8,128)S(1)} %collective-permute-done.3.refs_1_, f32[4,5,8,128]{3,2,1,0:T(8,128)S(1)} %collective-permute-done.4.refs_2_, f32[4,5,8,128]{3,2,1,0:T(8,128)S(1)} %collective-permute-done.5.refs_3_, ...), custom_call_target="tpu_custom_call" | custom-call | tf_op jit(solution)/shard_map/upper/pallas_call | solution.py:531
  34.0 1.3 %lower.1 = f32[8,16,512]{2,1,0:T(8,128)} custom-call(f32[16,3,8,128]{3,2,1,0:T(8,128)S(1)} %all-to-all-done.refs_0_, f32[16,4,8,128]{3,2,1,0:T(8,128)S(1)} %upper.1.refs_1_, f32[48,8,128]{2,1,0:T(8,128)S(1)} %get-tuple-element.29.refs_2_, bf16[256,256]{1,0:T(8,128)(2,1)S(1)} %get-tuple-element.30.refs_3_, f32[64,128]{1,0:T(8,128)S(1)} %get-tuple-element.31.refs_4_, ...), custom_call_target="tpu_custom_call" | custom-call | tf_op jit(solution)/shard_map/lower/pallas_call | solution.py:550
  (45 shorter events, 0.2 us)
Async XLA Ops:
  0.0 0.7 %copy-start.13 = (s32[32,2]{0,1:T(2,128)S(1)}, s32[32,2]{0,1:T(2,128)}, u32[]{:S(2)}) copy-start(s32[32,2]{0,1:T(2,128)} %param.14) | copy-start | bytes 772
  1.3 0.6 %copy-start.9 = (f32[2,32]{1,0:T(2,128)}, f32[2,32]{1,0:T(2,128)S(1)}, u32[]{:S(2)}) copy-start(f32[2,32]{1,0:T(2,128)S(1)} %convert_bitcast_fusion) | copy-start | bytes 772
  1.8 17.7 %collective-permute-start.6 = (f32[3,32]{1,0:T(4,128)}, f32[3,32]{1,0:T(4,128)}, u32[]{:S(2)}, u32[]{:S(2)}) collective-permute-start(f32[3,32]{1,0:T(4,128)} %pad_maximum_fusion.4), channel_id=1, source_target_pairs={{0,1},{1,0},{2,3},{3,2},{4,5},{5,4},{6,7},{7,6},{8,9},{9,8},{10,11... | collective-permute-start | bytes 1160 | tf_op jit(solution)/shard_map/ppermute | solution.py:627
  6.9 6.1 %copy-start.16 = (f32[4,5,8,128]{3,2,1,0:T(8,128)S(1)}, f32[4,5,8,128]{3,2,1,0:T(8,128)}, u32[]{:S(2)}) copy-start(f32[4,5,8,128]{3,2,1,0:T(8,128)} %get-tuple-element.21) | copy-start | bytes 245764
  6.9 8.1 %copy-start.15 = (f32[4,5,8,128]{3,2,1,0:T(8,128)S(1)}, f32[4,5,8,128]{3,2,1,0:T(8,128)}, u32[]{:S(2)}) copy-start(f32[4,5,8,128]{3,2,1,0:T(8,128)} %get-tuple-element.22) | copy-start | bytes 245764
  6.9 10.5 %copy-start.14 = (f32[4,5,8,128]{3,2,1,0:T(8,128)S(1)}, f32[4,5,8,128]{3,2,1,0:T(8,128)}, u32[]{:S(2)}) copy-start(f32[4,5,8,128]{3,2,1,0:T(8,128)} %get-tuple-element.23) | copy-start | bytes 245764
  6.9 10.7 %copy-start.8 = (f32[4,5,8,128]{3,2,1,0:T(8,128)S(1)}, f32[4,5,8,128]{3,2,1,0:T(8,128)}, u32[]{:S(2)}) copy-start(f32[4,5,8,128]{3,2,1,0:T(8,128)} %get-tuple-element.20) | copy-start | bytes 245764
  6.9 27.1 %all-to-all-start = ((f32[16,3,8,128]{3,2,1,0:T(8,128)}), f32[16,3,8,128]{3,2,1,0:T(8,128)S(1)}, u32[]{:S(2)}, u32[]{:S(2)}) async-start(f32[16,3,8,128]{3,2,1,0:T(8,128)} %get-tuple-element.19), calls=%async_computation | async-start | bytes 393216 | tf_op jit(solution)/shard_map/all_to_all | solution.py:600
  13.0 8.4 %collective-permute-start = (f32[4,5,8,128]{3,2,1,0:T(8,128)S(1)}, f32[4,5,8,128]{3,2,1,0:T(8,128)S(1)}, u32[]{:S(2)}, u32[]{:S(2)}) collective-permute-start(f32[4,5,8,128]{3,2,1,0:T(8,128)S(1)} %copy-done.16), channel_id=1, source_target_pairs={{0,8},{2,10},{4,12},{6,14},{8,0},{10,2},{12,4},{14,6},{16,24},{18,... | collective-permute-start | bytes 245768 | tf_op jit(solution)/shard_map/ppermute | solution.py:595
  15.0 12.0 %collective-permute-start.1 = (f32[4,5,8,128]{3,2,1,0:T(8,128)S(1)}, f32[4,5,8,128]{3,2,1,0:T(8,128)S(1)}, u32[]{:S(2)}, u32[]{:S(2)}) collective-permute-start(f32[4,5,8,128]{3,2,1,0:T(8,128)S(1)} %copy-done.15), channel_id=1, source_target_pairs={{0,16},{2,18},{4,20},{6,22},{8,24},{10,26},{12,28},{14,30},{16,0},... | collective-permute-start | bytes 245768 | tf_op jit(solution)/shard_map/ppermute | solution.py:595
  17.4 9.7 %collective-permute-start.2 = (f32[4,5,8,128]{3,2,1,0:T(8,128)S(1)}, f32[4,5,8,128]{3,2,1,0:T(8,128)S(1)}, u32[]{:S(2)}, u32[]{:S(2)}) collective-permute-start(f32[4,5,8,128]{3,2,1,0:T(8,128)S(1)} %copy-done.14), channel_id=1, source_target_pairs={{0,24},{2,26},{4,28},{6,30},{8,16},{10,18},{12,20},{14,22},{16,8},... | collective-permute-start | bytes 245768 | tf_op jit(solution)/shard_map/ppermute | solution.py:595
  17.5 0.7 %copy-start.6 = (f32[64,3]{0,1:T(4,128)S(1)}, f32[64,3]{0,1:T(4,128)}, u32[]{:S(2)}) copy-start(f32[64,3]{0,1:T(4,128)} %param.22) | copy-start | bytes 2308
  17.6 0.7 %copy-start.2 = (f32[16,3]{0,1:T(4,128)S(1)}, f32[16,3]{0,1:T(4,128)}, u32[]{:S(2)}) copy-start(f32[16,3]{0,1:T(4,128)} %param.23) | copy-start | bytes 580
  17.6 0.7 %copy-start.3 = (s32[128,3]{0,1:T(4,128)S(1)}, s32[128,3]{0,1:T(4,128)}, u32[]{:S(2)}) copy-start(s32[128,3]{0,1:T(4,128)} %param.18) | copy-start | bytes 4612
  17.6 0.7 %copy-start.4 = (f32[128,3]{0,1:T(4,128)S(1)}, f32[128,3]{0,1:T(4,128)}, u32[]{:S(2)}) copy-start(f32[128,3]{0,1:T(4,128)} %param.19) | copy-start | bytes 4612
  17.6 0.7 %copy-start.5 = (s32[64,3]{0,1:T(4,128)S(1)}, s32[64,3]{0,1:T(4,128)}, u32[]{:S(2)}) copy-start(s32[64,3]{0,1:T(4,128)} %param.21) | copy-start | bytes 2308
  17.6 0.7 %copy-start.1 = (f32[32,3]{0,1:T(4,128)S(1)}, f32[32,3]{0,1:T(4,128)}, u32[]{:S(2)}) copy-start(f32[32,3]{0,1:T(4,128)} %param.20) | copy-start | bytes 1156
  17.6 0.7 %copy-start = (s32[16,4]{0,1:T(4,128)S(1)}, s32[16,4]{0,1:T(4,128)}, u32[]{:S(2)}) copy-start(s32[16,4]{0,1:T(4,128)} %param.17) | copy-start | bytes 772
  17.6 0.7 %copy-start.7 = (f32[16,2]{0,1:T(2,128)S(1)}, f32[16,2]{0,1:T(2,128)}, u32[]{:S(2)}) copy-start(f32[16,2]{0,1:T(2,128)} %param.16) | copy-start | bytes 388
  18.3 1.2 %copy-start.10 = (f32[2,32]{1,0:T(2,128)S(1)}, f32[2,32]{1,0:T(2,128)}, u32[]{:S(2)}) copy-start(f32[2,32]{1,0:T(2,128)} %copy-done.9) | copy-start | bytes 772
  18.3 1.2 %copy-start.12 = (f32[1,32]{1,0:T(1,128)S(1)}, f32[1,32]{1,0:T(1,128)}, u32[]{:S(2)}) copy-start(f32[1,32]{1,0:T(1,128)} %copy-done.11) | copy-start | bytes 388
  27.1 2.0 %collective-permute-start.3 = (f32[4,5,8,128]{3,2,1,0:T(8,128)S(1)}, f32[4,5,8,128]{3,2,1,0:T(8,128)S(1)}, u32[]{:S(2)}, u32[]{:S(2)}) collective-permute-start(f32[4,5,8,128]{3,2,1,0:T(8,128)S(1)} %pad_maximum_fusion.1), channel_id=1, source_target_pairs={{0,2},{2,0},{4,6},{6,4},{8,10},{10,8},{12,14},{14,12},{16,18},{18,... | collective-permute-start | bytes 245768 | tf_op jit(solution)/shard_map/ppermute | solution.py:610
  27.2 5.1 %collective-permute-start.4 = (f32[4,5,8,128]{3,2,1,0:T(8,128)S(1)}, f32[4,5,8,128]{3,2,1,0:T(8,128)S(1)}, u32[]{:S(2)}, u32[]{:S(2)}) collective-permute-start(f32[4,5,8,128]{3,2,1,0:T(8,128)S(1)} %pad_maximum_fusion.2), channel_id=1, source_target_pairs={{0,4},{2,6},{4,0},{6,2},{8,12},{10,14},{12,8},{14,10},{16,20},{18,... | collective-permute-start | bytes 245768 | tf_op jit(solution)/shard_map/ppermute | solution.py:610
  28.7 4.7 %collective-permute-start.5 = (f32[4,5,8,128]{3,2,1,0:T(8,128)S(1)}, f32[4,5,8,128]{3,2,1,0:T(8,128)S(1)}, u32[]{:S(2)}, u32[]{:S(2)}) collective-permute-start(f32[4,5,8,128]{3,2,1,0:T(8,128)S(1)} %pad_maximum_fusion.3), channel_id=1, source_target_pairs={{0,6},{2,4},{4,2},{6,0},{8,14},{10,12},{12,10},{14,8},{16,22},{18,... | collective-permute-start | bytes 245768 | tf_op jit(solution)/shard_map/ppermute | solution.py:610
  (1 other events, 0.6 us)

commit v6 on v5

--- a/solution.py
+++ b/solution.py
@@ -62,9 +62,9 @@
     return dev_count // inner, inner
 
 
-def pack_kernel(per_dest, outer, inner, a_hbm, l_hbm, mid_hbm, *refs):
+def pack_kernel(per_dest, outer, inner, scale, a_hbm, l_hbm, off_hbm, wt_hbm, mid_hbm, *refs):
     top_hbm = refs[:outer]
-    re_ref, im_ref, mid_ref, top_out, mid_out, sems = refs[outer:]
+    own_hbm, re_ref, im_ref, mid_ref, top_out, mid_out, off_ref, wt_ref, own_ref, sems = refs[outer:]
     exc, phi_local, boxes, _ = re_ref.shape
     mid_phi, _ = mid_ref.shape[1:3]
     plane = lax.axis_index("dev") // inner
@@ -72,6 +72,8 @@
         pltpu.make_async_copy(a_hbm.at[:, :, :, pl.ds(0, LANES)], re_ref, sems.at[0]),
         pltpu.make_async_copy(a_hbm.at[:, :, :, pl.ds(LANES, LANES)], im_ref, sems.at[1]),
         pltpu.make_async_copy(l_hbm, mid_ref, sems.at[2]),
+        pltpu.make_async_copy(off_hbm, off_ref, sems.at[3]),
+        pltpu.make_async_copy(wt_hbm, wt_ref, sems.at[4]),
     ]
     for copy in arrive:
         copy.start()
@@ -90,7 +92,7 @@
         loop(width // group, one)
 
     def send(source, target):
-        copy = pltpu.make_async_copy(source, target, sems.at[3 + len(leave)])
+        copy = pltpu.make_async_copy(source, target, sems.at[5 + len(leave)])
         copy.start()
         leave.append(copy)
 
@@ -106,6 +108,11 @@
                         split.at[pl.ds((plane ^ other) * inner, inner), box],
                         top_hbm[other].at[:, box * phi_local * 2 + k],
                     )
+    arrive[3].wait()
+    arrive[4].wait()
+    own_ref[0:2, :] = off_ref[...].astype(jnp.float32)
+    own_ref[2:3, :] = wt_ref[...] * scale
+    send(own_ref, own_hbm)
     arrive[2].wait()
     for phi in range(mid_phi):
         scatter(mid_ref.at[:, phi], mid_out.at[phi])
@@ -126,7 +133,7 @@
         copy.wait()
 
 
-def pack(top_adj, level1_adj, dev_count):
+def pack(top_adj, level1_adj, offsets, weights, scale, dev_count):
     exc, phi_local, boxes, _ = top_adj.shape
     mid_phi, mids = level1_adj.shape[1:3]
     per_dest = boxes // dev_count
@@ -136,22 +143,26 @@
     f32 = jnp.float32
     hbm = pl.BlockSpec(memory_space=pltpu.HBM)
     return pl.pallas_call(
-        lambda *refs: pack_kernel(per_dest, outer, inner, *refs),
-        in_specs=[hbm] * 2,
-        out_specs=[hbm] * (1 + outer),
+        lambda *refs: pack_kernel(per_dest, outer, inner, scale, *refs),
+        in_specs=[hbm] * 4,
+        out_specs=[hbm] * (2 + outer),
         out_shape=[jax.ShapeDtypeStruct((dev_count, rest, exc, LANES), f32)]
-        + [jax.ShapeDtypeStruct((inner, tops, exc, LANES), f32)] * outer,
+        + [jax.ShapeDtypeStruct((inner, tops, exc, LANES), f32)] * outer
+        + [jax.ShapeDtypeStruct((3, offsets.shape[1]), f32)],
         scratch_shapes=[
             pltpu.VMEM((exc, phi_local, boxes, LANES), f32),
             pltpu.VMEM((exc, phi_local, boxes, LANES), f32),
             pltpu.VMEM((exc, mid_phi, mids, LANES), f32),
             pltpu.VMEM((phi_local * 2, boxes, exc, LANES), f32),
             pltpu.VMEM((mid_phi, mids, exc, LANES), f32),
-            pltpu.SemaphoreType.DMA((3 + outer * tops + rest,)),
+            pltpu.VMEM(offsets.shape, jnp.int32),
+            pltpu.VMEM(weights.shape, f32),
+            pltpu.VMEM((3, offsets.shape[1]), f32),
+            pltpu.SemaphoreType.DMA((6 + outer * tops + rest,)),
         ],
         compiler_params=pltpu.CompilerParams(vmem_limit_bytes=67043328),
         name="pack",
-    )(top_adj, level1_adj)
+    )(top_adj, level1_adj, offsets, weights)
 
 
 def theta_block(index_ref, weight_ref, columns):
@@ -589,7 +600,14 @@
 
     outer, inner = factors(dev_count)
     me = lax.axis_index("dev")
-    mids_out, *tops_out = pack(top_adj, level1_adj, dev_count)
+    mids_out, *tops_out, own = pack(
+        top_adj,
+        level1_adj,
+        image_offsets.T,
+        image_weights[None],
+        float(images) ** (-0.5),
+        dev_count,
+    )
     planes = {0: tops_out[0]}
     for k in order(outer):
         planes[k] = lax.ppermute(
@@ -614,13 +632,6 @@
             )
         parts.append(block)
 
-    own = jnp.concatenate(
-        [
-            image_offsets.T.astype(jnp.float32),
-            image_weights[None] * float(images) ** (-0.5),
-        ],
-        axis=0,
-    )
     images_of = [own]
     for shift in range(1, rhs_count):
         images_of.append(

time: 35.6 us -> 32.3 us (0.907)
  other arithmetic: 2.04 us -> 0.11 us
  waiting for transfers between devices: 10.1 us -> 9.3 us
  local copies, waits for them, and re-layouts: 1.44 us -> 0.87 us
    all_to_all x1, starting transfers between devices: 6.08 us -> 7.56 us  [local(): lax.all_to_all(mids_out, 'dev', split_axis=0, concat_axis=0, tiled=True)]
    ppermute x1, starting transfers between devices: 2.97 us -> 1.56 us  [local(): lax.ppermute(own, 'rhs', [(i, (i + shift) % rhs_count) for i in range(rhs...]
    ppermute x3, waiting for transfers between devices: 5.7 us -> 4.87 us  [local(): lax.ppermute(tops_out[k], 'dev', [(s, (s // inner ^ k) * inner + s % inne...]
    mul x1 -> x0, other arithmetic: 0.67 us -> none  [local(): image_weights[None] * float(images) ** (-0.5)]
    concatenate x1, other arithmetic: 0.74 us -> 0.08 us  [local(): jnp.concatenate(images_of + [jnp.zeros((3, LANES - images), jnp.float32)]...]
    concatenate x1 -> x0, other arithmetic: 0.59 us -> none  [local(): jnp.concatenate([image_offsets.T.astype(jnp.float32), image_weights[None]...]
    unnamed x34 -> x26, local copies, waits for them, and re-layouts: 1.33 us -> 0.74 us
  transfers between devices with their start and end apart: 8 -> 8, of which waited for: 3 -> 3; matrix products, arithmetic and copies ran while one was open for 3% -> 1% of each run, Pallas kernels for 14% -> 9%
where the time goes in v6:
time: 32.3 us; the launch traced here: 32 us
  starting transfers between devices  15.4 us (48%)
  waiting for transfers between devices  9.3 us (29%)
  Pallas kernels  6.12 us (19%)
  local copies, waits for them, and re-layouts  0.87 us (3%)
    all_to_all x1, starting transfers between devices, local(): lax.all_to_all(mids_out, 'dev', split_axis=0, concat_axis=0, tiled=True)  7.56 us
    ppermute x3, waiting for transfers between devices, local(): lax.ppermute(tops_out[k], 'dev', [(s, (s // inner ^ k) * inner + s % inne...  4.87 us
    ppermute x3, waiting for transfers between devices, local(): lax.ppermute(block, 'dev', [(s, s // inner * inner + (s % inner ^ j)) for...  4.42 us
    ppermute x3, starting transfers between devices, local(): lax.ppermute(tops_out[k], 'dev', [(s, (s // inner ^ k) * inner + s % inne...  4.39 us
    pallas_call x1, Pallas kernels, pack(): pl.pallas_call(lambda *refs: pack_kernel(per_dest, outer, inner, scale, *...  2.07 us
    ppermute x3, starting transfers between devices, local(): lax.ppermute(block, 'dev', [(s, s // inner * inner + (s % inner ^ j)) for...  1.91 us
    ppermute x1, starting transfers between devices, local(): lax.ppermute(own, 'rhs', [(i, (i + shift) % rhs_count) for i in range(rhs...  1.56 us
    pallas_call x1, Pallas kernels, lower(): pl.pallas_call(lambda *refs: lower_kernel(sizes, *refs), in_specs=[VMEM]...  1.31 us
  transfers between devices with their start and end apart: 8, of which 3 were waited for; matrix products, arithmetic and copies ran while one was open for 1% of the time, Pallas kernels for 9%

profile of v6, /device:TPU:0, one launch (start us, length us, event | category | flops | bytes accessed | tf_op | source)
XLA Modules:
  0.0 32.0 jit_solution(8146209335360425826)
XLA Ops:
  0.0 2.1 %pack.1 = (f32[16,3,8,128]{3,2,1,0:T(8,128)}, f32[4,5,8,128]{3,2,1,0:T(8,128)}, f32[4,5,8,128]{3,2,1,0:T(8,128)}, f32[4,5,8,128]{3,2,1,0:T(8,128)}, f32[4,5,8,128]{3,2,1,0:T(8,128)}, /*index=5*/f32[3,32]{1,0:T(4,128)}) custom-call(f32[8,2,16,256]{3,2,1,0:T(8,128)} %refs_0_.1, f32[8,1,64,128]{3,2,1,0:T(8,128)} %refs_1_.1, s32[2,32]{1,0:T(2,128)} %bitcast.18, ...), custom_call_target="tpu_custom_call" | custom-call | tf_op jit(solution)/shard_map/pack/pallas_call | solution.py:145
  2.1 7.6 %all-to-all-start = ((f32[16,3,8,128]{3,2,1,0:T(8,128)}), f32[16,3,8,128]{3,2,1,0:T(8,128)S(1)}, u32[]{:S(2)}, u32[]{:S(2)}) async-start(f32[16,3,8,128]{3,2,1,0:T(8,128)} %get-tuple-element.20), calls=%async_computation | async-start | bytes 393216 | tf_op jit(solution)/shard_map/all_to_all | solution.py:618
  9.7 1.6 %collective-permute-start.6 = (f32[3,32]{1,0:T(4,128)S(1)}, f32[3,32]{1,0:T(4,128)S(1)}, u32[]{:S(2)}, u32[]{:S(2)}) collective-permute-start(f32[3,32]{1,0:T(4,128)S(1)} %copy-done.9), channel_id=1, source_target_pairs={{0,1},{1,0},{2,3},{3,2},{4,5},{5,4},{6,7},{7,6},{8,9},{9,8},{10,11... | collective-permute-start | bytes 1160 | tf_op jit(solution)/shard_map/ppermute | solution.py:638
  11.3 1.9 %collective-permute-start = (f32[4,5,8,128]{3,2,1,0:T(8,128)S(1)}, f32[4,5,8,128]{3,2,1,0:T(8,128)S(1)}, u32[]{:S(2)}, u32[]{:S(2)}) collective-permute-start(f32[4,5,8,128]{3,2,1,0:T(8,128)S(1)} %copy-done.12), channel_id=1, source_target_pairs={{0,8},{2,10},{4,12},{6,14},{8,0},{10,2},{12,4},{14,6},{16,24},{18,... | collective-permute-start | bytes 245768 | tf_op jit(solution)/shard_map/ppermute | solution.py:613
  13.2 2.4 %collective-permute-start.1 = (f32[4,5,8,128]{3,2,1,0:T(8,128)S(1)}, f32[4,5,8,128]{3,2,1,0:T(8,128)S(1)}, u32[]{:S(2)}, u32[]{:S(2)}) collective-permute-start(f32[4,5,8,128]{3,2,1,0:T(8,128)S(1)} %copy-done.11), channel_id=1, source_target_pairs={{0,16},{2,18},{4,20},{6,22},{8,24},{10,26},{12,28},{14,30},{16,0},... | collective-permute-start | bytes 245768 | tf_op jit(solution)/shard_map/ppermute | solution.py:613
  15.6 0.1 collective-permute-start.2
  15.7 0.1 pad.2.clone
  15.8 0.6 %copy-done.6 = f32[64,3]{0,1:T(4,128)S(1)} copy-done((f32[64,3]{0,1:T(4,128)S(1)}, f32[64,3]{0,1:T(4,128)}, u32[]{:S(2)}) %copy-start.6) | copy-done | bytes 792
  16.4 0.0 copy-done.2
  16.4 0.0 copy-done.3
  16.5 0.0 copy-done.4
  16.5 0.0 copy-done.5
  16.5 0.0 copy-done.1
  16.5 1.2 %tables.1 = (f32[96,8,128]{2,1,0:T(8,128)S(1)}, f32[48,8,128]{2,1,0:T(8,128)S(1)}, bf16[256,256]{1,0:T(8,128)(2,1)S(1)}, bf16[256,256]{1,0:T(8,128)(2,1)S(1)}, f...) custom-call(s32[4,16]{1,0:T(4,128)S(1)} %bitcast.10, ...), custom_call_target="tpu_custom_call" | custom-call | tf_op jit(solution)/shard_map/tables/pallas_call | solution.py:321
  17.7 0.1 maximum_maximum_fusion.refs_1_
  17.8 1.0 %lattice.1.refs_4_ = f32[32,8,8,128]{3,2,1,0:T(8,128)S(1)} custom-call(f32[2,8,128]{2,1,0:T(8,128)S(1)} %get-tuple-element.25.refs_0_, f32[3,128]{1,0:T(4,128)S(1)} %maximum_maximum_fusion.refs_1_, f32[2,32,128]{2,1,0:T(8,128)S(1)} %get-tuple-element.27.refs_2_, f32[8,32,128]{2,1,0:T(8,128)S(1)} %get-tuple-element.28.refs_3_), custom_call_target="tpu_custom_call" | custom-call | tf_op jit(solution)/shard_map/lattice/pallas_call | solution.py:346
  18.9 4.9 %collective-permute-done.1 = f32[4,5,8,128]{3,2,1,0:T(8,128)S(1)} collective-permute-done((f32[4,5,8,128]{3,2,1,0:T(8,128)S(1)}, f32[4,5,8,128]{3,2,1,0:T(8,128)S(1)}, u32[]{:S(2)}, u32[]{:S(2)}) %collective-permute-start.1) | collective-permute-done | bytes 81952 | tf_op jit(solution)/shard_map/ppermute | solution.py:613
  23.8 0.1 collective-permute-start.3
  23.9 1.5 %collective-permute-start.4 = (f32[4,5,8,128]{3,2,1,0:T(8,128)S(1)}, f32[4,5,8,128]{3,2,1,0:T(8,128)S(1)}, u32[]{:S(2)}, u32[]{:S(2)}) collective-permute-start(f32[4,5,8,128]{3,2,1,0:T(8,128)S(1)} %pad_maximum_fusion.2), channel_id=1, source_target_pairs={{0,4},{2,6},{4,0},{6,2},{8,12},{10,14},{12,8},{14,10},{16,20},{18,... | collective-permute-start | bytes 245768 | tf_op jit(solution)/shard_map/ppermute | solution.py:628
  25.4 0.3 collective-permute-start.5
  25.8 3.3 %collective-permute-done.4.refs_2_ = f32[4,5,8,128]{3,2,1,0:T(8,128)S(1)} collective-permute-done((f32[4,5,8,128]{3,2,1,0:T(8,128)S(1)}, f32[4,5,8,128]{3,2,1,0:T(8,128)S(1)}, u32[]{:S(2)}, u32[]{:S(2)}) %collective-permute-start.4) | collective-permute-done | bytes 81952 | tf_op jit(solution)/shard_map/ppermute | solution.py:628
  29.0 1.1 %collective-permute-done.5.refs_3_ = f32[4,5,8,128]{3,2,1,0:T(8,128)S(1)} collective-permute-done((f32[4,5,8,128]{3,2,1,0:T(8,128)S(1)}, f32[4,5,8,128]{3,2,1,0:T(8,128)S(1)}, u32[]{:S(2)}, u32[]{:S(2)}) %collective-permute-start.5) | collective-permute-done | bytes 81952 | tf_op jit(solution)/shard_map/ppermute | solution.py:628
  30.2 0.5 %upper.1.refs_1_ = f32[16,4,8,128]{3,2,1,0:T(8,128)S(1)} custom-call(f32[4,5,8,128]{3,2,1,0:T(8,128)S(1)} %pad_maximum_fusion.refs_0_, f32[4,5,8,128]{3,2,1,0:T(8,128)S(1)} %collective-permute-done.3.refs_1_, f32[4,5,8,128]{3,2,1,0:T(8,128)S(1)} %collective-permute-done.4.refs_2_, f32[4,5,8,128]{3,2,1,0:T(8,128)S(1)} %collective-permute-done.5.refs_3_, ...), custom_call_target="tpu_custom_call" | custom-call | tf_op jit(solution)/shard_map/upper/pallas_call | solution.py:542
  30.7 1.3 %lower.1 = f32[8,16,512]{2,1,0:T(8,128)} custom-call(f32[16,3,8,128]{3,2,1,0:T(8,128)S(1)} %all-to-all-done.refs_0_, f32[16,4,8,128]{3,2,1,0:T(8,128)S(1)} %upper.1.refs_1_, f32[48,8,128]{2,1,0:T(8,128)S(1)} %get-tuple-element.31.refs_2_, bf16[256,256]{1,0:T(8,128)(2,1)S(1)} %get-tuple-element.32.refs_3_, f32[64,128]{1,0:T(8,128)S(1)} %get-tuple-element.33.refs_4_, ...), custom_call_target="tpu_custom_call" | custom-call | tf_op jit(solution)/shard_map/lower/pallas_call | solution.py:561
  (34 shorter events, 0.2 us)
Async XLA Ops:
  2.1 7.6 %copy-start.9 = (f32[3,32]{1,0:T(4,128)S(1)}, f32[3,32]{1,0:T(4,128)}, u32[]{:S(2)}) copy-start(f32[3,32]{1,0:T(4,128)} %get-tuple-element.26) | copy-start | bytes 1156
  2.1 9.2 %copy-start.12 = (f32[4,5,8,128]{3,2,1,0:T(8,128)S(1)}, f32[4,5,8,128]{3,2,1,0:T(8,128)}, u32[]{:S(2)}) copy-start(f32[4,5,8,128]{3,2,1,0:T(8,128)} %get-tuple-element.22) | copy-start | bytes 245764
  2.1 11.1 %copy-start.11 = (f32[4,5,8,128]{3,2,1,0:T(8,128)S(1)}, f32[4,5,8,128]{3,2,1,0:T(8,128)}, u32[]{:S(2)}) copy-start(f32[4,5,8,128]{3,2,1,0:T(8,128)} %get-tuple-element.23) | copy-start | bytes 245764
  2.1 13.4 %copy-start.10 = (f32[4,5,8,128]{3,2,1,0:T(8,128)S(1)}, f32[4,5,8,128]{3,2,1,0:T(8,128)}, u32[]{:S(2)}) copy-start(f32[4,5,8,128]{3,2,1,0:T(8,128)} %get-tuple-element.24) | copy-start | bytes 245764
  2.1 13.6 %copy-start.8 = (f32[4,5,8,128]{3,2,1,0:T(8,128)S(1)}, f32[4,5,8,128]{3,2,1,0:T(8,128)}, u32[]{:S(2)}) copy-start(f32[4,5,8,128]{3,2,1,0:T(8,128)} %get-tuple-element.21) | copy-start | bytes 245764
  2.1 28.6 %all-to-all-start = ((f32[16,3,8,128]{3,2,1,0:T(8,128)}), f32[16,3,8,128]{3,2,1,0:T(8,128)S(1)}, u32[]{:S(2)}, u32[]{:S(2)}) async-start(f32[16,3,8,128]{3,2,1,0:T(8,128)} %get-tuple-element.20), calls=%async_computation | async-start | bytes 393216 | tf_op jit(solution)/shard_map/all_to_all | solution.py:618
  9.7 8.0 %collective-permute-start.6 = (f32[3,32]{1,0:T(4,128)S(1)}, f32[3,32]{1,0:T(4,128)S(1)}, u32[]{:S(2)}, u32[]{:S(2)}) collective-permute-start(f32[3,32]{1,0:T(4,128)S(1)} %copy-done.9), channel_id=1, source_target_pairs={{0,1},{1,0},{2,3},{3,2},{4,5},{5,4},{6,7},{7,6},{8,9},{9,8},{10,11... | collective-permute-start | bytes 1160 | tf_op jit(solution)/shard_map/ppermute | solution.py:638
  11.3 7.6 %collective-permute-start = (f32[4,5,8,128]{3,2,1,0:T(8,128)S(1)}, f32[4,5,8,128]{3,2,1,0:T(8,128)S(1)}, u32[]{:S(2)}, u32[]{:S(2)}) collective-permute-start(f32[4,5,8,128]{3,2,1,0:T(8,128)S(1)} %copy-done.12), channel_id=1, source_target_pairs={{0,8},{2,10},{4,12},{6,14},{8,0},{10,2},{12,4},{14,6},{16,24},{18,... | collective-permute-start | bytes 245768 | tf_op jit(solution)/shard_map/ppermute | solution.py:613
  13.2 10.6 %collective-permute-start.1 = (f32[4,5,8,128]{3,2,1,0:T(8,128)S(1)}, f32[4,5,8,128]{3,2,1,0:T(8,128)S(1)}, u32[]{:S(2)}, u32[]{:S(2)}) collective-permute-start(f32[4,5,8,128]{3,2,1,0:T(8,128)S(1)} %copy-done.11), channel_id=1, source_target_pairs={{0,16},{2,18},{4,20},{6,22},{8,24},{10,26},{12,28},{14,30},{16,0},... | collective-permute-start | bytes 245768 | tf_op jit(solution)/shard_map/ppermute | solution.py:613
  15.6 8.2 %collective-permute-start.2 = (f32[4,5,8,128]{3,2,1,0:T(8,128)S(1)}, f32[4,5,8,128]{3,2,1,0:T(8,128)S(1)}, u32[]{:S(2)}, u32[]{:S(2)}) collective-permute-start(f32[4,5,8,128]{3,2,1,0:T(8,128)S(1)} %copy-done.10), channel_id=1, source_target_pairs={{0,24},{2,26},{4,28},{6,30},{8,16},{10,18},{12,20},{14,22},{16,8},... | collective-permute-start | bytes 245768 | tf_op jit(solution)/shard_map/ppermute | solution.py:613
  15.7 0.7 %copy-start.6 = (f32[64,3]{0,1:T(4,128)S(1)}, f32[64,3]{0,1:T(4,128)}, u32[]{:S(2)}) copy-start(f32[64,3]{0,1:T(4,128)} %param.22) | copy-start | bytes 2308
  15.8 0.7 %copy-start.2 = (f32[16,3]{0,1:T(4,128)S(1)}, f32[16,3]{0,1:T(4,128)}, u32[]{:S(2)}) copy-start(f32[16,3]{0,1:T(4,128)} %param.23) | copy-start | bytes 580
  15.8 0.7 %copy-start.3 = (s32[128,3]{0,1:T(4,128)S(1)}, s32[128,3]{0,1:T(4,128)}, u32[]{:S(2)}) copy-start(s32[128,3]{0,1:T(4,128)} %param.18) | copy-start | bytes 4612
  15.8 0.7 %copy-start.4 = (f32[128,3]{0,1:T(4,128)S(1)}, f32[128,3]{0,1:T(4,128)}, u32[]{:S(2)}) copy-start(f32[128,3]{0,1:T(4,128)} %param.19) | copy-start | bytes 4612
  15.8 0.7 %copy-start.5 = (s32[64,3]{0,1:T(4,128)S(1)}, s32[64,3]{0,1:T(4,128)}, u32[]{:S(2)}) copy-start(s32[64,3]{0,1:T(4,128)} %param.21) | copy-start | bytes 2308
  15.8 0.7 %copy-start.1 = (f32[32,3]{0,1:T(4,128)S(1)}, f32[32,3]{0,1:T(4,128)}, u32[]{:S(2)}) copy-start(f32[32,3]{0,1:T(4,128)} %param.20) | copy-start | bytes 1156
  15.8 0.7 %copy-start = (s32[16,4]{0,1:T(4,128)S(1)}, s32[16,4]{0,1:T(4,128)}, u32[]{:S(2)}) copy-start(s32[16,4]{0,1:T(4,128)} %param.17) | copy-start | bytes 772
  15.8 0.7 %copy-start.7 = (f32[16,2]{0,1:T(2,128)S(1)}, f32[16,2]{0,1:T(2,128)}, u32[]{:S(2)}) copy-start(f32[16,2]{0,1:T(2,128)} %param.16) | copy-start | bytes 388
  23.8 2.0 %collective-permute-start.3 = (f32[4,5,8,128]{3,2,1,0:T(8,128)S(1)}, f32[4,5,8,128]{3,2,1,0:T(8,128)S(1)}, u32[]{:S(2)}, u32[]{:S(2)}) collective-permute-start(f32[4,5,8,128]{3,2,1,0:T(8,128)S(1)} %pad_maximum_fusion.1), channel_id=1, source_target_pairs={{0,2},{2,0},{4,6},{6,4},{8,10},{10,8},{12,14},{14,12},{16,18},{18,... | collective-permute-start | bytes 245768 | tf_op jit(solution)/shard_map/ppermute | solution.py:628
  23.9 5.1 %collective-permute-start.4 = (f32[4,5,8,128]{3,2,1,0:T(8,128)S(1)}, f32[4,5,8,128]{3,2,1,0:T(8,128)S(1)}, u32[]{:S(2)}, u32[]{:S(2)}) collective-permute-start(f32[4,5,8,128]{3,2,1,0:T(8,128)S(1)} %pad_maximum_fusion.2), channel_id=1, source_target_pairs={{0,4},{2,6},{4,0},{6,2},{8,12},{10,14},{12,8},{14,10},{16,20},{18,... | collective-permute-start | bytes 245768 | tf_op jit(solution)/shard_map/ppermute | solution.py:628
  25.4 4.7 %collective-permute-start.5 = (f32[4,5,8,128]{3,2,1,0:T(8,128)S(1)}, f32[4,5,8,128]{3,2,1,0:T(8,128)S(1)}, u32[]{:S(2)}, u32[]{:S(2)}) collective-permute-start(f32[4,5,8,128]{3,2,1,0:T(8,128)S(1)} %pad_maximum_fusion.3), channel_id=1, source_target_pairs={{0,6},{2,4},{4,2},{6,0},{8,14},{10,12},{12,10},{14,8},{16,22},{18,... | collective-permute-start | bytes 245768 | tf_op jit(solution)/shard_map/ppermute | solution.py:628
